TPU v7x, 512 devices: a whole 4x8x8 slice. The times are simulated.
512 devices in a mesh: gx: 32 (over x, z), gy: 16 (over y, core).
Axes of the slice: x: 4, y: 8, z: 8, core: 2. Of those that a mesh axis runs over, the one named last changes fastest.
Arguments:
- labels: int32 [192, 128, 256], P('gx', 'gy'), may hold values from 0 to 7
- permittivity_real: float32 [8], replicated, may hold values from 1 to 2.5
- permittivity_imag: float32 [8], replicated, may hold values from 0 to 0.5
- angles: float32 [360], replicated, may hold values from -3.140625 to 3.140625
- angle_pick: int32 [4], replicated, may hold values from 0 to 359
Outputs:
- scattered_field: float32 [2, 4, 192, 128, 256], P(None, None, 'gx', 'gy')
All inputs are finite; a program needn't handle non-finite values.
Results may differ from a plain program's by a relative error of at most 0.000054.
Values sent between devices are 32-bit elements; how exact they have to be, the bound alone decides.
No kernel may reach another device: no remote copies, remote signals or barrier semaphores. Data moves between devices by JAX's collectives and lax.ppermute only.
A program may use at most 64 MiB of HBM per device.

v0:
```python
import jax
import jax.numpy as jnp
from jax import lax
from jax.sharding import PartitionSpec as P

NANG = 360
MAT = 8
COARSE_SWEEPS = 4


WEIGHTS = (128.0, -14.0, -3.0, -1.0)
DAMPING = 0.8
WAVE_SQUARED = 0.1
SHIFT_IMAG = 0.5
SOURCE_GAIN = 4.0


def with_halo(cells, sides, width):
    for axis, dim in sides:
        count = lax.axis_size(axis)
        ends = count - 1
        head = lax.slice_in_dim(cells, 0, width, axis=dim)
        tail = lax.slice_in_dim(cells, cells.shape[dim] - width, cells.shape[dim], axis=dim)
        cells = jnp.concatenate(
            [
                lax.ppermute(tail, axis, [(i, (i + 1) % count) for i in range(ends)]),
                cells,
                lax.ppermute(head, axis, [((i + 1) % count, i) for i in range(ends)]),
            ],
            axis=dim,
        )
    return cells


def shifted(shard, axis, by):
    size = lax.axis_size(axis)
    pairs = [(i, i + by) for i in range(size) if 0 <= i + by < size]
    return lax.ppermute(shard, axis, pairs)


def stencil(padded):
    extent_x = padded.shape[-3] - 2
    extent_y = padded.shape[-2] - 2
    extent_z = padded.shape[-1] - 2
    summed = jnp.zeros(padded.shape[:-3] + (extent_x, extent_y, extent_z), padded.dtype)
    for offset_x in (0, 1, 2):
        for offset_y in (0, 1, 2):
            for offset_z in (0, 1, 2):
                weight = WEIGHTS[abs(offset_x - 1) + abs(offset_y - 1) + abs(offset_z - 1)]
                summed = (
                    summed
                    + weight
                    * padded[
                        ...,
                        offset_x : offset_x + extent_x,
                        offset_y : offset_y + extent_y,
                        offset_z : offset_z + extent_z,
                    ]
                )
    return summed / 30.0


def complex_product(coefs, values):
    real_out = coefs[0] * values[0] - coefs[1] * values[1]
    imag_out = coefs[0] * values[1] + coefs[1] * values[0]
    return jnp.stack([real_out, imag_out])


def apply_operator(iterate, padded, medium, factor):
    laplace = stencil(padded) * factor
    return laplace - complex_product(medium, iterate)


def inverse_diagonal(medium, centre_weight):
    diag_real = centre_weight - medium[0]
    diag_imag = -medium[1]
    modulus = diag_real * diag_real + diag_imag * diag_imag
    return jnp.stack([diag_real / modulus, -diag_imag / modulus])


def restrict_axis(values, along):
    planes = (values.shape[along] - 1) // 2
    low_side = lax.slice_in_dim(values, 0, 2 * planes, 2, along)
    centre = lax.slice_in_dim(values, 1, 2 * planes, 2, along)
    high_side = lax.slice_in_dim(values, 2, 2 * planes + 1, 2, along)
    return (low_side + 2.0 * centre + high_side) * 0.25


def prolong_axis(values, along):
    planes = values.shape[along] - 1
    lower_part = lax.slice_in_dim(values, 0, planes, 1, along)
    upper_part = lax.slice_in_dim(values, 1, planes + 1, 1, along)
    even_rows = (lower_part + upper_part) * 0.5
    stacked = jnp.stack([even_rows, upper_part], axis=along + 1)
    new_shape = list(values.shape)
    new_shape[along] = 2 * planes
    return stacked.reshape(new_shape)


def fine_padded(iterate):
    padded = with_halo(iterate, (("gx", 2), ("gy", 3)), 1)
    return jnp.pad(padded, ((0, 0), (0, 0), (0, 0), (0, 0), (1, 1)))


def coarse_padded(correction):
    padded = with_halo(correction, (("gx", 2), ("gy", 3)), 1)
    return jnp.pad(padded, ((0, 0), (0, 0), (0, 0), (0, 0), (1, 1)))


def local(labels, permittivity_real, permittivity_imag, angles, angle_pick):
    cells_x, cells_y, cells_z = labels.shape
    eps_real = jnp.zeros(labels.shape, jnp.float32)
    eps_imag = jnp.zeros(labels.shape, jnp.float32)
    for material in range(MAT):
        chosen = labels == material
        eps_real = jnp.where(chosen, permittivity_real[material], eps_real)
        eps_imag = jnp.where(chosen, permittivity_imag[material], eps_imag)
    medium = WAVE_SQUARED * jnp.stack(
        [eps_real + SHIFT_IMAG * eps_imag, eps_imag - SHIFT_IMAG * eps_real]
    )
    pick_table = (angle_pick[:, None] == jnp.arange(NANG, dtype=jnp.int32)[None, :]).astype(
        jnp.float32
    )
    incidence = jnp.sum(pick_table * angles[None, :], axis=1)
    wavenumber = jnp.sqrt(WAVE_SQUARED)
    first_x = lax.axis_index("gx") * cells_x
    first_y = lax.axis_index("gy") * cells_y
    pos_x = (first_x + jnp.arange(cells_x, dtype=jnp.int32)).astype(jnp.float32)
    pos_y = (first_y + jnp.arange(cells_y, dtype=jnp.int32)).astype(jnp.float32)
    phases = wavenumber * (
        jnp.cos(incidence)[:, None, None] * pos_x[None, :, None]
        + jnp.sin(incidence)[:, None, None] * pos_y[None, None, :]
    )
    phases = phases[..., None]
    contrast = eps_real - 1.0
    source = SOURCE_GAIN * jnp.stack(
        [
            contrast * jnp.cos(phases) - eps_imag * jnp.sin(phases),
            contrast * jnp.sin(phases) + eps_imag * jnp.cos(phases),
        ]
    )
    inverse = inverse_diagonal(medium, 128.0 / 30.0)
    iterate = DAMPING * complex_product(inverse, source)
    residual = source - apply_operator(iterate, fine_padded(iterate), medium, 1.0)
    iterate = iterate + DAMPING * complex_product(inverse, residual)
    residual = source - apply_operator(iterate, fine_padded(iterate), medium, 1.0)
    rim_x = shifted(residual[:, :, :1], "gx", -1)
    extended = jnp.concatenate([residual, rim_x], axis=2)
    rim_y = shifted(extended[:, :, :, :1], "gy", -1)
    extended = jnp.concatenate([extended, rim_y], axis=3)
    extended = jnp.pad(extended, ((0, 0), (0, 0), (0, 0), (0, 0), (0, 1)))
    coarse_rhs = restrict_axis(restrict_axis(restrict_axis(extended, 2), 3), 4)
    coarse_medium = medium[:, 1::2, 1::2, 1::2]
    coarse_inverse = inverse_diagonal(coarse_medium, 128.0 / 120.0)
    correction = DAMPING * complex_product(coarse_inverse, coarse_rhs)
    for sweep_index in range(COARSE_SWEEPS - 1):
        coarse_res = coarse_rhs - apply_operator(
            correction, coarse_padded(correction), coarse_medium, 0.25
        )
        correction = correction + DAMPING * complex_product(coarse_inverse, coarse_res)
    rim_left = shifted(correction[:, :, -1:], "gx", 1)
    with_rim = jnp.concatenate([rim_left, correction], axis=2)
    rim_upper = shifted(with_rim[:, :, :, -1:], "gy", 1)
    with_rim = jnp.concatenate([rim_upper, with_rim], axis=3)
    with_rim = jnp.pad(with_rim, ((0, 0), (0, 0), (0, 0), (0, 0), (1, 0)))
    fine_correction = prolong_axis(prolong_axis(prolong_axis(with_rim, 2), 3), 4)
    return iterate + fine_correction


def solution(mesh):
    return jax.shard_map(
        local,
        mesh=mesh,
        in_specs=(P("gx", "gy", None), P(), P(), P(), P()),
        out_specs=P(None, None, "gx", "gy", None),
        check_vma=False,
    )
```

profile of v0, /device:TPU:38, one launch (start us, length us, event | category | flops | bytes accessed | tf_op | source)
XLA Modules:
  0.0 165.8 jit_solution(3704426102742120759)
XLA Ops:
  5.0 10.0 %add_bitcast_fusion = (f32[1,6,8,256]{3,2,1,0:T(8,128)S(1)}, f32[6,8,256]{2,1,0:T(8,128)S(1)}, f32[6,8,256]{2,1,0:T(8,128)S(1)}) fusion(pred[6,8,256]{2,1,0:T(8,128)(4,1)S(1)} %get-tuple-element.80, pred[6,8,256]{2,1,0:T(8,128)(4,1)S(1)} %get-tuple-element.79, pred[6,8,256]{2,1,0:T(8,128)(4,1)S(1)} %get-tuple-element.78, ...), kind=kLoop, calls=%fused_computation.383 | loop fusion | flops 221184 | bytes 245824 | tf_op jit(solution)/shard_map/stack | solution.py:118
  15.7 4.3 %collective-permute-start = (f32[2,4,1,8,256]{4,3,2,1,0:T(8,128)S(1)}, f32[2,4,1,8,256]{4,3,2,1,0:T(8,128)S(1)}, u32[]{:S(2)}, u32[]{:S(2)}) collective-permute-start(f32[2,4,1,8,256]{4,3,2,1,0:T(8,128)S(1)} %get-tuple-element.28), channel_id=1, source_target_pairs={{0,16},{16,32},{32,48},{48,64},{64,80},{80,96},{96,112},{112,128},... | collective-permute-start | bytes 196616 | tf_op jit(solution)/shard_map/ppermute | solution.py:26
  20.0 8.9 %collective-permute-start.1 = (f32[2,4,1,8,256]{4,3,2,1,0:T(8,128)S(1)}, f32[2,4,1,8,256]{4,3,2,1,0:T(8,128)S(1)}, u32[]{:S(2)}, u32[]{:S(2)}) collective-permute-start(f32[2,4,1,8,256]{4,3,2,1,0:T(8,128)S(1)} %get-tuple-element.29), channel_id=1, source_target_pairs={{16,0},{32,16},{48,32},{64,48},{80,64},{96,80},{112,96},{128,112},... | collective-permute-start | bytes 196616 | tf_op jit(solution)/shard_map/ppermute | solution.py:28
  30.8 1.9 %collective-permute-start.3 = (f32[2,4,8,1,256]{4,2,3,1,0:T(8,128)S(1)}, f32[2,4,8,1,256]{4,2,3,1,0:T(8,128)S(1)}, u32[]{:S(2)}, u32[]{:S(2)}) collective-permute-start(f32[2,4,8,1,256]{4,2,3,1,0:T(8,128)S(1)} %copy.365), channel_id=1, source_target_pairs={{1,0},{2,1},{3,2},{4,3},{5,4},{6,5},{7,6},{8,7},{9,8},{10,9},{11,1... | collective-permute-start | bytes 196616 | tf_op jit(solution)/shard_map/ppermute | solution.py:28
  32.8 2.4 %collective-permute-start.2 = (f32[2,4,8,1,256]{4,2,3,1,0:T(8,128)S(1)}, f32[2,4,8,1,256]{4,2,3,1,0:T(8,128)S(1)}, u32[]{:S(2)}, u32[]{:S(2)}) collective-permute-start(f32[2,4,8,1,256]{4,2,3,1,0:T(8,128)S(1)} %copy.364), channel_id=1, source_target_pairs={{0,1},{1,2},{2,3},{3,4},{4,5},{5,6},{6,7},{7,8},{8,9},{9,10},{10,1... | collective-permute-start | bytes 196616 | tf_op jit(solution)/shard_map/ppermute | solution.py:26
  35.3 4.2 %collective-permute-done.2 = f32[2,4,8,1,256]{4,2,3,1,0:T(8,128)S(1)} collective-permute-done((f32[2,4,8,1,256]{4,2,3,1,0:T(8,128)S(1)}, f32[2,4,8,1,256]{4,2,3,1,0:T(8,128)S(1)}, u32[]{:S(2)}, u32[]{:S(2)}) %collective-permute-start.2) | collective-permute-done | bytes 65568 | tf_op jit(solution)/shard_map/ppermute | solution.py:26
  42.4 1.9 %collective-permute-start.4 = (f32[2,4,1,8,256]{4,3,2,1,0:T(8,128)S(1)}, f32[2,4,1,8,256]{4,3,2,1,0:T(8,128)S(1)}, u32[]{:S(2)}, u32[]{:S(2)}) collective-permute-start(f32[2,4,1,8,256]{4,3,2,1,0:T(8,128)S(1)} %get-tuple-element.26), channel_id=1, source_target_pairs={{0,16},{16,32},{32,48},{48,64},{64,80},{80,96},{96,112},{112,128},... | collective-permute-start | bytes 196616 | tf_op jit(solution)/shard_map/ppermute | solution.py:26
  44.4 6.4 %collective-permute-start.5 = (f32[2,4,1,8,256]{4,3,2,1,0:T(8,128)S(1)}, f32[2,4,1,8,256]{4,3,2,1,0:T(8,128)S(1)}, u32[]{:S(2)}, u32[]{:S(2)}) collective-permute-start(f32[2,4,1,8,256]{4,3,2,1,0:T(8,128)S(1)} %get-tuple-element.27), channel_id=1, source_target_pairs={{16,0},{32,16},{48,32},{64,48},{80,64},{96,80},{112,96},{128,112},... | collective-permute-start | bytes 196616 | tf_op jit(solution)/shard_map/ppermute | solution.py:28
  52.7 1.9 %collective-permute-start.7 = (f32[2,4,8,1,256]{4,2,3,1,0:T(8,128)S(1)}, f32[2,4,8,1,256]{4,2,3,1,0:T(8,128)S(1)}, u32[]{:S(2)}, u32[]{:S(2)}) collective-permute-start(f32[2,4,8,1,256]{4,2,3,1,0:T(8,128)S(1)} %copy.371), channel_id=1, source_target_pairs={{1,0},{2,1},{3,2},{4,3},{5,4},{6,5},{7,6},{8,7},{9,8},{10,9},{11,1... | collective-permute-start | bytes 196616 | tf_op jit(solution)/shard_map/ppermute | solution.py:28
  54.7 2.4 %collective-permute-start.6 = (f32[2,4,8,1,256]{4,2,3,1,0:T(8,128)S(1)}, f32[2,4,8,1,256]{4,2,3,1,0:T(8,128)S(1)}, u32[]{:S(2)}, u32[]{:S(2)}) collective-permute-start(f32[2,4,8,1,256]{4,2,3,1,0:T(8,128)S(1)} %copy.370), channel_id=1, source_target_pairs={{0,1},{1,2},{2,3},{3,4},{4,5},{5,6},{6,7},{7,8},{8,9},{9,10},{10,1... | collective-permute-start | bytes 196616 | tf_op jit(solution)/shard_map/ppermute | solution.py:26
  57.2 4.2 %collective-permute-done.6 = f32[2,4,8,1,256]{4,2,3,1,0:T(8,128)S(1)} collective-permute-done((f32[2,4,8,1,256]{4,2,3,1,0:T(8,128)S(1)}, f32[2,4,8,1,256]{4,2,3,1,0:T(8,128)S(1)}, u32[]{:S(2)}, u32[]{:S(2)}) %collective-permute-start.6) | collective-permute-done | bytes 65568 | tf_op jit(solution)/shard_map/ppermute | solution.py:26
  64.2 6.4 %collective-permute-start.8 = (f32[2,4,1,8,256]{4,3,2,1,0:T(8,128)S(1)}, f32[2,4,1,8,256]{4,3,2,1,0:T(8,128)S(1)}, u32[]{:S(2)}, u32[]{:S(2)}) collective-permute-start(f32[2,4,1,8,256]{4,3,2,1,0:T(8,128)S(1)} %slice.1059), channel_id=1, source_target_pairs={{16,0},{32,16},{48,32},{64,48},{80,64},{96,80},{112,96},{128,112},... | collective-permute-start | bytes 196616 | tf_op jit(solution)/shard_map/ppermute | solution.py:38
  72.5 1.9 %collective-permute-start.9 = (f32[2,4,7,1,256]{4,1,3,2,0:T(4,128)S(1)}, f32[2,4,7,1,256]{4,1,3,2,0:T(4,128)S(1)}, u32[]{:S(2)}, u32[]{:S(2)}) collective-permute-start(f32[2,4,7,1,256]{4,1,3,2,0:T(4,128)S(1)} %copy.376), channel_id=1, source_target_pairs={{1,0},{2,1},{3,2},{4,3},{5,4},{6,5},{7,6},{8,7},{9,8},{10,9},{11,1... | collective-permute-start | bytes 172040 | tf_op jit(solution)/shard_map/ppermute | solution.py:38
  76.6 2.2 %slice.882 = f32[2,4,3,4,128]{4,1,3,2,0:T(4,128)S(1)} slice(f32[2,4,3,4,257]{4,1,3,2,0:T(4,128)S(1)} %add_multiply_fusion.1), slice={[0:2:1], [0:4:1], [0:3:1], [0:4:1], [2:257:2]} | slice | bytes 98304 | tf_op jit(solution)/shard_map/slice | solution.py:85
  78.8 2.2 %slice.881 = f32[2,4,3,4,128]{4,1,3,2,0:T(4,128)S(1)} slice(f32[2,4,3,4,257]{4,1,3,2,0:T(4,128)S(1)} %add_multiply_fusion.1), slice={[0:2:1], [0:4:1], [0:3:1], [0:4:1], [1:256:2]} | slice | bytes 98304 | tf_op jit(solution)/shard_map/slice | solution.py:84
  81.0 2.2 %slice.880 = f32[2,4,3,4,128]{4,1,3,2,0:T(4,128)S(1)} slice(f32[2,4,3,4,257]{4,1,3,2,0:T(4,128)S(1)} %add_multiply_fusion.1), slice={[0:2:1], [0:4:1], [0:3:1], [0:4:1], [0:256:2]} | slice | bytes 98304 | tf_op jit(solution)/shard_map/slice | solution.py:83
  83.3 1.9 %collective-permute-start.10 = (f32[2,4,1,4,128]{4,1,3,2,0:T(4,128)S(1)}, f32[2,4,1,4,128]{4,1,3,2,0:T(4,128)S(1)}, u32[]{:S(2)}, u32[]{:S(2)}) collective-permute-start(f32[2,4,1,4,128]{4,1,3,2,0:T(4,128)S(1)} %get-tuple-element.70), channel_id=1, source_target_pairs={{0,16},{16,32},{32,48},{48,64},{64,80},{80,96},{96,112},{112,128},... | collective-permute-start | bytes 49160 | tf_op jit(solution)/shard_map/ppermute | solution.py:26
  85.2 6.4 %collective-permute-start.11 = (f32[2,4,1,4,128]{4,1,3,2,0:T(4,128)S(1)}, f32[2,4,1,4,128]{4,1,3,2,0:T(4,128)S(1)}, u32[]{:S(2)}, u32[]{:S(2)}) collective-permute-start(f32[2,4,1,4,128]{4,1,3,2,0:T(4,128)S(1)} %get-tuple-element.71), channel_id=1, source_target_pairs={{16,0},{32,16},{48,32},{64,48},{80,64},{96,80},{112,96},{128,112},... | collective-permute-start | bytes 49160 | tf_op jit(solution)/shard_map/ppermute | solution.py:28
  93.1 1.9 %collective-permute-start.12 = (f32[2,4,5,1,128]{4,1,3,2,0:T(4,128)S(1)}, f32[2,4,5,1,128]{4,1,3,2,0:T(4,128)S(1)}, u32[]{:S(2)}, u32[]{:S(2)}) collective-permute-start(f32[2,4,5,1,128]{4,1,3,2,0:T(4,128)S(1)} %get-tuple-element.50), channel_id=1, source_target_pairs={{0,1},{1,2},{2,3},{3,4},{4,5},{5,6},{6,7},{7,8},{8,9},{9,10},{10,1... | collective-permute-start | bytes 61448 | tf_op jit(solution)/shard_map/ppermute | solution.py:26
  95.0 4.9 %collective-permute-start.13 = (f32[2,4,5,1,128]{4,1,3,2,0:T(4,128)S(1)}, f32[2,4,5,1,128]{4,1,3,2,0:T(4,128)S(1)}, u32[]{:S(2)}, u32[]{:S(2)}) collective-permute-start(f32[2,4,5,1,128]{4,1,3,2,0:T(4,128)S(1)} %get-tuple-element.51), channel_id=1, source_target_pairs={{1,0},{2,1},{3,2},{4,3},{5,4},{6,5},{7,6},{8,7},{9,8},{10,9},{11,1... | collective-permute-start | bytes 61448 | tf_op jit(solution)/shard_map/ppermute | solution.py:28
  101.9 1.9 %collective-permute-start.14 = (f32[2,4,1,4,128]{4,1,3,2,0:T(4,128)S(1)}, f32[2,4,1,4,128]{4,1,3,2,0:T(4,128)S(1)}, u32[]{:S(2)}, u32[]{:S(2)}) collective-permute-start(f32[2,4,1,4,128]{4,1,3,2,0:T(4,128)S(1)} %get-tuple-element.68), channel_id=1, source_target_pairs={{0,16},{16,32},{32,48},{48,64},{64,80},{80,96},{96,112},{112,128},... | collective-permute-start | bytes 49160 | tf_op jit(solution)/shard_map/ppermute | solution.py:26
  103.9 6.3 %collective-permute-start.15 = (f32[2,4,1,4,128]{4,1,3,2,0:T(4,128)S(1)}, f32[2,4,1,4,128]{4,1,3,2,0:T(4,128)S(1)}, u32[]{:S(2)}, u32[]{:S(2)}) collective-permute-start(f32[2,4,1,4,128]{4,1,3,2,0:T(4,128)S(1)} %get-tuple-element.69), channel_id=1, source_target_pairs={{16,0},{32,16},{48,32},{64,48},{80,64},{96,80},{112,96},{128,112},... | collective-permute-start | bytes 49160 | tf_op jit(solution)/shard_map/ppermute | solution.py:28
  111.6 1.9 %collective-permute-start.16 = (f32[2,4,5,1,128]{4,1,3,2,0:T(4,128)S(1)}, f32[2,4,5,1,128]{4,1,3,2,0:T(4,128)S(1)}, u32[]{:S(2)}, u32[]{:S(2)}) collective-permute-start(f32[2,4,5,1,128]{4,1,3,2,0:T(4,128)S(1)} %get-tuple-element.46), channel_id=1, source_target_pairs={{0,1},{1,2},{2,3},{3,4},{4,5},{5,6},{6,7},{7,8},{8,9},{9,10},{10,1... | collective-permute-start | bytes 61448 | tf_op jit(solution)/shard_map/ppermute | solution.py:26
  113.6 4.9 %collective-permute-start.17 = (f32[2,4,5,1,128]{4,1,3,2,0:T(4,128)S(1)}, f32[2,4,5,1,128]{4,1,3,2,0:T(4,128)S(1)}, u32[]{:S(2)}, u32[]{:S(2)}) collective-permute-start(f32[2,4,5,1,128]{4,1,3,2,0:T(4,128)S(1)} %get-tuple-element.47), channel_id=1, source_target_pairs={{1,0},{2,1},{3,2},{4,3},{5,4},{6,5},{7,6},{8,7},{9,8},{10,9},{11,1... | collective-permute-start | bytes 61448 | tf_op jit(solution)/shard_map/ppermute | solution.py:28
  120.5 1.9 %collective-permute-start.18 = (f32[2,4,1,4,128]{4,1,3,2,0:T(4,128)S(1)}, f32[2,4,1,4,128]{4,1,3,2,0:T(4,128)S(1)}, u32[]{:S(2)}, u32[]{:S(2)}) collective-permute-start(f32[2,4,1,4,128]{4,1,3,2,0:T(4,128)S(1)} %get-tuple-element.66), channel_id=1, source_target_pairs={{0,16},{16,32},{32,48},{48,64},{64,80},{80,96},{96,112},{112,128},... | collective-permute-start | bytes 49160 | tf_op jit(solution)/shard_map/ppermute | solution.py:26
  122.4 6.3 %collective-permute-start.19 = (f32[2,4,1,4,128]{4,1,3,2,0:T(4,128)S(1)}, f32[2,4,1,4,128]{4,1,3,2,0:T(4,128)S(1)}, u32[]{:S(2)}, u32[]{:S(2)}) collective-permute-start(f32[2,4,1,4,128]{4,1,3,2,0:T(4,128)S(1)} %get-tuple-element.67), channel_id=1, source_target_pairs={{16,0},{32,16},{48,32},{64,48},{80,64},{96,80},{112,96},{128,112},... | collective-permute-start | bytes 49160 | tf_op jit(solution)/shard_map/ppermute | solution.py:28
  130.2 1.9 %collective-permute-start.20 = (f32[2,4,5,1,128]{4,1,3,2,0:T(4,128)S(1)}, f32[2,4,5,1,128]{4,1,3,2,0:T(4,128)S(1)}, u32[]{:S(2)}, u32[]{:S(2)}) collective-permute-start(f32[2,4,5,1,128]{4,1,3,2,0:T(4,128)S(1)} %get-tuple-element.42), channel_id=1, source_target_pairs={{0,1},{1,2},{2,3},{3,4},{4,5},{5,6},{6,7},{7,8},{8,9},{9,10},{10,1... | collective-permute-start | bytes 61448 | tf_op jit(solution)/shard_map/ppermute | solution.py:26
  132.1 4.9 %collective-permute-start.21 = (f32[2,4,5,1,128]{4,1,3,2,0:T(4,128)S(1)}, f32[2,4,5,1,128]{4,1,3,2,0:T(4,128)S(1)}, u32[]{:S(2)}, u32[]{:S(2)}) collective-permute-start(f32[2,4,5,1,128]{4,1,3,2,0:T(4,128)S(1)} %get-tuple-element.43), channel_id=1, source_target_pairs={{1,0},{2,1},{3,2},{4,3},{5,4},{6,5},{7,6},{8,7},{9,8},{10,9},{11,1... | collective-permute-start | bytes 61448 | tf_op jit(solution)/shard_map/ppermute | solution.py:28
  141.0 6.1 %collective-permute-done.22 = f32[2,4,1,4,128]{4,1,3,2,0:T(4,128)S(1)} collective-permute-done((f32[2,4,1,4,128]{4,1,3,2,0:T(4,128)S(1)}, f32[2,4,1,4,128]{4,1,3,2,0:T(4,128)S(1)}, u32[]{:S(2)}, u32[]{:S(2)}) %collective-permute-start.22) | collective-permute-done | bytes 16416 | tf_op jit(solution)/shard_map/ppermute | solution.py:38
  149.1 4.3 %collective-permute-done.23 = f32[2,4,4,1,128]{4,2,3,1,0:T(4,128)S(1)} collective-permute-done((f32[2,4,4,1,128]{4,2,3,1,0:T(4,128)S(1)}, f32[2,4,4,1,128]{4,2,3,1,0:T(4,128)S(1)}, u32[]{:S(2)}, u32[]{:S(2)}) %collective-permute-start.23) | collective-permute-done | bytes 16416 | tf_op jit(solution)/shard_map/ppermute | solution.py:38
  154.3 6.4 %copy.385 = f32[2,4,6,8,128,2]{3,5,4,2,1,0:T(2,128)} copy(f32[2,4,6,8,128,2]{4,1,3,2,0,5:T(4,128)S(1)} %pad_maximum_fusion.9) | data formatting | bytes 786432 | tf_op jit(solution)/shard_map/stack | solution.py:94
  160.7 4.3 %copy.386 = f32[2,4,6,8,256]{4,3,2,1,0:T(8,128)S(1)} copy(f32[2,4,6,8,256]{3,4,2,1,0:T(8,128)} %bitcast.51) | data formatting | bytes 786432 | tf_op jit(solution)/shard_map/reshape | solution.py:97
  (114 shorter events, 35.5 us)
Async XLA Ops:
  15.7 13.5 %collective-permute-start = (f32[2,4,1,8,256]{4,3,2,1,0:T(8,128)S(1)}, f32[2,4,1,8,256]{4,3,2,1,0:T(8,128)S(1)}, u32[]{:S(2)}, u32[]{:S(2)}) collective-permute-start(f32[2,4,1,8,256]{4,3,2,1,0:T(8,128)S(1)} %get-tuple-element.28), channel_id=1, source_target_pairs={{0,16},{16,32},{32,48},{48,64},{64,80},{80,96},{96,112},{112,128},... | collective-permute-start | bytes 196616 | tf_op jit(solution)/shard_map/ppermute | solution.py:26
  20.0 10.7 %collective-permute-start.1 = (f32[2,4,1,8,256]{4,3,2,1,0:T(8,128)S(1)}, f32[2,4,1,8,256]{4,3,2,1,0:T(8,128)S(1)}, u32[]{:S(2)}, u32[]{:S(2)}) collective-permute-start(f32[2,4,1,8,256]{4,3,2,1,0:T(8,128)S(1)} %get-tuple-element.29), channel_id=1, source_target_pairs={{16,0},{32,16},{48,32},{64,48},{80,64},{96,80},{112,96},{128,112},... | collective-permute-start | bytes 196616 | tf_op jit(solution)/shard_map/ppermute | solution.py:28
  30.8 4.4 %collective-permute-start.3 = (f32[2,4,8,1,256]{4,2,3,1,0:T(8,128)S(1)}, f32[2,4,8,1,256]{4,2,3,1,0:T(8,128)S(1)}, u32[]{:S(2)}, u32[]{:S(2)}) collective-permute-start(f32[2,4,8,1,256]{4,2,3,1,0:T(8,128)S(1)} %copy.365), channel_id=1, source_target_pairs={{1,0},{2,1},{3,2},{4,3},{5,4},{6,5},{7,6},{8,7},{9,8},{10,9},{11,1... | collective-permute-start | bytes 196616 | tf_op jit(solution)/shard_map/ppermute | solution.py:28
  32.8 6.8 %collective-permute-start.2 = (f32[2,4,8,1,256]{4,2,3,1,0:T(8,128)S(1)}, f32[2,4,8,1,256]{4,2,3,1,0:T(8,128)S(1)}, u32[]{:S(2)}, u32[]{:S(2)}) collective-permute-start(f32[2,4,8,1,256]{4,2,3,1,0:T(8,128)S(1)} %copy.364), channel_id=1, source_target_pairs={{0,1},{1,2},{2,3},{3,4},{4,5},{5,6},{6,7},{7,8},{8,9},{9,10},{10,1... | collective-permute-start | bytes 196616 | tf_op jit(solution)/shard_map/ppermute | solution.py:26
  42.4 9.7 %collective-permute-start.4 = (f32[2,4,1,8,256]{4,3,2,1,0:T(8,128)S(1)}, f32[2,4,1,8,256]{4,3,2,1,0:T(8,128)S(1)}, u32[]{:S(2)}, u32[]{:S(2)}) collective-permute-start(f32[2,4,1,8,256]{4,3,2,1,0:T(8,128)S(1)} %get-tuple-element.26), channel_id=1, source_target_pairs={{0,16},{16,32},{32,48},{48,64},{64,80},{80,96},{96,112},{112,128},... | collective-permute-start | bytes 196616 | tf_op jit(solution)/shard_map/ppermute | solution.py:26
  44.4 8.3 %collective-permute-start.5 = (f32[2,4,1,8,256]{4,3,2,1,0:T(8,128)S(1)}, f32[2,4,1,8,256]{4,3,2,1,0:T(8,128)S(1)}, u32[]{:S(2)}, u32[]{:S(2)}) collective-permute-start(f32[2,4,1,8,256]{4,3,2,1,0:T(8,128)S(1)} %get-tuple-element.27), channel_id=1, source_target_pairs={{16,0},{32,16},{48,32},{64,48},{80,64},{96,80},{112,96},{128,112},... | collective-permute-start | bytes 196616 | tf_op jit(solution)/shard_map/ppermute | solution.py:28
  52.7 4.4 %collective-permute-start.7 = (f32[2,4,8,1,256]{4,2,3,1,0:T(8,128)S(1)}, f32[2,4,8,1,256]{4,2,3,1,0:T(8,128)S(1)}, u32[]{:S(2)}, u32[]{:S(2)}) collective-permute-start(f32[2,4,8,1,256]{4,2,3,1,0:T(8,128)S(1)} %copy.371), channel_id=1, source_target_pairs={{1,0},{2,1},{3,2},{4,3},{5,4},{6,5},{7,6},{8,7},{9,8},{10,9},{11,1... | collective-permute-start | bytes 196616 | tf_op jit(solution)/shard_map/ppermute | solution.py:28
  54.7 6.8 %collective-permute-start.6 = (f32[2,4,8,1,256]{4,2,3,1,0:T(8,128)S(1)}, f32[2,4,8,1,256]{4,2,3,1,0:T(8,128)S(1)}, u32[]{:S(2)}, u32[]{:S(2)}) collective-permute-start(f32[2,4,8,1,256]{4,2,3,1,0:T(8,128)S(1)} %copy.370), channel_id=1, source_target_pairs={{0,1},{1,2},{2,3},{3,4},{4,5},{5,6},{6,7},{7,8},{8,9},{9,10},{10,1... | collective-permute-start | bytes 196616 | tf_op jit(solution)/shard_map/ppermute | solution.py:26
  64.2 8.3 %collective-permute-start.8 = (f32[2,4,1,8,256]{4,3,2,1,0:T(8,128)S(1)}, f32[2,4,1,8,256]{4,3,2,1,0:T(8,128)S(1)}, u32[]{:S(2)}, u32[]{:S(2)}) collective-permute-start(f32[2,4,1,8,256]{4,3,2,1,0:T(8,128)S(1)} %slice.1059), channel_id=1, source_target_pairs={{16,0},{32,16},{48,32},{64,48},{80,64},{96,80},{112,96},{128,112},... | collective-permute-start | bytes 196616 | tf_op jit(solution)/shard_map/ppermute | solution.py:38
  72.5 3.7 %collective-permute-start.9 = (f32[2,4,7,1,256]{4,1,3,2,0:T(4,128)S(1)}, f32[2,4,7,1,256]{4,1,3,2,0:T(4,128)S(1)}, u32[]{:S(2)}, u32[]{:S(2)}) collective-permute-start(f32[2,4,7,1,256]{4,1,3,2,0:T(4,128)S(1)} %copy.376), channel_id=1, source_target_pairs={{1,0},{2,1},{3,2},{4,3},{5,4},{6,5},{7,6},{8,7},{9,8},{10,9},{11,1... | collective-permute-start | bytes 172040 | tf_op jit(solution)/shard_map/ppermute | solution.py:38
  83.3 8.3 %collective-permute-start.10 = (f32[2,4,1,4,128]{4,1,3,2,0:T(4,128)S(1)}, f32[2,4,1,4,128]{4,1,3,2,0:T(4,128)S(1)}, u32[]{:S(2)}, u32[]{:S(2)}) collective-permute-start(f32[2,4,1,4,128]{4,1,3,2,0:T(4,128)S(1)} %get-tuple-element.70), channel_id=1, source_target_pairs={{0,16},{16,32},{32,48},{48,64},{64,80},{80,96},{96,112},{112,128},... | collective-permute-start | bytes 49160 | tf_op jit(solution)/shard_map/ppermute | solution.py:26
  85.2 7.8 %collective-permute-start.11 = (f32[2,4,1,4,128]{4,1,3,2,0:T(4,128)S(1)}, f32[2,4,1,4,128]{4,1,3,2,0:T(4,128)S(1)}, u32[]{:S(2)}, u32[]{:S(2)}) collective-permute-start(f32[2,4,1,4,128]{4,1,3,2,0:T(4,128)S(1)} %get-tuple-element.71), channel_id=1, source_target_pairs={{16,0},{32,16},{48,32},{64,48},{80,64},{96,80},{112,96},{128,112},... | collective-permute-start | bytes 49160 | tf_op jit(solution)/shard_map/ppermute | solution.py:28
  93.1 6.8 %collective-permute-start.12 = (f32[2,4,5,1,128]{4,1,3,2,0:T(4,128)S(1)}, f32[2,4,5,1,128]{4,1,3,2,0:T(4,128)S(1)}, u32[]{:S(2)}, u32[]{:S(2)}) collective-permute-start(f32[2,4,5,1,128]{4,1,3,2,0:T(4,128)S(1)} %get-tuple-element.50), channel_id=1, source_target_pairs={{0,1},{1,2},{2,3},{3,4},{4,5},{5,6},{6,7},{7,8},{8,9},{9,10},{10,1... | collective-permute-start | bytes 61448 | tf_op jit(solution)/shard_map/ppermute | solution.py:26
  95.0 6.3 %collective-permute-start.13 = (f32[2,4,5,1,128]{4,1,3,2,0:T(4,128)S(1)}, f32[2,4,5,1,128]{4,1,3,2,0:T(4,128)S(1)}, u32[]{:S(2)}, u32[]{:S(2)}) collective-permute-start(f32[2,4,5,1,128]{4,1,3,2,0:T(4,128)S(1)} %get-tuple-element.51), channel_id=1, source_target_pairs={{1,0},{2,1},{3,2},{4,3},{5,4},{6,5},{7,6},{8,7},{9,8},{10,9},{11,1... | collective-permute-start | bytes 61448 | tf_op jit(solution)/shard_map/ppermute | solution.py:28
  101.9 8.3 %collective-permute-start.14 = (f32[2,4,1,4,128]{4,1,3,2,0:T(4,128)S(1)}, f32[2,4,1,4,128]{4,1,3,2,0:T(4,128)S(1)}, u32[]{:S(2)}, u32[]{:S(2)}) collective-permute-start(f32[2,4,1,4,128]{4,1,3,2,0:T(4,128)S(1)} %get-tuple-element.68), channel_id=1, source_target_pairs={{0,16},{16,32},{32,48},{48,64},{64,80},{80,96},{96,112},{112,128},... | collective-permute-start | bytes 49160 | tf_op jit(solution)/shard_map/ppermute | solution.py:26
  103.9 7.7 %collective-permute-start.15 = (f32[2,4,1,4,128]{4,1,3,2,0:T(4,128)S(1)}, f32[2,4,1,4,128]{4,1,3,2,0:T(4,128)S(1)}, u32[]{:S(2)}, u32[]{:S(2)}) collective-permute-start(f32[2,4,1,4,128]{4,1,3,2,0:T(4,128)S(1)} %get-tuple-element.69), channel_id=1, source_target_pairs={{16,0},{32,16},{48,32},{64,48},{80,64},{96,80},{112,96},{128,112},... | collective-permute-start | bytes 49160 | tf_op jit(solution)/shard_map/ppermute | solution.py:28
  111.6 6.8 %collective-permute-start.16 = (f32[2,4,5,1,128]{4,1,3,2,0:T(4,128)S(1)}, f32[2,4,5,1,128]{4,1,3,2,0:T(4,128)S(1)}, u32[]{:S(2)}, u32[]{:S(2)}) collective-permute-start(f32[2,4,5,1,128]{4,1,3,2,0:T(4,128)S(1)} %get-tuple-element.46), channel_id=1, source_target_pairs={{0,1},{1,2},{2,3},{3,4},{4,5},{5,6},{6,7},{7,8},{8,9},{9,10},{10,1... | collective-permute-start | bytes 61448 | tf_op jit(solution)/shard_map/ppermute | solution.py:26
  113.6 6.3 %collective-permute-start.17 = (f32[2,4,5,1,128]{4,1,3,2,0:T(4,128)S(1)}, f32[2,4,5,1,128]{4,1,3,2,0:T(4,128)S(1)}, u32[]{:S(2)}, u32[]{:S(2)}) collective-permute-start(f32[2,4,5,1,128]{4,1,3,2,0:T(4,128)S(1)} %get-tuple-element.47), channel_id=1, source_target_pairs={{1,0},{2,1},{3,2},{4,3},{5,4},{6,5},{7,6},{8,7},{9,8},{10,9},{11,1... | collective-permute-start | bytes 61448 | tf_op jit(solution)/shard_map/ppermute | solution.py:28
  120.5 8.3 %collective-permute-start.18 = (f32[2,4,1,4,128]{4,1,3,2,0:T(4,128)S(1)}, f32[2,4,1,4,128]{4,1,3,2,0:T(4,128)S(1)}, u32[]{:S(2)}, u32[]{:S(2)}) collective-permute-start(f32[2,4,1,4,128]{4,1,3,2,0:T(4,128)S(1)} %get-tuple-element.66), channel_id=1, source_target_pairs={{0,16},{16,32},{32,48},{48,64},{64,80},{80,96},{96,112},{112,128},... | collective-permute-start | bytes 49160 | tf_op jit(solution)/shard_map/ppermute | solution.py:26
  122.4 7.7 %collective-permute-start.19 = (f32[2,4,1,4,128]{4,1,3,2,0:T(4,128)S(1)}, f32[2,4,1,4,128]{4,1,3,2,0:T(4,128)S(1)}, u32[]{:S(2)}, u32[]{:S(2)}) collective-permute-start(f32[2,4,1,4,128]{4,1,3,2,0:T(4,128)S(1)} %get-tuple-element.67), channel_id=1, source_target_pairs={{16,0},{32,16},{48,32},{64,48},{80,64},{96,80},{112,96},{128,112},... | collective-permute-start | bytes 49160 | tf_op jit(solution)/shard_map/ppermute | solution.py:28
  130.2 6.8 %collective-permute-start.20 = (f32[2,4,5,1,128]{4,1,3,2,0:T(4,128)S(1)}, f32[2,4,5,1,128]{4,1,3,2,0:T(4,128)S(1)}, u32[]{:S(2)}, u32[]{:S(2)}) collective-permute-start(f32[2,4,5,1,128]{4,1,3,2,0:T(4,128)S(1)} %get-tuple-element.42), channel_id=1, source_target_pairs={{0,1},{1,2},{2,3},{3,4},{4,5},{5,6},{6,7},{7,8},{8,9},{9,10},{10,1... | collective-permute-start | bytes 61448 | tf_op jit(solution)/shard_map/ppermute | solution.py:26
  132.1 6.3 %collective-permute-start.21 = (f32[2,4,5,1,128]{4,1,3,2,0:T(4,128)S(1)}, f32[2,4,5,1,128]{4,1,3,2,0:T(4,128)S(1)}, u32[]{:S(2)}, u32[]{:S(2)}) collective-permute-start(f32[2,4,5,1,128]{4,1,3,2,0:T(4,128)S(1)} %get-tuple-element.43), channel_id=1, source_target_pairs={{1,0},{2,1},{3,2},{4,3},{5,4},{6,5},{7,6},{8,7},{9,8},{10,9},{11,1... | collective-permute-start | bytes 61448 | tf_op jit(solution)/shard_map/ppermute | solution.py:28
  139.1 8.0 %collective-permute-start.22 = (f32[2,4,1,4,128]{4,1,3,2,0:T(4,128)S(1)}, f32[2,4,1,4,128]{4,1,3,2,0:T(4,128)S(1)}, u32[]{:S(2)}, u32[]{:S(2)}) collective-permute-start(f32[2,4,1,4,128]{4,1,3,2,0:T(4,128)S(1)} %slice.1154), channel_id=1, source_target_pairs={{0,16},{16,32},{32,48},{48,64},{64,80},{80,96},{96,112},{112,128},... | collective-permute-start | bytes 49160 | tf_op jit(solution)/shard_map/ppermute | solution.py:38
  147.1 6.3 %collective-permute-start.23 = (f32[2,4,4,1,128]{4,2,3,1,0:T(4,128)S(1)}, f32[2,4,4,1,128]{4,2,3,1,0:T(4,128)S(1)}, u32[]{:S(2)}, u32[]{:S(2)}) collective-permute-start(f32[2,4,4,1,128]{4,2,3,1,0:T(4,128)S(1)} %copy.378), channel_id=1, source_target_pairs={{0,1},{1,2},{2,3},{3,4},{4,5},{5,6},{6,7},{7,8},{8,9},{9,10},{10,1... | collective-permute-start | bytes 49160 | tf_op jit(solution)/shard_map/ppermute | solution.py:38
where the time goes:
time: 167 us; the launch traced here: 166 us
  starting transfers between devices  87.3 us (52%)
  waiting for transfers between devices  33.2 us (20%)
  local copies, waits for them, and re-layouts  22.6 us (14%)
  other arithmetic  21.9 us (13%)
    ppermute x10, starting transfers between devices, with_halo(): lax.ppermute(head, axis, [((i + 1) % count, i) for i in range(ends)])  52.6 us
    ppermute x10, starting transfers between devices, with_halo(): lax.ppermute(tail, axis, [(i, (i + 1) % count) for i in range(ends)])  22.5 us
    ppermute x4, waiting for transfers between devices, shifted(): return lax.ppermute(shard, axis, pairs)  13.8 us
    ppermute x4, starting transfers between devices, shifted(): return lax.ppermute(shard, axis, pairs)  12.1 us
    ppermute x10, waiting for transfers between devices, with_halo(): lax.ppermute(head, axis, [((i + 1) % count, i) for i in range(ends)])  10.5 us
    another operation x2, other arithmetic, local(): jnp.stack([eps_real + SHIFT_IMAG * eps_imag, eps_imag - SHIFT_IMAG * eps_...  9.99 us
    ppermute x10, waiting for transfers between devices, with_halo(): lax.ppermute(tail, axis, [(i, (i + 1) % count) for i in range(ends)])  8.8 us
    another operation x4, local copies, waits for them, and re-layouts, prolong_axis(): stacked = jnp.stack([even_rows, upper_part], axis=along + 1)  6.46 us
  transfers between devices with their start and end apart: 24, of which 15 were waited for; matrix products, arithmetic and copies ran while one was open for 1% of the time, Pallas kernels for 0%

commit v1 on v0

v1 whole, which is shorter than its diff:
```python
import jax
import jax.numpy as jnp
from jax import lax
from jax.experimental import pallas as pl
from jax.experimental.pallas import tpu as pltpu
from jax.sharding import PartitionSpec as P

NANG = 360
MAT = 8
DAMPING = 0.8
WAVE_SQUARED = 0.1
SHIFT_IMAG = 0.5
SOURCE_GAIN = 4.0

OWN_X = 6
OWN_Y = 8
PX = 16
PY = 35
LOW = 10
CX, CY = 5, 15
NI, NJ = 10, 11
LANES = 128
F32 = jnp.float32
OUTSIDE = 8


def lane_iota():
    return lax.broadcasted_iota(jnp.int32, (8, LANES), 1)


def sign_rows():
    rows = lax.broadcasted_iota(jnp.int32, (8, LANES), 0)
    return jnp.where(rows < 4, -1.0, 1.0).astype(F32)


def up(values, first):
    return jnp.where(first, 0.0, pltpu.roll(values, 1, 1))


def down(values, last):
    return jnp.where(last, 0.0, pltpu.roll(values, LANES - 1, 1))


def turned(values):
    return pltpu.roll(values, 4, 0)


def row_of(ref, y, x):
    return jnp.broadcast_to(ref[y, pl.ds(x, 1), :], (8, LANES))


def edge_face(values, near):
    edge = 3.0 * values + near
    face = 3.0 * edge + 5.0 * values
    return edge, face


def region_kernel(
    sc, mid, low, high, tab, ex, ey,
    c1_out, ck_out, send_out, it2_out, inv_out,
    ge_r, go_r, ge_i, go_i, ie_r, io_r, ie_i, io_i, sa_r, sa_i, kr_t, ki_t,
    it1, pp, qq, va, vb, sy,
):
    core = sc[0]
    x0 = sc[1]
    y0 = sc[2]
    nx = sc[3]
    ny = sc[4]
    lanes = lane_iota()
    first = lanes == 0
    last = lanes == LANES - 1
    sgn = sign_rows()

    rows = lax.broadcasted_iota(jnp.int32, (2 * LANES, 2 * LANES), 0)
    cols = lax.broadcasted_iota(jnp.int32, (2 * LANES, 2 * LANES), 1)
    source_row = jnp.where(cols < LANES, 2 * cols, 2 * (cols - LANES) + 1)
    perm = jnp.where(rows == source_row, 1.0, 0.0).astype(jnp.bfloat16)

    def tables(labels, first_row, count):
        flat = labels[...].reshape(count * PX, 2 * LANES).astype(F32).astype(jnp.bfloat16)
        apart = jnp.dot(flat, perm, preferred_element_type=F32)
        for k in range(count):
            y = first_row + k
            y_in = jnp.logical_and(y0 + y >= 0, y0 + y < ny)
            for h in range(2):
                xs = x0 + 8 * h + lax.broadcasted_iota(jnp.int32, (8, LANES), 0)
                valid = jnp.logical_and(jnp.logical_and(xs >= 0, xs < nx), y_in)
                part = apart[k * PX + 8 * h : k * PX + 8 * h + 8]
                even = jnp.where(valid, part[:, :LANES].astype(jnp.int32), OUTSIDE)
                odd = jnp.where(valid, part[:, LANES:].astype(jnp.int32), OUTSIDE)

                def pick(row, index):
                    table = jnp.broadcast_to(tab[row : row + 1, :], (8, LANES))
                    return jnp.take_along_axis(
                        table, index, axis=1, mode="promise_in_bounds"
                    )

                at = (y, pl.ds(8 * h, 8), slice(None))
                ge_r[at] = pick(0, even)
                go_r[at] = pick(0, odd)
                ge_i[at] = pick(1, even)
                go_i[at] = pick(1, odd)
                ie_r[at] = pick(2, even)
                io_r[at] = pick(2, odd)
                ie_i[at] = pick(3, even)
                io_i[at] = pick(3, odd)
                for row, out in ((4, sa_r), (5, sa_i)):
                    se = pick(row, even)
                    so = pick(row, odd)
                    out[at] = se + down(se, last) + 2.0 * so
                kr_t[at] = pick(6, odd)
                ki_t[at] = pick(7, odd)

    tables(low, 0, LOW)
    tables(mid, LOW, 16)
    tables(high, LOW + 16, PY - LOW - 16)

    def first_stage(y, carry):
        wave = ey[y, 0]
        wave_t = ey[y, 1]
        edges, faces, centres = [[], []], [[], []], [[], []]
        for x in range(PX):
            c = ex[x, 0]
            s = ex[x, 1]
            e = c * wave + s * wave_t
            e_t = c * wave_t - s * wave
            even = row_of(ge_r, y, x) * e + row_of(ge_i, y, x) * e_t
            odd = row_of(go_r, y, x) * e + row_of(go_i, y, x) * e_t
            sy[y * PX + x] = row_of(sa_r, y, x) * e + row_of(sa_i, y, x) * e_t
            at = (y * PX + x) * 2
            it1[at] = even
            it1[at + 1] = odd
            near_e = odd + up(odd, first)
            near_o = even + down(even, last)
            for h, (v, near) in enumerate(((even, near_e), (odd, near_o))):
                edge, face = edge_face(v, near)
                edges[h].append(edge)
                faces[h].append(face)
                centres[h].append(14.0 * near)
        for x in range(PX):
            at = (y * PX + x) * 2
            for h in range(2):
                p = centres[h][x]
                q = faces[h][x]
                if x > 0 and x < PX - 1:
                    p = p + (faces[h][x - 1] + faces[h][x + 1])
                    q = q + (edges[h][x - 1] + edges[h][x + 1])
                elif x > 0:
                    p = p + faces[h][x - 1]
                    q = q + edges[h][x - 1]
                else:
                    p = p + faces[h][x + 1]
                    q = q + edges[h][x + 1]
                pp[at + h] = p
                qq[at + h] = q
        return carry

    lax.fori_loop(0, PY, first_stage, 0)

    def update(y, x, h, ir, ii):
        at = (y * PX + x) * 2 + h
        row = PX * 2
        n = pp[at] + (qq[at - row] + qq[at + row])
        return row_of(ir, y, x) * n + (row_of(ii, y, x) * sgn) * turned(n)

    def second_stage(y, carry):
        for x in range(1, 14):
            at = (y * PX + x) * 2
            we = 0.4 * it1[at] + update(y, x, 0, ie_r, ie_i)
            wo = 0.4 * it1[at + 1] + update(y, x, 1, io_r, io_i)
            p = we + down(we, last)
            after = jnp.where(last, -wo, pltpu.roll(wo, LANES - 1, 1))
            va[y * PX + x] = p + 2.0 * wo
            vb[y * PX + x] = (up(wo, first) + after) + 2.0 * (p + wo)
        return carry

    lax.fori_loop(1, PY - 1, second_stage, 0)

    def third_stage(j, carry):
        my = jnp.where(y0 + 4 + 2 * j == ny, 1.0, 2.0).astype(F32)
        base = (2 + 2 * j) * PX
        gs, hs = {}, {}
        for x in range(1, 14):

            def combos(ref):
                vm, v0, v1, v2, v3 = (ref[base + (d - 1) * PX + x] for d in range(5))
                p = v0 + v2
                return p + 2.0 * v1, (vm + v3) + 2.0 * p + my * v1

            aa, ba = combos(va)
            ab, bb = combos(vb)
            u = ba + ab
            g = 14.0 * u + 3.0 * bb
            if 2 <= x <= 12:
                g = g + (
                    (sy[base + x] + sy[base + 2 * PX + x]) + 2.0 * sy[base + PX + x]
                )
            gs[x] = g
            hs[x] = 14.0 * aa + 3.0 * u + bb
        for i in range(CX):
            b = 2 + 2 * i
            mx = jnp.where(x0 + b + 2 == nx, 1.0, 2.0).astype(F32)
            raw = (
                (gs[b] + gs[b + 2])
                + 2.0 * gs[b + 1]
                + (hs[b - 1] + hs[b + 3])
                + 2.0 * (hs[b] + hs[b + 2])
                + mx * hs[b + 1]
            ) * (1.0 / 1920.0)
            kr = row_of(kr_t, 3 + 2 * j, b + 1)
            ki = row_of(ki_t, 3 + 2 * j, b + 1)
            c1_out[i, j] = kr * raw + (ki * sgn) * turned(raw)
            ck_out[0, i, pl.ds(j, 1), :] = kr_t[3 + 2 * j, b + 1 : b + 2, :]
            ck_out[1, i, pl.ds(j, 1), :] = ki_t[3 + 2 * j, b + 1 : b + 2, :]
        return carry

    for k in range(2):
        for i in range(CX):
            ck_out[k, i, 8:16, :] = jnp.zeros((8, LANES), F32)
    lax.fori_loop(0, CY, third_stage, 0)

    xb = core * LOW
    yb = LOW + core * OWN_Y

    def own_stage(k, carry):
        y = yb + k
        for xx in range(OWN_X):
            x = xb + xx
            at = (y * PX + x) * 2
            it2_out[xx * OWN_Y + k, 0] = 1.2 * it1[at] + update(y, x, 0, ie_r, ie_i)
            it2_out[xx * OWN_Y + k, 1] = 1.2 * it1[at + 1] + update(y, x, 1, io_r, io_i)
        xe = core * (PX - 1)
        for n, ref in enumerate((ie_r, io_r, ie_i, io_i)):
            inv_out[n, pl.ds(k, 1), :] = ref[y, pl.ds(xe, 1), :]
        return carry

    lax.fori_loop(0, OWN_Y, own_stage, 0)

    j0 = 4 - 4 * core
    for i in range(CX):
        for j in range(NJ):
            send_out[i * NJ + j] = c1_out[i, j0 + j]
        for k in range(2):
            send_out[CX * NJ + (k * CX + i) * 2] = ck_out[k, i, 0:8, :]
            send_out[CX * NJ + (k * CX + i) * 2 + 1] = ck_out[k, i, 8:16, :]
    plane = 6 + 3 * core
    ys = LOW + OWN_Y - core * OWN_Y
    edges, faces = [], []
    for k in range(OWN_Y + 2):
        at = ((ys - 1 + k) * PX + plane) * 2
        even = it1[at]
        odd = it1[at + 1]
        ee, fe = edge_face(even, odd + up(odd, first))
        eo, fo = edge_face(odd, even + down(even, last))
        edges.append((ee, eo))
        faces.append((fe, fo))
    for k in range(OWN_Y):
        for h in range(2):
            send_out[CX * NJ + 4 * CX + 2 * k + h] = faces[k + 1][h] + (
                edges[k][h] + edges[k + 2][h]
            )


SEND = CX * NJ + 4 * CX + 2 * OWN_Y


def cycle_kernel(sc, c1_own, ck_own, recv, it2, inv, out, c1, ckr, cki, cc, pp, qq, vv, oo):
    core = sc[0]
    lanes = lane_iota()
    first = lanes == 0
    last = lanes == LANES - 1
    sgn = sign_rows()
    own_i = CX - core * CX
    other_i = core * CX
    own_j = 4 * core
    other_j = 4 - 4 * core

    for i in range(CX):
        for j in range(NJ):
            at = (own_i + i) * NJ + j
            c1[at] = c1_own[i, own_j + j]
            ckr[at] = jnp.broadcast_to(ck_own[0, i, pl.ds(own_j + j, 1), :], (8, LANES))
            cki[at] = (
                jnp.broadcast_to(ck_own[1, i, pl.ds(own_j + j, 1), :], (8, LANES)) * sgn
            )
            at = (other_i + i) * NJ + j
            c1[at] = recv[i * NJ + j]
            for k, ref in ((0, ckr), (1, cki)):
                row = (CX * NJ + (k * CX + i) * 2) * 8 + own_j + j
                value = recv[row // 8, pl.ds(row % 8, 1), :]
                value = jnp.broadcast_to(value, (8, LANES))
                ref[at] = value * sgn if k else value

    for sweep in range(3):
        ref = c1 if sweep == 0 else cc

        def sums(i, carry, ref=ref, sweep=sweep):
            edges, faces, centres = {}, {}, {}
            for j in range(sweep, NJ - sweep):
                v = ref[i * NJ + j]
                near = up(v, first) + down(v, last)
                edges[j], faces[j] = edge_face(v, near)
                centres[j] = 14.0 * near
            for j in range(sweep + 1, NJ - sweep - 1):
                pp[i * NJ + j] = centres[j] + (faces[j - 1] + faces[j + 1])
                qq[i * NJ + j] = faces[j] + (edges[j - 1] + edges[j + 1])
            return carry

        lax.fori_loop(sweep, NI - sweep, sums, 0)

        def relax(i, carry, ref=ref, sweep=sweep):
            for j in range(sweep + 1, NJ - sweep - 1):
                at = i * NJ + j
                n = (pp[at] + (qq[at - NJ] + qq[at + NJ])) * (1.0 / 120.0)
                cc[at] = (0.2 * ref[at] + c1[at]) + (ckr[at] * n + cki[at] * turned(n))
            return carry

        lax.fori_loop(sweep + 1, NI - sweep - 1, relax, 0)

    def put(x, y, value):
        col = x * OWN_Y + y
        even = 0.5 * (value + up(value, first))
        vv[col * 8 : col * 8 + 8, :LANES] = it2[col, 0] + even
        vv[col * 8 : col * 8 + 8, LANES:] = it2[col, 1] + value

    for i in range(OWN_X // 2):
        for j in range(OWN_Y // 2):
            at = (i + 4) * NJ + j + 4
            here = cc[at]
            left = cc[at - NJ]
            mix = 0.5 * (left + here)
            below = cc[at - 1]
            mix_below = 0.5 * (cc[at - NJ - 1] + below)
            put(2 * i + 1, 2 * j + 1, here)
            put(2 * i, 2 * j + 1, mix)
            put(2 * i + 1, 2 * j, 0.5 * (below + here))
            put(2 * i, 2 * j, 0.5 * (mix_below + mix))

    for k in range(OWN_Y):
        at = pl.multiple_of((core * (OWN_X - 1) * OWN_Y + k) * 8, 8)
        for h in range(2):
            n = recv[CX * NJ + 4 * CX + 2 * k + h]
            ir = jnp.broadcast_to(inv[h, k : k + 1, :], (8, LANES))
            ii = jnp.broadcast_to(inv[2 + h, k : k + 1, :], (8, LANES))
            where = (pl.ds(at, 8), slice(h * LANES, (h + 1) * LANES))
            vv[where] = vv[where] + (ir * n + (ii * sgn) * turned(n))

    rows = lax.broadcasted_iota(jnp.int32, (2 * LANES, 2 * LANES), 0)
    cols = lax.broadcasted_iota(jnp.int32, (2 * LANES, 2 * LANES), 1)
    target = jnp.where(rows < LANES, 2 * rows, 2 * (rows - LANES) + 1)
    perm = jnp.where(cols == target, 1.0, 0.0).astype(jnp.bfloat16)
    value = vv[...]
    top = value.astype(jnp.bfloat16)
    rest = value - top.astype(F32)
    middle = rest.astype(jnp.bfloat16)
    bottom = (rest - middle.astype(F32)).astype(jnp.bfloat16)
    oo[...] = (
        jnp.dot(bottom, perm, preferred_element_type=F32)
        + jnp.dot(middle, perm, preferred_element_type=F32)
    ) + jnp.dot(top, perm, preferred_element_type=F32)
    count = OWN_X * OWN_Y
    for col in range(count):
        block = oo[col * 8 : col * 8 + 8, :]
        for f in range(8):
            out[f * count + col : f * count + col + 1, :] = block[f : f + 1, :]


def vmem(*shape):
    return pltpu.VMEM(shape, F32)


def region_call(*args):
    spec = pl.BlockSpec(memory_space=pltpu.VMEM)
    cells = PY * PX
    return pl.pallas_call(
        region_kernel,
        out_shape=(
            jax.ShapeDtypeStruct((CX, CY, 8, LANES), F32),
            jax.ShapeDtypeStruct((2, CX, 16, LANES), F32),
            jax.ShapeDtypeStruct((SEND, 8, LANES), F32),
            jax.ShapeDtypeStruct((OWN_X * OWN_Y, 2, 8, LANES), F32),
            jax.ShapeDtypeStruct((4, 8, LANES), F32),
        ),
        in_specs=[pl.BlockSpec(memory_space=pltpu.SMEM)] + [spec] * 6,
        out_specs=(spec,) * 5,
        scratch_shapes=[vmem(PY, PX, LANES)] * 12
        + [vmem(cells * 2, 8, LANES)] * 3
        + [vmem(cells, 8, LANES)] * 3,
    )(*args)


def cycle_call(*args):
    spec = pl.BlockSpec(memory_space=pltpu.VMEM)
    points = NI * NJ
    rows = OWN_X * OWN_Y * 8
    return pl.pallas_call(
        cycle_kernel,
        out_shape=jax.ShapeDtypeStruct((rows, 2 * LANES), F32),
        in_specs=[pl.BlockSpec(memory_space=pltpu.SMEM)] + [spec] * 5,
        out_specs=spec,
        scratch_shapes=[vmem(points, 8, LANES)] * 6 + [vmem(rows, 2 * LANES)] * 2,
    )(*args)


def complex_inverse(real, imag):
    modulus = real * real + imag * imag
    return real / modulus, -imag / modulus


def material_tables(er, ei):
    med_r = WAVE_SQUARED * (er + SHIFT_IMAG * ei)
    med_i = WAVE_SQUARED * (ei - SHIFT_IMAG * er)
    inv_r, inv_i = complex_inverse(128.0 / 30.0 - med_r, -med_i)
    src_r = SOURCE_GAIN * (er - 1.0)
    src_i = SOURCE_GAIN * ei
    g_r = DAMPING * (inv_r * src_r - inv_i * src_i)
    g_i = DAMPING * (inv_r * src_i + inv_i * src_r)
    ci_r, ci_i = complex_inverse(128.0 / 120.0 - med_r, -med_i)
    scale = DAMPING / 30.0
    rows = jnp.stack(
        [g_r, g_i, scale * inv_r, scale * inv_i, 1.2 * src_r, 1.2 * src_i,
         DAMPING * ci_r, DAMPING * ci_i]
    )
    return jnp.pad(rows, ((0, 0), (0, LANES - MAT)))


def local(labels, permittivity_real, permittivity_imag, angles, angle_pick):
    gx_n = lax.axis_size("gx")
    gy_n = lax.axis_size("gy")
    gx = lax.axis_index("gx")
    gy = lax.axis_index("gy")
    core = gy % 2
    x0 = OWN_X * gx - LOW * core
    y0 = 2 * OWN_Y * (gy // 2) - LOW
    is_low = core == 0

    def along_x(values, by):
        pairs = []
        for j in range(gy_n):
            step = by if j % 2 == 0 else -by
            for i in range(gx_n):
                if 0 <= i + step < gx_n:
                    pairs.append(((i + step) * gy_n + j, i * gy_n + j))
        return lax.ppermute(values, ("gx", "gy"), pairs)

    def along_y(values, by):
        pairs = [(j, j + by) for j in range(gy_n) if 0 <= j + by < gy_n]
        return lax.ppermute(values, "gy", pairs)

    def core_swap(values):
        return lax.ppermute(values, "gy", [(j, j ^ 1) for j in range(gy_n)])

    other = core_swap(labels)
    both = jnp.where(
        is_low,
        jnp.concatenate([labels, other], axis=1),
        jnp.concatenate([other, labels], axis=1),
    )
    far = along_x(jnp.where(is_low, both[:4], both[2:]), 2)
    near = along_x(both, 1)
    region = jnp.where(
        is_low,
        jnp.concatenate([both, near, far], axis=0),
        jnp.concatenate([far, near, both], axis=0),
    )
    region = jnp.transpose(region, (1, 0, 2))
    low = along_y(region[2 * OWN_Y - LOW :], 2)
    high = along_y(region[: PY - LOW - 2 * OWN_Y], -2)

    table = material_tables(permittivity_real, permittivity_imag)
    pick = (angle_pick[:, None] == jnp.arange(NANG, dtype=jnp.int32)[None, :]).astype(F32)
    incidence = jnp.sum(pick * angles[None, :], axis=1)
    wavenumber = jnp.sqrt(WAVE_SQUARED)
    pos_x = (x0 + jnp.arange(PX, dtype=jnp.int32)).astype(F32)
    pos_y = (y0 + jnp.arange(PY, dtype=jnp.int32)).astype(F32)
    phase_x = wavenumber * (jnp.cos(incidence)[None, :] * pos_x[:, None])
    phase_y = wavenumber * (jnp.sin(incidence)[None, :] * pos_y[:, None])
    phases = jnp.concatenate([phase_x, phase_y], axis=0)
    cosine, sine = lax.optimization_barrier((jnp.cos(phases), jnp.sin(phases)))
    cx, sx, cy, sny = cosine[:PX], sine[:PX], cosine[PX:], sine[PX:]
    ex = jnp.stack(
        [jnp.concatenate([cx, cx], axis=1), jnp.concatenate([sx, sx], axis=1)], axis=1
    )
    ey = jnp.stack(
        [jnp.concatenate([cy, sny], axis=1), jnp.concatenate([-sny, cy], axis=1)], axis=1
    )
    ex = jnp.broadcast_to(ex[..., None], (PX, 2, 8, LANES))
    ey = jnp.broadcast_to(ey[..., None], (PY, 2, 8, LANES))
    scalars = jnp.stack(
        [core, x0, y0, jnp.int32(OWN_X * gx_n), jnp.int32(OWN_Y * gy_n)]
    ).astype(jnp.int32)
    c1, ck, send, it2, inv = region_call(scalars, region, low, high, table, ex, ey)
    recv = core_swap(send)
    out = cycle_call(scalars, c1, ck, recv, it2, inv)
    return out.reshape(2, 4, OWN_X, OWN_Y, 2 * LANES)


def solution(mesh):
    return jax.shard_map(
        local,
        mesh=mesh,
        in_specs=(P("gx", "gy", None), P(), P(), P(), P()),
        out_specs=P(None, None, "gx", "gy", None),
        check_vma=False,
    )
```

time: 167 us -> 69 us (0.41)
  starting transfers between devices: 87.3 us -> 23.3 us
  Pallas kernels: 0 us -> 27.4 us
  waiting for transfers between devices: 33.2 us -> 10.1 us
  other arithmetic: 21.9 us -> 0.72 us
  local copies, waits for them, and re-layouts: 22.6 us -> 6.63 us
    ppermute x24 -> x6, starting transfers between devices: 87.3 us -> 23.3 us  [the longest x2 13.7 us: along_x(): return lax.ppermute(values, ('gx', 'gy'), pairs)]
    pallas_call x0 -> x2, Pallas kernels: none -> 27.4 us  [the longest x1 21.7 us: region_call(): pl.pallas_call(region_kernel, out_shape=(jax.ShapeDtypeStruct((CX, CY, 8,...]
    ppermute x24 -> x6, waiting for transfers between devices: 33.2 us -> 10.1 us  [the longest x2 4.5 us: along_x(): return lax.ppermute(values, ('gx', 'gy'), pairs)]
    slice x19 -> x3, local copies, waits for them, and re-layouts: 11.3 us -> 0.1 us  [the longest x1 0.07 us: local(): cx, sx, cy, sny = (cosine[:PX], sine[:PX], cosine[PX:], sine[PX:])]
    another operation x8 -> x7, other arithmetic: 10.6 us -> 0.06 us  [the longest x3 0.03 us: material_tables(): jnp.stack([g_r, g_i, scale * inv_r, scale * inv_i, 1.2 * src_r, 1.2 * src...]
    another operation x4, local copies, waits for them, and re-layouts: 6.46 us -> 0.8 us  [the longest x1 0.6 us: local(): jnp.stack([core, x0, y0, jnp.int32(OWN_X * gx_n), jnp.int32(OWN_Y * gy_n)])]
    reshape x1 -> x0, local copies, waits for them, and re-layouts: 4.33 us -> none  [prolong_axis(): return stacked.reshape(new_shape)]
    sub x17 -> x0, other arithmetic: 4.12 us -> none  [the longest x2 2.77 us: local(): source - apply_operator(iterate, fine_padded(iterate), medium, 1.0)]
  transfers between devices with their start and end apart: 24 -> 6, of which waited for: 15 -> 3; matrix products, arithmetic and copies ran while one was open for 1% -> 3% of each run, Pallas kernels for 0% -> 0%
where the time goes in v1:
time: 69 us; the launch traced here: 68.4 us
  Pallas kernels  27.4 us (40%)
  starting transfers between devices  23.3 us (34%)
  waiting for transfers between devices  10.1 us (15%)
  local copies, waits for them, and re-layouts  6.63 us (10%)
  other arithmetic  0.72 us (1%)
    pallas_call x1, Pallas kernels, region_call(): pl.pallas_call(region_kernel, out_shape=(jax.ShapeDtypeStruct((CX, CY, 8,...  21.7 us
    ppermute x2, starting transfers between devices, along_x(): return lax.ppermute(values, ('gx', 'gy'), pairs)  13.7 us
    ppermute x2, starting transfers between devices, along_y(): return lax.ppermute(values, 'gy', pairs)  5.83 us
    pallas_call x1, Pallas kernels, cycle_call(): pl.pallas_call(cycle_kernel, out_shape=jax.ShapeDtypeStruct((rows, 2 * LA...  5.74 us
    ppermute x2, waiting for transfers between devices, along_x(): return lax.ppermute(values, ('gx', 'gy'), pairs)  4.5 us
    ppermute x2, starting transfers between devices, core_swap(): return lax.ppermute(values, 'gy', [(j, j ^ 1) for j in range(gy_n)])  3.83 us
    ppermute x2, waiting for transfers between devices, along_y(): return lax.ppermute(values, 'gy', pairs)  3.7 us
    unnamed x17, local copies, waits for them, and re-layouts  3.5 us
  transfers between devices with their start and end apart: 6, of which 3 were waited for; matrix products, arithmetic and copies ran while one was open for 3% of the time, Pallas kernels for 0%

profile of v1, /device:TPU:38, one launch (start us, length us, event | category | flops | bytes accessed | tf_op | source)
XLA Modules:
  0.0 68.4 jit_solution(8788843214991653652)
XLA Ops:
  0.0 0.8 %copy.12 = s32[6,8,256]{2,0,1:T(8,128)S(1)} copy(s32[6,8,256]{2,1,0:T(8,128)} %param.5) | data formatting | bytes 98304 | tf_op args[0]
  0.8 1.9 %collective-permute-start = (s32[6,8,256]{2,0,1:T(8,128)S(1)}, s32[6,8,256]{2,0,1:T(8,128)S(1)}, u32[]{:S(2)}, u32[]{:S(2)}) collective-permute-start(s32[6,8,256]{2,0,1:T(8,128)S(1)} %copy.12), channel_id=1, source_target_pairs={{0,1},{1,0},{2,3},{3,2},{4,5},{5,4},{6,7},{7,6},{8,9},{9,8},{10,11... | collective-permute-start | bytes 147464 | tf_op jit(solution)/shard_map/ppermute | solution.py:451
  2.8 0.0 copy-start.4
  2.8 0.0 copy-start.7
  2.8 0.6 copy-done.4
  3.5 0.2 select_reduce_fusion
  3.7 0.1 multiply_multiply_fusion.1
  3.8 0.1 multiply_multiply_fusion
  3.9 0.1 fusion.1
  4.0 0.1 slice.30
  4.1 0.1 fusion.5
  4.1 0.6 copy-done.5
  4.7 0.0 copy-done.6
  4.8 0.1 copy.14
  4.9 11.2 %collective-permute-start.1 = (s32[6,16,256]{2,0,1:T(8,128)S(1)}, s32[6,16,256]{2,0,1:T(8,128)S(1)}, u32[]{:S(2)}, u32[]{:S(2)}) collective-permute-start(s32[6,16,256]{2,0,1:T(8,128)S(1)} %add_select_fusion.1), channel_id=1, source_target_pairs={{16,0},{32,16},{48,32},{64,48},{80,64},{96,80},{112,96},{128,112},... | collective-permute-start | bytes 294920 | tf_op jit(solution)/shard_map/ppermute | solution.py:444
  16.2 2.5 %collective-permute-start.2 = (s32[4,16,256]{2,0,1:T(4,128)S(1)}, s32[4,16,256]{2,0,1:T(4,128)S(1)}, u32[]{:S(2)}, u32[]{:S(2)}) collective-permute-start(s32[4,16,256]{2,0,1:T(4,128)S(1)} %slice_select_fusion), channel_id=1, source_target_pairs={{32,0},{48,16},{64,32},{80,48},{96,64},{112,80},{128,96},{144,112}... | collective-permute-start | bytes 196616 | tf_op jit(solution)/shard_map/ppermute | solution.py:444
  18.6 0.1 copy.15
  18.7 4.5 %collective-permute-done.2 = s32[4,16,256]{2,0,1:T(4,128)S(1)} collective-permute-done((s32[4,16,256]{2,0,1:T(4,128)S(1)}, s32[4,16,256]{2,0,1:T(4,128)S(1)}, u32[]{:S(2)}, u32[]{:S(2)}) %collective-permute-start.2) | collective-permute-done | bytes 65568 | tf_op jit(solution)/shard_map/ppermute | solution.py:444
  23.2 0.1 fusion.mid
  23.4 0.6 copy-done
  24.0 2.3 %collective-permute-start.4 = (s32[9,16,256]{2,1,0:T(8,128)S(1)}, s32[9,16,256]{2,1,0:T(8,128)S(1)}, u32[]{:S(2)}, u32[]{:S(2)}) collective-permute-start(s32[9,16,256]{2,1,0:T(8,128)S(1)} %slice.35), channel_id=1, source_target_pairs={{2,0},{3,1},{4,2},{5,3},{6,4},{7,5},{8,6},{9,7},{10,8},{11,9},{12,... | collective-permute-start | bytes 442376 | tf_op jit(solution)/shard_map/ppermute | solution.py:448
  26.4 3.5 %collective-permute-start.3 = (s32[10,16,256]{2,1,0:T(8,128)S(1)}, s32[10,16,256]{2,1,0:T(8,128)S(1)}, u32[]{:S(2)}, u32[]{:S(2)}) collective-permute-start(s32[10,16,256]{2,1,0:T(8,128)S(1)} %slice.34), channel_id=1, source_target_pairs={{0,2},{1,3},{2,4},{3,5},{4,6},{5,7},{6,8},{7,9},{8,10},{9,11},{10,... | collective-permute-start | bytes 491528 | tf_op jit(solution)/shard_map/ppermute | solution.py:448
  29.9 0.6 pad.4.tab
  30.5 0.6 stack.60.sc
  31.1 3.7 %collective-permute-done.3.low = s32[10,16,256]{2,1,0:T(8,128)S(1)} collective-permute-done((s32[10,16,256]{2,1,0:T(8,128)S(1)}, s32[10,16,256]{2,1,0:T(8,128)S(1)}, u32[]{:S(2)}, u32[]{:S(2)}) %collective-permute-start.3) | collective-permute-done | bytes 163872 | tf_op jit(solution)/shard_map/ppermute | solution.py:448
  34.8 0.8 %broadcast_in_dim.4.ex = f32[16,2,8,128]{3,2,1,0:T(8,128)} broadcast(f32[16,2,8]{2,1,0:T(2,128)S(1)} %copy.14), dimensions={0,1,2} | broadcast | bytes 132096 | tf_op jit(solution)/shard_map/broadcast_in_dim | solution.py:487
  35.6 0.8 %broadcast_in_dim.5.ey = f32[35,2,8,128]{3,2,1,0:T(8,128)} broadcast(f32[35,2,8]{2,1,0:T(2,128)S(1)} %copy.15), dimensions={0,1,2} | broadcast | bytes 288960 | tf_op jit(solution)/shard_map/broadcast_in_dim | solution.py:488
  36.4 21.7 %shard_map.55 = (f32[5,15,8,128]{3,2,1,0:T(8,128)}, f32[2,5,16,128]{3,2,1,0:T(8,128)}, f32[91,8,128]{2,1,0:T(8,128)}, f32[48,2,8,128]{3,2,1,0:T(8,128)}, f32[4,8,128]{2,1,0:T(8,128)}) custom-call(s32[5]{0:T(128)} %stack.60.sc, s32[16,16,256]{2,1,0:T(8,128)} %copy-done, s32[10,16,256]{2,1,0:T(8,128)} %copy-done.2, s32[9,16,256]{2,1,0:T(8,128)} %copy-done.3, ...), custom_call_target="tpu_custom_call" | custom-call | tf_op jit(solution)/shard_map/pallas_call | solution.py:375
  58.1 1.9 %collective-permute-start.5 = (f32[91,8,128]{2,1,0:T(8,128)}, f32[91,8,128]{2,1,0:T(8,128)S(1)}, u32[]{:S(2)}, u32[]{:S(2)}) collective-permute-start(f32[91,8,128]{2,1,0:T(8,128)} %get-tuple-element.16), channel_id=1, source_target_pairs={{0,1},{1,0},{2,3},{3,2},{4,5},{5,4},{6,7},{7,6},{8,9},{9,8},{10,11... | collective-permute-start | bytes 1118216 | tf_op jit(solution)/shard_map/ppermute | solution.py:451
  60.0 1.9 %collective-permute-done.5.recv = f32[91,8,128]{2,1,0:T(8,128)S(1)} collective-permute-done((f32[91,8,128]{2,1,0:T(8,128)}, f32[91,8,128]{2,1,0:T(8,128)S(1)}, u32[]{:S(2)}, u32[]{:S(2)}) %collective-permute-start.5) | collective-permute-done | bytes 372768 | tf_op jit(solution)/shard_map/ppermute | solution.py:451
  61.9 0.8 %copy-done.1 = f32[91,8,128]{2,1,0:T(8,128)} copy-done((f32[91,8,128]{2,1,0:T(8,128)}, f32[91,8,128]{2,1,0:T(8,128)S(1)}, u32[]{:S(2)}) %copy-start.1) | copy-done | bytes 372760
  62.6 5.7 %shard_map.56 = f32[384,256]{1,0:T(8,128)} custom-call(s32[5]{0:T(128)} %stack.60.sc, f32[5,15,8,128]{3,2,1,0:T(8,128)} %get-tuple-element.14.c1_own, f32[2,5,16,128]{3,2,1,0:T(8,128)} %get-tuple-element.15.ck_own, f32[91,8,128]{2,1,0:T(8,128)} %copy-done.1, f32[48,2,8,128]{3,2,1,0:T(8,128)} %get-tuple-element.17.it2, f32[4,8,128]{2,1,0:T(8,128)} %get-tuple-element.18.inv), custom_call_target="tpu_custom_call" | custom-call | tf_op jit(solution)/shard_map/pallas_call | solution.py:396
  (27 shorter events, 0.2 us)
Async XLA Ops:
  0.8 4.1 %collective-permute-start = (s32[6,8,256]{2,0,1:T(8,128)S(1)}, s32[6,8,256]{2,0,1:T(8,128)S(1)}, u32[]{:S(2)}, u32[]{:S(2)}) collective-permute-start(s32[6,8,256]{2,0,1:T(8,128)S(1)} %copy.12), channel_id=1, source_target_pairs={{0,1},{1,0},{2,3},{3,2},{4,5},{5,4},{6,7},{7,6},{8,9},{9,8},{10,11... | collective-permute-start | bytes 147464 | tf_op jit(solution)/shard_map/ppermute | solution.py:451
  2.8 0.7 %copy-start.4 = (f32[360]{0:T(512)S(1)}, f32[360]{0:T(512)}, u32[]{:S(2)}) copy-start(f32[360]{0:T(512)} %param.8) | copy-start | bytes 4324
  2.8 0.7 copy-start.7
  4.0 0.7 copy-start.5
  4.0 0.7 copy-start.6
  4.9 18.3 %collective-permute-start.1 = (s32[6,16,256]{2,0,1:T(8,128)S(1)}, s32[6,16,256]{2,0,1:T(8,128)S(1)}, u32[]{:S(2)}, u32[]{:S(2)}) collective-permute-start(s32[6,16,256]{2,0,1:T(8,128)S(1)} %add_select_fusion.1), channel_id=1, source_target_pairs={{16,0},{32,16},{48,32},{64,48},{80,64},{96,80},{112,96},{128,112},... | collective-permute-start | bytes 294920 | tf_op jit(solution)/shard_map/ppermute | solution.py:444
  16.2 7.1 %collective-permute-start.2 = (s32[4,16,256]{2,0,1:T(4,128)S(1)}, s32[4,16,256]{2,0,1:T(4,128)S(1)}, u32[]{:S(2)}, u32[]{:S(2)}) collective-permute-start(s32[4,16,256]{2,0,1:T(4,128)S(1)} %slice_select_fusion), channel_id=1, source_target_pairs={{32,0},{48,16},{64,32},{80,48},{96,64},{112,80},{128,96},{144,112}... | collective-permute-start | bytes 196616 | tf_op jit(solution)/shard_map/ppermute | solution.py:444
  23.3 0.7 %copy-start = (s32[16,16,256]{2,1,0:T(8,128)}, s32[16,16,256]{2,1,0:T(8,128)S(1)}, u32[]{:S(2)}) copy-start(s32[16,16,256]{2,1,0:T(8,128)S(1)} %fusion.mid) | copy-start | bytes 786436
  24.0 7.1 %collective-permute-start.4 = (s32[9,16,256]{2,1,0:T(8,128)S(1)}, s32[9,16,256]{2,1,0:T(8,128)S(1)}, u32[]{:S(2)}, u32[]{:S(2)}) collective-permute-start(s32[9,16,256]{2,1,0:T(8,128)S(1)} %slice.35), channel_id=1, source_target_pairs={{2,0},{3,1},{4,2},{5,3},{6,4},{7,5},{8,6},{9,7},{10,8},{11,9},{12,... | collective-permute-start | bytes 442376 | tf_op jit(solution)/shard_map/ppermute | solution.py:448
  26.4 8.4 %collective-permute-start.3 = (s32[10,16,256]{2,1,0:T(8,128)S(1)}, s32[10,16,256]{2,1,0:T(8,128)S(1)}, u32[]{:S(2)}, u32[]{:S(2)}) collective-permute-start(s32[10,16,256]{2,1,0:T(8,128)S(1)} %slice.34), channel_id=1, source_target_pairs={{0,2},{1,3},{2,4},{3,5},{4,6},{5,7},{6,8},{7,9},{8,10},{9,11},{10,... | collective-permute-start | bytes 491528 | tf_op jit(solution)/shard_map/ppermute | solution.py:448
  31.1 5.3 %copy-start.3 = (s32[9,16,256]{2,1,0:T(8,128)}, s32[9,16,256]{2,1,0:T(8,128)S(1)}, u32[]{:S(2)}) copy-start(s32[9,16,256]{2,1,0:T(8,128)S(1)} %collective-permute-done.4.high) | copy-start | bytes 442372
  34.8 1.6 %copy-start.2 = (s32[10,16,256]{2,1,0:T(8,128)}, s32[10,16,256]{2,1,0:T(8,128)S(1)}, u32[]{:S(2)}) copy-start(s32[10,16,256]{2,1,0:T(8,128)S(1)} %collective-permute-done.3.low) | copy-start | bytes 491524
  58.1 3.8 %collective-permute-start.5 = (f32[91,8,128]{2,1,0:T(8,128)}, f32[91,8,128]{2,1,0:T(8,128)S(1)}, u32[]{:S(2)}, u32[]{:S(2)}) collective-permute-start(f32[91,8,128]{2,1,0:T(8,128)} %get-tuple-element.16), channel_id=1, source_target_pairs={{0,1},{1,0},{2,3},{3,2},{4,5},{5,4},{6,7},{7,6},{8,9},{9,8},{10,11... | collective-permute-start | bytes 1118216 | tf_op jit(solution)/shard_map/ppermute | solution.py:451
  61.9 0.8 %copy-start.1 = (f32[91,8,128]{2,1,0:T(8,128)}, f32[91,8,128]{2,1,0:T(8,128)S(1)}, u32[]{:S(2)}) copy-start(f32[91,8,128]{2,1,0:T(8,128)S(1)} %collective-permute-done.5.recv) | copy-start | bytes 1118212

commit v2 on v1

v2 whole, which is shorter than its diff:
```python
import jax
import jax.numpy as jnp
from jax import lax
from jax.experimental import pallas as pl
from jax.experimental.pallas import tpu as pltpu
from jax.sharding import PartitionSpec as P

NANG = 360
MAT = 8
DAMPING = 0.8
WAVE_SQUARED = 0.1
SHIFT_IMAG = 0.5
SOURCE_GAIN = 4.0

OWN_X = 6
OWN_Y = 8
PX = 16
PY = 35
LOW = 10
CX, CY = 5, 15
NI, NJ = 10, 11
LANES = 128
F32 = jnp.float32
OUTSIDE = 8


def lane_iota():
    return lax.broadcasted_iota(jnp.int32, (8, LANES), 1)


def sign_rows():
    rows = lax.broadcasted_iota(jnp.int32, (8, LANES), 0)
    return jnp.where(rows < 4, -1.0, 1.0).astype(F32)


def up(values, first):
    return jnp.where(first, 0.0, pltpu.roll(values, 1, 1))


def down(values, last):
    return jnp.where(last, 0.0, pltpu.roll(values, LANES - 1, 1))


def turned(values):
    return pltpu.roll(values, 4, 0)


def row_of(ref, y, x):
    return jnp.broadcast_to(ref[y, pl.ds(x, 1), :], (8, LANES))


def edge_face(values, near):
    edge = (3.0 / 14.0) * (values + (1.0 / 3.0) * near)
    face = values + (3.0 / 14.0) * near
    return edge, face


def where_am_i():
    gx = lax.axis_index("gx")
    gy = lax.axis_index("gy")
    core = lax.rem(gy, 2)
    x0 = OWN_X * gx - LOW * core
    y0 = OWN_Y * (gy - core) - LOW
    return core, x0, y0


def wave_kernel(ex, ey, wave):
    def rows(y, carry):
        w = ey[y, 0]
        w_t = ey[y, 1]
        for x in range(PX):
            c = ex[x, 0]
            s = ex[x, 1]
            wave[(y * PX + x) * 2] = c * w + s * w_t
            wave[(y * PX + x) * 2 + 1] = c * w_t - s * w
        return carry

    lax.fori_loop(0, PY, rows, 0)


def row_loop(first, count, step, body):
    def some(n, carry):
        for k in range(step):
            body(first + n * step + k)
        return carry

    lax.fori_loop(0, count // step, some, 0)


class Region:
    def __init__(self, sizes, tab, wave, shared, scratch):
        self.nx, self.ny = sizes
        self.core, self.x0, self.y0 = where_am_i()
        self.tab = tab
        self.wave = wave
        (self.ie_r, self.io_r, self.ie_i, self.io_i, self.kr, self.ki,
         self.it1, self.pp, self.qq, self.va, self.vb, self.sy) = shared
        (self.ge_r, self.go_r, self.ge_i, self.go_i, self.sa_r, self.sa_i,
         self.apart) = scratch
        lanes = lane_iota()
        self.first = lanes == 0
        self.last = lanes == LANES - 1
        self.sgn = sign_rows()
        rows = lax.broadcasted_iota(jnp.int32, (2 * LANES, 2 * LANES), 0)
        cols = lax.broadcasted_iota(jnp.int32, (2 * LANES, 2 * LANES), 1)
        source = jnp.where(cols < LANES, 2 * cols, 2 * (cols - LANES) + 1)
        self.perm = jnp.where(rows == source, 1.0, 0.0).astype(jnp.bfloat16)

    def pick(self, row, index):
        table = jnp.broadcast_to(self.tab[row : row + 1, :], (8, LANES))
        return jnp.take_along_axis(table, index, axis=1, mode="promise_in_bounds")

    def tables(self, labels, first_row, count, step):
        flat = labels[...].reshape(count * PX, 2 * LANES).astype(F32).astype(jnp.bfloat16)
        self.apart[0 : count * PX, :] = jnp.dot(
            flat, self.perm, preferred_element_type=F32
        )
        rows = lax.broadcasted_iota(jnp.int32, (8, LANES), 0)
        inside = []
        for h in range(2):
            xs = self.x0 + 8 * h + rows
            inside.append(jnp.logical_and(xs >= 0, xs < self.nx))

        def some(n, carry):
            for k in range(step):
                y = first_row + n * step + k
                y_in = jnp.logical_and(self.y0 + y >= 0, self.y0 + y < self.ny)
                beyond = jnp.where(y_in, 0, OUTSIDE)
                for h in range(2):
                    start = pl.multiple_of((n * step + k) * PX + 8 * h, 8)
                    part = self.apart[pl.ds(start, 8), :]
                    at = (y, pl.ds(8 * h, 8), slice(None))
                    halves = []
                    for odd, (inv_r, inv_i, g_r, g_i) in enumerate(
                        (
                            (self.ie_r, self.ie_i, self.ge_r, self.ge_i),
                            (self.io_r, self.io_i, self.go_r, self.go_i),
                        )
                    ):
                        label = part[:, odd * LANES : (odd + 1) * LANES].astype(jnp.int32)
                        index = jnp.where(inside[h], label, OUTSIDE) + beyond
                        ir = self.pick(0, index)
                        ii = self.pick(1, index)
                        sr = self.pick(2, index)
                        si = self.pick(3, index)
                        inv_r[at] = ir
                        inv_i[at] = ii
                        g_r[at] = (25.0 / 14.0) * (ir * sr - ii * si)
                        g_i[at] = (25.0 / 14.0) * (ir * si + ii * sr)
                        halves.append((sr, si))
                        if odd and (first_row + k) % 2 == 1:
                            self.kr[at] = self.pick(4, index)
                            self.ki[at] = self.pick(5, index)
                    for c, out in ((0, self.sa_r), (1, self.sa_i)):
                        se = halves[0][c]
                        out[at] = se + down(se, self.last) + 2.0 * halves[1][c]
            return carry

        lax.fori_loop(0, count // step, some, 0)

    def first_stage(self, y):
        edges, faces, centres = [[], []], [[], []], [[], []]
        for x in range(PX):
            at = (y * PX + x) * 2
            e = self.wave[at]
            e_t = self.wave[at + 1]
            even = row_of(self.ge_r, y, x) * e + row_of(self.ge_i, y, x) * e_t
            odd = row_of(self.go_r, y, x) * e + row_of(self.go_i, y, x) * e_t
            if 2 <= x <= 12:
                self.sy[y * PX + x] = (
                    row_of(self.sa_r, y, x) * e + row_of(self.sa_i, y, x) * e_t
                )
            self.it1[at] = even
            self.it1[at + 1] = odd
            near_e = odd + up(odd, self.first)
            near_o = even + down(even, self.last)
            for h, (v, near) in enumerate(((even, near_e), (odd, near_o))):
                edge, face = edge_face(v, near)
                edges[h].append(edge)
                faces[h].append(face)
                centres[h].append(near)
        for x in range(PX):
            at = (y * PX + x) * 2
            for h in range(2):
                p = centres[h][x]
                q = faces[h][x]
                if 0 < x < PX - 1:
                    p = p + (faces[h][x - 1] + faces[h][x + 1])
                    q = q + (edges[h][x - 1] + edges[h][x + 1])
                else:
                    beside = x - 1 if x else x + 1
                    p = p + faces[h][beside]
                    q = q + edges[h][beside]
                self.pp[at + h] = p
                self.qq[at + h] = q

    def update(self, y, x, h):
        at = (y * PX + x) * 2 + h
        row = PX * 2
        ir, ii = ((self.ie_r, self.ie_i), (self.io_r, self.io_i))[h]
        n = self.pp[at] + (self.qq[at - row] + self.qq[at + row])
        return row_of(ir, y, x) * n + row_of(ii, y, x) * (self.sgn * turned(n))

    def second_stage(self, y):
        for x in range(1, 14):
            at = (y * PX + x) * 2
            we = 0.4 * self.it1[at] + self.update(y, x, 0)
            wo = 0.4 * self.it1[at + 1] + self.update(y, x, 1)
            p = we + down(we, self.last)
            half = p + wo
            after = jnp.where(self.last, -wo, pltpu.roll(wo, LANES - 1, 1))
            self.va[y * PX + x] = half + wo
            self.vb[y * PX + x] = (up(wo, self.first) + after) + 2.0 * half

    def third_stage(self, j, c1_out, ck_out):
        base = (2 + 2 * j) * PX
        gs, hs = {}, {}
        for x in range(1, 14):

            def combos(ref):
                vm, v0, v1, v2, v3 = (ref[base + (d - 1) * PX + x] for d in range(5))
                half = (v0 + v2) + v1
                return half + v1, (vm + v3) + 2.0 * half

            aa, ba = combos(self.va)
            ab, bb = combos(self.vb)
            u = ba + ab
            if 2 <= x <= 12:
                at = base + x
                gs[x] = (14.0 * u + 3.0 * bb) + (
                    (self.sy[at] + self.sy[at + 2 * PX]) + 2.0 * self.sy[at + PX]
                )
            hs[x] = 14.0 * aa + (3.0 * u + bb)
        for i in range(CX):
            b = 2 + 2 * i
            mx = jnp.where(self.x0 + b + 2 == self.nx, 1.0, 2.0).astype(F32)
            raw = (
                (gs[b] + gs[b + 2])
                + 2.0 * (gs[b + 1] + (hs[b] + hs[b + 2]))
                + (hs[b - 1] + hs[b + 3])
                + mx * hs[b + 1]
            ) * (1.0 / 1920.0)
            kr = row_of(self.kr, 3 + 2 * j, b + 1)
            ki = row_of(self.ki, 3 + 2 * j, b + 1)
            c1_out[i, j] = kr * raw + ki * (self.sgn * turned(raw))
            ck_out[0, i, pl.ds(j, 1), :] = self.kr[3 + 2 * j, b + 1 : b + 2, :]
            ck_out[1, i, pl.ds(j, 1), :] = self.ki[3 + 2 * j, b + 1 : b + 2, :]


def middle_kernel(sizes, labels, tab, wave, *refs):
    region = Region(sizes, tab, wave, refs[:12], refs[12:])
    region.tables(labels, LOW, 2 * OWN_Y, 8)
    row_loop(LOW, 2 * OWN_Y, 2, region.first_stage)
    row_loop(LOW + 1, 2 * OWN_Y - 2, 2, region.second_stage)


def outer_kernel(sizes, low, high, tab, wave, *refs):
    region = Region(sizes, tab, wave, refs[12:24], refs[29:])
    c1_out, ck_out, send_out, it2_out, inv_out = refs[24:29]
    core, y0, ny = region.core, region.y0, region.ny
    it1 = region.it1
    top = LOW + 2 * OWN_Y
    region.tables(low, 0, LOW, LOW)
    row_loop(0, LOW, 2, region.first_stage)
    row_loop(1, LOW, 2, region.second_stage)
    region.tables(high, top, PY - top, PY - top)
    row_loop(top, PY - top, 3, region.first_stage)
    row_loop(top - 1, PY - top, 3, region.second_stage)

    @pl.when(y0 + top == ny)
    def _():
        for x in range(1, 14):
            for ref in (region.va, region.vb):
                ref[(top + 1) * PX + x] = -ref[(top - 1) * PX + x]

    for k in range(2):
        for i in range(CX):
            ck_out[k, i, 8:16, :] = jnp.zeros((8, LANES), F32)
    row_loop(0, CY, 1, lambda j: region.third_stage(j, c1_out, ck_out))

    xb = core * LOW
    yb = LOW + core * OWN_Y
    xe = core * (PX - 1)
    tables = (region.ie_r, region.io_r, region.ie_i, region.io_i)

    def own_stage(k):
        y = yb + k
        for xx in range(OWN_X):
            x = xb + xx
            at = (y * PX + x) * 2
            for h in range(2):
                it2_out[xx * OWN_Y + k, h] = 1.2 * it1[at + h] + region.update(y, x, h)
        for n, ref in enumerate(tables):
            inv_out[n, pl.ds(k, 1), :] = ref[y, pl.ds(xe, 1), :]

    row_loop(0, OWN_Y, 2, own_stage)

    j0 = 4 - 4 * core
    for i in range(CX):
        for j in range(NJ):
            send_out[i * NJ + j] = c1_out[i, j0 + j]
        for k in range(2):
            send_out[CX * NJ + (k * CX + i) * 2] = ck_out[k, i, 0:8, :]
            send_out[CX * NJ + (k * CX + i) * 2 + 1] = ck_out[k, i, 8:16, :]
    plane = 6 + 3 * core
    ys = LOW + OWN_Y - core * OWN_Y
    edges, faces = [], []
    for k in range(OWN_Y + 2):
        at = ((ys - 1 + k) * PX + plane) * 2
        even = it1[at]
        odd = it1[at + 1]
        ee, fe = edge_face(even, odd + up(odd, region.first))
        eo, fo = edge_face(odd, even + down(even, region.last))
        edges.append((ee, eo))
        faces.append((fe, fo))
    for k in range(OWN_Y):
        for h in range(2):
            send_out[CX * NJ + 4 * CX + 2 * k + h] = faces[k + 1][h] + (
                edges[k][h] + edges[k + 2][h]
            )


SEND = CX * NJ + 4 * CX + 2 * OWN_Y


def cycle_kernel(c1_own, ck_own, recv, it2, inv, out, c1, ckr, cki, cc, pp, qq, vv, o0, o1):
    core = where_am_i()[0]
    lanes = lane_iota()
    first = lanes == 0
    last = lanes == LANES - 1
    sgn = sign_rows()

    def spread(row):
        return jnp.broadcast_to(row, (8, LANES))

    def assemble(which):
        own_i, other_i, j0 = CX - which * CX, which * CX, 4 * which
        for i in range(CX):
            for j in range(NJ):
                at = (own_i + i) * NJ + j
                row = j0 + j
                c1[at] = c1_own[i, row]
                ckr[at] = spread(ck_own[0, i, row : row + 1, :])
                cki[at] = spread(ck_own[1, i, row : row + 1, :]) * sgn
                at = (other_i + i) * NJ + j
                c1[at] = recv[i * NJ + j]
                for k, ref in ((0, ckr), (1, cki)):
                    tile = CX * NJ + (k * CX + i) * 2 + row // 8
                    value = spread(recv[tile, row % 8 : row % 8 + 1, :])
                    ref[at] = value * sgn if k else value

    @pl.when(core == 0)
    def _():
        assemble(0)

    @pl.when(core == 1)
    def _():
        assemble(1)

    for sweep in range(3):
        ref = c1 if sweep == 0 else cc

        def sums(i, ref=ref, sweep=sweep):
            edges, faces, centres = {}, {}, {}
            for j in range(sweep, NJ - sweep):
                v = ref[i * NJ + j]
                near = up(v, first) + down(v, last)
                edges[j], faces[j] = edge_face(v, near)
                centres[j] = near
            for j in range(sweep + 1, NJ - sweep - 1):
                pp[i * NJ + j] = centres[j] + (faces[j - 1] + faces[j + 1])
                qq[i * NJ + j] = faces[j] + (edges[j - 1] + edges[j + 1])

        row_loop(sweep, NI - 2 * sweep, 2, sums)

        def relax(i, ref=ref, sweep=sweep):
            for j in range(sweep + 1, NJ - sweep - 1):
                at = i * NJ + j
                n = (pp[at] + (qq[at - NJ] + qq[at + NJ])) * (14.0 / 120.0)
                cc[at] = (0.2 * ref[at] + c1[at]) + (ckr[at] * n + cki[at] * turned(n))

        row_loop(sweep + 1, NI - 2 * sweep - 2, 2, relax)

    def put(x, y, value):
        col = x * OWN_Y + y
        even = 0.5 * (value + up(value, first))
        vv[col * 8 : col * 8 + 8, :LANES] = it2[col, 0] + even
        vv[col * 8 : col * 8 + 8, LANES:] = it2[col, 1] + value

    for i in range(OWN_X // 2):
        for j in range(OWN_Y // 2):
            at = (i + 4) * NJ + j + 4
            here = cc[at]
            left = cc[at - NJ]
            mix = 0.5 * (left + here)
            below = cc[at - 1]
            mix_below = 0.5 * (cc[at - NJ - 1] + below)
            put(2 * i + 1, 2 * j + 1, here)
            put(2 * i, 2 * j + 1, mix)
            put(2 * i + 1, 2 * j, 0.5 * (below + here))
            put(2 * i, 2 * j, 0.5 * (mix_below + mix))

    for k in range(OWN_Y):
        at = pl.multiple_of((core * (OWN_X - 1) * OWN_Y + k) * 8, 8)
        for h in range(2):
            n = recv[CX * NJ + 4 * CX + 2 * k + h]
            ir = spread(inv[h, k : k + 1, :])
            ii = spread(inv[2 + h, k : k + 1, :])
            where = (pl.ds(at, 8), slice(h * LANES, (h + 1) * LANES))
            vv[where] = vv[where] + (ir * n + (ii * sgn) * turned(n))

    rows = lax.broadcasted_iota(jnp.int32, (2 * LANES, 2 * LANES), 0)
    cols = lax.broadcasted_iota(jnp.int32, (2 * LANES, 2 * LANES), 1)
    target = jnp.where(rows < LANES, 2 * rows, 2 * (rows - LANES) + 1)
    perm = jnp.where(cols == target, 1.0, 0.0).astype(jnp.bfloat16)
    count = OWN_X * OWN_Y
    for x in range(OWN_X):
        value = vv[x * 64 : x * 64 + 64, :]
        top = value.astype(jnp.bfloat16)
        rest = value - top.astype(F32)
        middle = rest.astype(jnp.bfloat16)
        bottom = (rest - middle.astype(F32)).astype(jnp.bfloat16)
        mixed = (
            jnp.dot(bottom, perm, preferred_element_type=F32)
            + jnp.dot(middle, perm, preferred_element_type=F32)
        ) + jnp.dot(top, perm, preferred_element_type=F32)
        for y in range(OWN_Y):
            block = mixed[y * 8 : y * 8 + 8]
            o0[pl.ds(x * OWN_Y + y, 8, stride=count), :] = block[:, :LANES]
            o1[pl.ds(x * OWN_Y + y, 8, stride=count), :] = block[:, LANES:]
    out[:, :LANES] = o0[...]
    out[:, LANES:] = o1[...]


def vmem(*shape):
    return pltpu.VMEM(shape, F32)


SPEC = pl.BlockSpec(memory_space=pltpu.VMEM)
CELLS = PY * PX
SHARED = (vmem(PY, PX, LANES),) * 6 + (vmem(CELLS * 2, 8, LANES),) * 3 + (
    vmem(CELLS, 8, LANES),
) * 3
TABLES = [vmem(PY, PX, LANES)] * 6


def limit(mib):
    return pltpu.CompilerParams(vmem_limit_bytes=mib << 20)


def near_core(*arrays):
    return [pltpu.with_memory_space_constraint(a, pltpu.VMEM) for a in arrays]


def wave_call(ex, ey):
    return pl.pallas_call(
        wave_kernel,
        out_shape=vmem(CELLS * 2, 8, LANES),
        in_specs=[SPEC] * 2,
        out_specs=SPEC,
        compiler_params=limit(2),
    )(*near_core(ex, ey))


def middle_call(sizes, labels, tab, wave):
    def kernel(*refs):
        middle_kernel(sizes, *refs)

    return pl.pallas_call(
        kernel,
        out_shape=SHARED,
        in_specs=[SPEC] * 3,
        out_specs=(SPEC,) * 12,
        scratch_shapes=TABLES + [vmem(2 * OWN_Y * PX, 2 * LANES)],
        compiler_params=limit(6),
    )(*near_core(labels, tab, wave))


def outer_call(sizes, low, high, tab, wave, shared):
    def kernel(*refs):
        outer_kernel(sizes, *refs)

    results = pl.pallas_call(
        kernel,
        out_shape=SHARED
        + (
            vmem(CX, CY, 8, LANES),
            vmem(2, CX, 16, LANES),
            vmem(SEND, 8, LANES),
            vmem(OWN_X * OWN_Y, 2, 8, LANES),
            vmem(4, 8, LANES),
        ),
        in_specs=[SPEC] * 16,
        out_specs=(SPEC,) * 17,
        input_output_aliases={4 + n: n for n in range(12)},
        scratch_shapes=TABLES + [vmem(LOW * PX, 2 * LANES)],
        compiler_params=limit(6),
    )(*near_core(low, high, tab, wave), *shared)
    return results[12:]


def cycle_call(*args):
    points = NI * NJ
    rows = OWN_X * OWN_Y * 8
    return pl.pallas_call(
        cycle_kernel,
        out_shape=jax.ShapeDtypeStruct((rows, 2 * LANES), F32),
        in_specs=[SPEC] * 5,
        out_specs=SPEC,
        scratch_shapes=[vmem(points, 8, LANES)] * 6
        + [vmem(rows, 2 * LANES)]
        + [vmem(rows, LANES)] * 2,
        compiler_params=limit(8),
    )(*near_core(*args))


def complex_inverse(real, imag):
    modulus = real * real + imag * imag
    return real / modulus, -imag / modulus


def material_tables(er, ei):
    med_r = WAVE_SQUARED * (er + SHIFT_IMAG * ei)
    med_i = WAVE_SQUARED * (ei - SHIFT_IMAG * er)
    inv_r, inv_i = complex_inverse(128.0 / 30.0 - med_r, -med_i)
    src_r = SOURCE_GAIN * (er - 1.0)
    src_i = SOURCE_GAIN * ei
    ci_r, ci_i = complex_inverse(128.0 / 120.0 - med_r, -med_i)
    scale = 14.0 * DAMPING / 30.0
    rows = jnp.stack(
        [scale * inv_r, scale * inv_i, 1.2 * src_r, 1.2 * src_i,
         DAMPING * ci_r, DAMPING * ci_i]
    )
    return jnp.pad(rows, ((0, 2), (0, LANES - MAT)))


def local(labels, permittivity_real, permittivity_imag, angles, angle_pick):
    gx_n = lax.axis_size("gx")
    gy_n = lax.axis_size("gy")
    gx = lax.axis_index("gx")
    gy = lax.axis_index("gy")
    core = gy % 2
    x0 = OWN_X * gx - LOW * core
    y0 = 2 * OWN_Y * (gy // 2) - LOW
    is_low = core == 0

    def along_x(values, by):
        pairs = []
        for j in range(gy_n):
            step = by if j % 2 == 0 else -by
            for i in range(gx_n):
                if 0 <= i + step < gx_n:
                    pairs.append(((i + step) * gy_n + j, i * gy_n + j))
        return lax.ppermute(values, ("gx", "gy"), pairs)

    def along_y(values, by):
        pairs = [(j, j + by) for j in range(gy_n) if 0 <= j + by < gy_n]
        return lax.ppermute(values, "gy", pairs)

    def core_swap(values):
        return lax.ppermute(values, "gy", [(j, j ^ 1) for j in range(gy_n)])

    other = core_swap(labels)
    both = jnp.where(
        is_low,
        jnp.concatenate([labels, other], axis=1),
        jnp.concatenate([other, labels], axis=1),
    )
    far = along_x(jnp.where(is_low, both[:4], both[2:]), 2)
    near = along_x(both, 1)
    region = jnp.where(
        is_low,
        jnp.concatenate([both, near, far], axis=0),
        jnp.concatenate([far, near, both], axis=0),
    )
    region = jnp.transpose(region, (1, 0, 2))
    low = along_y(region[2 * OWN_Y - LOW :], 2)
    high = along_y(region[: PY - LOW - 2 * OWN_Y], -2)

    table = material_tables(permittivity_real, permittivity_imag)
    pick = (angle_pick[:, None] == jnp.arange(NANG, dtype=jnp.int32)[None, :]).astype(F32)
    incidence = jnp.sum(pick * angles[None, :], axis=1)
    wavenumber = jnp.sqrt(WAVE_SQUARED)
    pos_x = (x0 + jnp.arange(PX, dtype=jnp.int32)).astype(F32)
    pos_y = (y0 + jnp.arange(PY, dtype=jnp.int32)).astype(F32)
    phase_x = wavenumber * (jnp.cos(incidence)[None, :] * pos_x[:, None])
    phase_y = wavenumber * (jnp.sin(incidence)[None, :] * pos_y[:, None])
    phases = jnp.concatenate([phase_x, phase_y], axis=0)
    cosine, sine = lax.optimization_barrier((jnp.cos(phases), jnp.sin(phases)))
    cx, sx, cy, sny = cosine[:PX], sine[:PX], cosine[PX:], sine[PX:]
    ex = jnp.stack(
        [jnp.concatenate([cx, cx], axis=1), jnp.concatenate([sx, sx], axis=1)], axis=1
    )
    ey = jnp.stack(
        [jnp.concatenate([cy, sny], axis=1), jnp.concatenate([-sny, cy], axis=1)], axis=1
    )
    ex = jnp.broadcast_to(ex[..., None], (PX, 2, 8, LANES))
    ey = jnp.broadcast_to(ey[..., None], (PY, 2, 8, LANES))
    wave = wave_call(ex, ey)
    sizes = (OWN_X * gx_n, OWN_Y * gy_n)
    shared = middle_call(sizes, region, table, wave)
    c1, ck, send, it2, inv = outer_call(sizes, low, high, table, wave, shared)
    recv = core_swap(send)
    out = cycle_call(c1, ck, recv, it2, inv)
    return out.reshape(2, 4, OWN_X, OWN_Y, 2 * LANES)


def solution(mesh):
    return jax.shard_map(
        local,
        mesh=mesh,
        in_specs=(P("gx", "gy", None), P(), P(), P(), P()),
        out_specs=P(None, None, "gx", "gy", None),
        check_vma=False,
    )
```

time: 69 us -> 48.7 us (0.71)
  the two profiles are of different devices: /device:TPU:38 before, /device:TPU:31 now
where the time goes in v2:
time: 48.7 us; the launch traced here: 48.4 us
  starting transfers between devices  24 us (49%)
  Pallas kernels  13.7 us (28%)
  waiting for transfers between devices  7.06 us (14%)
  other arithmetic  2.07 us (4%)
  local copies, waits for them, and re-layouts  1.38 us (3%)
    ppermute x2, starting transfers between devices, along_x(): return lax.ppermute(values, ('gx', 'gy'), pairs)  9.81 us
    ppermute x2, starting transfers between devices, core_swap(): return lax.ppermute(values, 'gy', [(j, j ^ 1) for j in range(gy_n)])  7.65 us
    ppermute x2, starting transfers between devices, along_y(): return lax.ppermute(values, 'gy', pairs)  6.49 us
    ppermute x2, waiting for transfers between devices, along_x(): return lax.ppermute(values, ('gx', 'gy'), pairs)  5.75 us
    pallas_call x1, Pallas kernels, outer_call(): pl.pallas_call(kernel, out_shape=SHARED + (vmem(CX, CY, 8, LANES), vmem(2...  5.63 us
    pallas_call x1, Pallas kernels, middle_call(): pl.pallas_call(kernel, out_shape=SHARED, in_specs=[SPEC] * 3, out_specs=(...  4.34 us
    pallas_call x1, Pallas kernels, cycle_call(): pl.pallas_call(cycle_kernel, out_shape=jax.ShapeDtypeStruct((rows, 2 * LA...  3.14 us
    ppermute x2, waiting for transfers between devices, core_swap(): return lax.ppermute(values, 'gy', [(j, j ^ 1) for j in range(gy_n)])  1.3 us
  transfers between devices with their start and end apart: 6, of which 2 were waited for; matrix products, arithmetic and copies ran while one was open for 5% of the time, Pallas kernels for 10%

profile of v2, /device:TPU:31, one launch (start us, length us, event | category | flops | bytes accessed | tf_op | source)
XLA Modules:
  0.0 48.4 jit_solution(667628573519713353)
XLA Ops:
  0.0 0.8 %copy.24 = s32[6,8,256]{2,0,1:T(8,128)S(1)} copy(s32[6,8,256]{2,1,0:T(8,128)} %param.5) | data formatting | bytes 98304 | tf_op args[0]
  0.8 2.6 %collective-permute-start = (s32[6,8,256]{2,0,1:T(8,128)S(1)}, s32[6,8,256]{2,0,1:T(8,128)S(1)}, u32[]{:S(2)}, u32[]{:S(2)}) collective-permute-start(s32[6,8,256]{2,0,1:T(8,128)S(1)} %copy.24), channel_id=1, source_target_pairs={{0,1},{1,0},{2,3},{3,2},{4,5},{5,4},{6,7},{7,6},{8,9},{9,8},{10,11... | collective-permute-start | bytes 147464 | tf_op jit(solution)/shard_map/ppermute | solution.py:561
  3.5 0.9 %select_reduce_fusion = f32[4]{0:T(128)S(1)} fusion(f32[360]{0:T(512)} %param.8, s32[4]{0:T(128)} %param.9), kind=kLoop, calls=%fused_computation.6 | loop fusion | flops 4316 | bytes 1472 | tf_op jit(solution)/shard_map/reduce_sum | solution.py:582
  4.4 0.1 multiply_multiply_fusion.1
  4.5 0.1 multiply_multiply_fusion
  4.5 0.1 fusion.1
  4.6 0.1 slice.30
  4.7 0.1 fusion.3
  4.8 0.7 %multiply_bitcast_fusion = (f32[1,8]{1,0:T(1,128)S(1)}, f32[8]{0:T(128)S(1)}, f32[8]{0:T(128)S(1)}, f32[1,8]{1,0:T(1,128)S(1)}, f32[1,8]{1,0:T(1,128)S(1)}) fusion(f32[8]{0:T(128)} %param.7, f32[8]{0:T(128)} %param.6), kind=kLoop, calls=%fused_computation.17 | loop fusion | flops 120 | bytes 224 | tf_op jit(solution)/shard_map/stack | solution.py:530
  5.5 0.1 copy.26
  5.6 0.0 collective-permute-done
  5.7 4.0 %collective-permute-start.1 = (s32[6,16,256]{2,0,1:T(8,128)S(1)}, s32[6,16,256]{2,0,1:T(8,128)S(1)}, u32[]{:S(2)}, u32[]{:S(2)}) collective-permute-start(s32[6,16,256]{2,0,1:T(8,128)S(1)} %add_select_fusion.1), channel_id=1, source_target_pairs={{16,0},{32,16},{48,32},{64,48},{80,64},{96,80},{112,96},{128,112},... | collective-permute-start | bytes 294920 | tf_op jit(solution)/shard_map/ppermute | solution.py:554
  9.7 5.8 %collective-permute-start.2 = (s32[4,16,256]{2,0,1:T(4,128)S(1)}, s32[4,16,256]{2,0,1:T(4,128)S(1)}, u32[]{:S(2)}, u32[]{:S(2)}) collective-permute-start(s32[4,16,256]{2,0,1:T(4,128)S(1)} %slice_select_fusion), channel_id=1, source_target_pairs={{32,0},{48,16},{64,32},{80,48},{96,64},{112,80},{128,96},{144,112}... | collective-permute-start | bytes 196616 | tf_op jit(solution)/shard_map/ppermute | solution.py:554
  15.5 0.1 copy.27
  15.6 5.7 %collective-permute-done.2 = s32[4,16,256]{2,0,1:T(4,128)S(1)} collective-permute-done((s32[4,16,256]{2,0,1:T(4,128)S(1)}, s32[4,16,256]{2,0,1:T(4,128)S(1)}, u32[]{:S(2)}, u32[]{:S(2)}) %collective-permute-start.2) | collective-permute-done | bytes 65568 | tf_op jit(solution)/shard_map/ppermute | solution.py:554
  21.3 0.0 collective-permute-done.1
  21.3 0.1 fusion.refs_0_
  21.5 2.1 %collective-permute-start.4 = (s32[9,16,256]{2,1,0:T(8,128)S(1)}, s32[9,16,256]{2,1,0:T(8,128)S(1)}, u32[]{:S(2)}, u32[]{:S(2)}) collective-permute-start(s32[9,16,256]{2,1,0:T(8,128)S(1)} %slice.35), channel_id=1, source_target_pairs={{2,0},{3,1},{4,2},{5,3},{6,4},{7,5},{8,6},{9,7},{10,8},{11,9},{12,... | collective-permute-start | bytes 442376 | tf_op jit(solution)/shard_map/ppermute | solution.py:558
  23.6 4.4 %collective-permute-start.3 = (s32[10,16,256]{2,1,0:T(8,128)S(1)}, s32[10,16,256]{2,1,0:T(8,128)S(1)}, u32[]{:S(2)}, u32[]{:S(2)}) collective-permute-start(s32[10,16,256]{2,1,0:T(8,128)S(1)} %slice.34), channel_id=1, source_target_pairs={{0,2},{1,3},{2,4},{3,5},{4,6},{5,7},{6,8},{7,9},{8,10},{9,11},{10,... | collective-permute-start | bytes 491528 | tf_op jit(solution)/shard_map/ppermute | solution.py:558
  28.0 0.1 broadcast_in_dim.4.ex
  28.1 0.1 broadcast_in_dim.5.ey
  28.3 0.6 %shard_map.55.refs_2_.refs_3_ = f32[1120,8,128]{2,1,0:T(8,128)S(1)} custom-call(f32[16,2,8,128]{3,2,1,0:T(8,128)S(1)} %broadcast_in_dim.4.ex, f32[35,2,8,128]{3,2,1,0:T(8,128)S(1)} %broadcast_in_dim.5.ey), custom_call_target="tpu_custom_call" | custom-call | tf_op jit(solution)/shard_map/pallas_call | solution.py:456
  28.9 4.3 %shard_map.56 = (f32[35,16,128]{2,1,0:T(8,128)S(1)}, f32[35,16,128]{2,1,0:T(8,128)S(1)}, f32[35,16,128]{2,1,0:T(8,128)S(1)}, f32[35,16,128]{2,1,0:T(8,128)S(1)},...) custom-call(s32[16,16,256]{2,1,0:T(8,128)S(1)} %fusion.refs_0_, ...), custom_call_target="tpu_custom_call" | custom-call | tf_op jit(solution)/shard_map/pallas_call | solution.py:469
  33.2 0.0 collective-permute-done.4.refs_1_
  33.3 0.0 collective-permute-done.3.refs_0_
  33.3 5.6 %shard_map.57 = (f32[35,16,128]{2,1,0:T(8,128)S(1)}, f32[35,16,128]{2,1,0:T(8,128)S(1)}, f32[35,16,128]{2,1,0:T(8,128)S(1)}, f32[35,16,128]{2,1,0:T(8,128)S(1)},...) custom-call(s32[10,16,256]{2,1,0:T(8,128)S(1)} %collective-permute-d, ...), custom_call_target="tpu_custom_call", output_to_operand_aliasing={{0}: (4, {}), {1}: (5, {}), {2}: (6, {}), {3}: (7, {}), {4}... | custom-call | tf_op jit(solution)/shard_map/pallas_call | solution.py:483
  38.9 5.1 %collective-permute-start.5 = (f32[91,8,128]{2,1,0:T(8,128)S(1)}, f32[91,8,128]{2,1,0:T(8,128)S(1)}, u32[]{:S(2)}, u32[]{:S(2)}) collective-permute-start(f32[91,8,128]{2,1,0:T(8,128)S(1)} %get-tuple-element.40), channel_id=1, source_target_pairs={{0,1},{1,0},{2,3},{3,2},{4,5},{5,4},{6,7},{7,6},{8,9},{9,8},{10,11... | collective-permute-start | bytes 1118216 | tf_op jit(solution)/shard_map/ppermute | solution.py:561
  44.0 1.3 %collective-permute-done.5.recv = f32[91,8,128]{2,1,0:T(8,128)S(1)} collective-permute-done((f32[91,8,128]{2,1,0:T(8,128)S(1)}, f32[91,8,128]{2,1,0:T(8,128)S(1)}, u32[]{:S(2)}, u32[]{:S(2)}) %collective-permute-start.5) | collective-permute-done | bytes 372768 | tf_op jit(solution)/shard_map/ppermute | solution.py:561
  45.3 3.1 %shard_map.58 = f32[384,256]{1,0:T(8,128)} custom-call(f32[5,15,8,128]{3,2,1,0:T(8,128)S(1)} %get-tuple-element.38.c1_own, f32[2,5,16,128]{3,2,1,0:T(8,128)S(1)} %get-tuple-element.39.ck_own, f32[91,8,128]{2,1,0:T(8,128)S(1)} %collective-permute-done.5.recv, f32[48,2,8,128]{3,2,1,0:T(8,128)S(1)} %get-tuple-element.41.it2, f32[4,8,128]{2,1,0:T(8,128)S(1)} %get-tuple-element.42.inv), custom_call_target="tpu_custom_call" | custom-call | tf_op jit(solution)/shard_map/pallas_call | solution.py:505
  (14 shorter events, 0.2 us)
Async XLA Ops:
  0.8 4.8 %collective-permute-start = (s32[6,8,256]{2,0,1:T(8,128)S(1)}, s32[6,8,256]{2,0,1:T(8,128)S(1)}, u32[]{:S(2)}, u32[]{:S(2)}) collective-permute-start(s32[6,8,256]{2,0,1:T(8,128)S(1)} %copy.24), channel_id=1, source_target_pairs={{0,1},{1,0},{2,3},{3,2},{4,5},{5,4},{6,7},{7,6},{8,9},{9,8},{10,11... | collective-permute-start | bytes 147464 | tf_op jit(solution)/shard_map/ppermute | solution.py:561
  5.7 15.7 %collective-permute-start.1 = (s32[6,16,256]{2,0,1:T(8,128)S(1)}, s32[6,16,256]{2,0,1:T(8,128)S(1)}, u32[]{:S(2)}, u32[]{:S(2)}) collective-permute-start(s32[6,16,256]{2,0,1:T(8,128)S(1)} %add_select_fusion.1), channel_id=1, source_target_pairs={{16,0},{32,16},{48,32},{64,48},{80,64},{96,80},{112,96},{128,112},... | collective-permute-start | bytes 294920 | tf_op jit(solution)/shard_map/ppermute | solution.py:554
  9.7 11.7 %collective-permute-start.2 = (s32[4,16,256]{2,0,1:T(4,128)S(1)}, s32[4,16,256]{2,0,1:T(4,128)S(1)}, u32[]{:S(2)}, u32[]{:S(2)}) collective-permute-start(s32[4,16,256]{2,0,1:T(4,128)S(1)} %slice_select_fusion), channel_id=1, source_target_pairs={{32,0},{48,16},{64,32},{80,48},{96,64},{112,80},{128,96},{144,112}... | collective-permute-start | bytes 196616 | tf_op jit(solution)/shard_map/ppermute | solution.py:554
  21.5 11.8 %collective-permute-start.4 = (s32[9,16,256]{2,1,0:T(8,128)S(1)}, s32[9,16,256]{2,1,0:T(8,128)S(1)}, u32[]{:S(2)}, u32[]{:S(2)}) collective-permute-start(s32[9,16,256]{2,1,0:T(8,128)S(1)} %slice.35), channel_id=1, source_target_pairs={{2,0},{3,1},{4,2},{5,3},{6,4},{7,5},{8,6},{9,7},{10,8},{11,9},{12,... | collective-permute-start | bytes 442376 | tf_op jit(solution)/shard_map/ppermute | solution.py:558
  23.6 9.7 %collective-permute-start.3 = (s32[10,16,256]{2,1,0:T(8,128)S(1)}, s32[10,16,256]{2,1,0:T(8,128)S(1)}, u32[]{:S(2)}, u32[]{:S(2)}) collective-permute-start(s32[10,16,256]{2,1,0:T(8,128)S(1)} %slice.34), channel_id=1, source_target_pairs={{0,2},{1,3},{2,4},{3,5},{4,6},{5,7},{6,8},{7,9},{8,10},{9,11},{10,... | collective-permute-start | bytes 491528 | tf_op jit(solution)/shard_map/ppermute | solution.py:558
  38.9 6.4 %collective-permute-start.5 = (f32[91,8,128]{2,1,0:T(8,128)S(1)}, f32[91,8,128]{2,1,0:T(8,128)S(1)}, u32[]{:S(2)}, u32[]{:S(2)}) collective-permute-start(f32[91,8,128]{2,1,0:T(8,128)S(1)} %get-tuple-element.40), channel_id=1, source_target_pairs={{0,1},{1,0},{2,3},{3,2},{4,5},{5,4},{6,7},{7,6},{8,9},{9,8},{10,11... | collective-permute-start | bytes 1118216 | tf_op jit(solution)/shard_map/ppermute | solution.py:561

commit v3 on v2

--- a/solution.py
+++ b/solution.py
@@ -1,11 +1,12 @@
 import jax
 import jax.numpy as jnp
+import numpy as np
 from jax import lax
 from jax.experimental import pallas as pl
 from jax.experimental.pallas import tpu as pltpu
+from jax.experimental.layout import Layout, with_layout_constraint
 from jax.sharding import PartitionSpec as P
 
-NANG = 360
 MAT = 8
 DAMPING = 0.8
 WAVE_SQUARED = 0.1
@@ -22,6 +23,7 @@
 LANES = 128
 F32 = jnp.float32
 OUTSIDE = 8
+WAVENUMBER = float(np.sqrt(np.float32(WAVE_SQUARED)))
 
 
 def lane_iota():
@@ -64,18 +66,69 @@
     return core, x0, y0
 
 
-def wave_kernel(ex, ey, wave):
-    def rows(y, carry):
-        w = ey[y, 0]
-        w_t = ey[y, 1]
+def splat(value):
+    return jnp.full((8, LANES), value, F32)
+
+
+def wave_kernel(
+    real_in, imag_in, angles_in, picks_in, after, wave, tab, real, imag, angles, picks, sems
+):
+    del after
+    copies = [
+        pltpu.make_async_copy(src, dst, sems.at[n])
+        for n, (src, dst) in enumerate(
+            (
+                (real_in, real),
+                (imag_in, imag),
+                (angles_in, angles),
+                (picks_in, picks),
+            )
+        )
+    ]
+    for copy in copies:
+        copy.start()
+    for copy in copies:
+        copy.wait()
+    _, x0, y0 = where_am_i()
+    lanes = lane_iota()
+    rows = lax.broadcasted_iota(jnp.int32, (8, LANES), 0)
+
+    er = jnp.zeros((8, LANES), F32)
+    ei = jnp.zeros((8, LANES), F32)
+    for m in range(MAT):
+        er = jnp.where(lanes == m, splat(real[m]), er)
+        ei = jnp.where(lanes == m, splat(imag[m]), ei)
+    for n, table in enumerate(material_tables(er, ei)):
+        tab[n : n + 1, :] = jnp.where(lanes < MAT, table, 0.0)[0:1]
+
+    incidence = jnp.zeros((8, LANES), F32)
+    for c in range(4):
+        mine = jnp.bitwise_and(rows, 3) == c
+        incidence = jnp.where(mine, splat(angles[picks[c]]), incidence)
+    in_x = lanes < PX
+    place = jnp.where(in_x, x0 + lanes, y0 + (lanes - PX)).astype(F32)
+    slope = jnp.where(in_x, jnp.cos(incidence), jnp.sin(incidence))
+    phases = WAVENUMBER * (slope * place)
+    cosine = jnp.cos(phases)
+    sine = jnp.sin(phases)
+    upper = rows < 4
+    front = jnp.where(upper, cosine, sine)
+    turn = jnp.where(upper, -sine, cosine)
+
+    def along(values, n):
+        return jnp.broadcast_to(values[:, n : n + 1], (8, LANES))
+
+    for x in range(PX):
+        wave[x * 2] = along(cosine, x)
+        wave[x * 2 + 1] = along(sine, x)
+    for y in reversed(range(PY)):
+        w = along(front, PX + y)
+        w_t = along(turn, PX + y)
         for x in range(PX):
-            c = ex[x, 0]
-            s = ex[x, 1]
+            c = wave[x * 2]
+            s = wave[x * 2 + 1]
             wave[(y * PX + x) * 2] = c * w + s * w_t
             wave[(y * PX + x) * 2 + 1] = c * w_t - s * w
-        return carry
-
-    lax.fori_loop(0, PY, rows, 0)
 
 
 def row_loop(first, count, step, body):
@@ -250,8 +303,8 @@
 def middle_kernel(sizes, labels, tab, wave, *refs):
     region = Region(sizes, tab, wave, refs[:12], refs[12:])
     region.tables(labels, LOW, 2 * OWN_Y, 8)
-    row_loop(LOW, 2 * OWN_Y, 2, region.first_stage)
-    row_loop(LOW + 1, 2 * OWN_Y - 2, 2, region.second_stage)
+    row_loop(LOW, 2 * OWN_Y, 4, region.first_stage)
+    row_loop(LOW + 1, 2 * OWN_Y - 2, 7, region.second_stage)
 
 
 def outer_kernel(sizes, low, high, tab, wave, *refs):
@@ -261,8 +314,8 @@
     it1 = region.it1
     top = LOW + 2 * OWN_Y
     region.tables(low, 0, LOW, LOW)
-    row_loop(0, LOW, 2, region.first_stage)
-    row_loop(1, LOW, 2, region.second_stage)
+    row_loop(0, LOW, 5, region.first_stage)
+    row_loop(1, LOW, 5, region.second_stage)
     region.tables(high, top, PY - top, PY - top)
     row_loop(top, PY - top, 3, region.first_stage)
     row_loop(top - 1, PY - top, 3, region.second_stage)
@@ -323,31 +376,28 @@
 SEND = CX * NJ + 4 * CX + 2 * OWN_Y
 
 
-def cycle_kernel(c1_own, ck_own, recv, it2, inv, out, c1, ckr, cki, cc, pp, qq, vv, o0, o1):
+def cycle_kernel(c1_own, ck_own, recv, it2, inv, out, c1, ck, cc, pp, qq, parts, o0, o1):
     core = where_am_i()[0]
     lanes = lane_iota()
     first = lanes == 0
     last = lanes == LANES - 1
     sgn = sign_rows()
+    j0 = 4 * core
 
     def spread(row):
         return jnp.broadcast_to(row, (8, LANES))
 
     def assemble(which):
-        own_i, other_i, j0 = CX - which * CX, which * CX, 4 * which
+        own_i, other_i = CX - which * CX, which * CX
         for i in range(CX):
             for j in range(NJ):
-                at = (own_i + i) * NJ + j
-                row = j0 + j
-                c1[at] = c1_own[i, row]
-                ckr[at] = spread(ck_own[0, i, row : row + 1, :])
-                cki[at] = spread(ck_own[1, i, row : row + 1, :]) * sgn
-                at = (other_i + i) * NJ + j
-                c1[at] = recv[i * NJ + j]
-                for k, ref in ((0, ckr), (1, cki)):
-                    tile = CX * NJ + (k * CX + i) * 2 + row // 8
-                    value = spread(recv[tile, row % 8 : row % 8 + 1, :])
-                    ref[at] = value * sgn if k else value
+                c1[(own_i + i) * NJ + j] = c1_own[i, 4 * which + j]
+                c1[(other_i + i) * NJ + j] = recv[i * NJ + j]
+            for k in range(2):
+                for h in range(2):
+                    tile = slice(8 * h, 8 * h + 8)
+                    ck[k, own_i + i, tile, :] = ck_own[k, i, tile, :]
+                    ck[k, other_i + i, tile, :] = recv[CX * NJ + (k * CX + i) * 2 + h]
 
     @pl.when(core == 0)
     def _():
@@ -357,7 +407,7 @@
     def _():
         assemble(1)
 
-    for sweep in range(3):
+    for sweep, (sum_step, relax_step) in enumerate(((5, 4), (4, 3), (3, 4))):
         ref = c1 if sweep == 0 else cc
 
         def sums(i, ref=ref, sweep=sweep):
@@ -371,22 +421,45 @@
                 pp[i * NJ + j] = centres[j] + (faces[j - 1] + faces[j + 1])
                 qq[i * NJ + j] = faces[j] + (edges[j - 1] + edges[j + 1])
 
-        row_loop(sweep, NI - 2 * sweep, 2, sums)
+        row_loop(sweep, NI - 2 * sweep, sum_step, sums)
 
         def relax(i, ref=ref, sweep=sweep):
             for j in range(sweep + 1, NJ - sweep - 1):
                 at = i * NJ + j
                 n = (pp[at] + (qq[at - NJ] + qq[at + NJ])) * (14.0 / 120.0)
-                cc[at] = (0.2 * ref[at] + c1[at]) + (ckr[at] * n + cki[at] * turned(n))
-
-        row_loop(sweep + 1, NI - 2 * sweep - 2, 2, relax)
-
-    def put(x, y, value):
+                kr = spread(ck[0, i, pl.ds(j0 + j, 1), :])
+                ki = spread(ck[1, i, pl.ds(j0 + j, 1), :])
+                cc[at] = (0.2 * ref[at] + c1[at]) + (kr * n + ki * (sgn * turned(n)))
+
+        row_loop(sweep + 1, NI - 2 * sweep - 2, relax_step, relax)
+
+    flags = {0: jnp.where(core == 0, 1.0, 0.0), OWN_X - 1: jnp.where(core == 1, 1.0, 0.0)}
+    added = []
+    for k in range(OWN_Y):
+        pair = []
+        for h in range(2):
+            n = recv[CX * NJ + 4 * CX + 2 * k + h]
+            ir = spread(inv[h, k : k + 1, :])
+            ii = spread(inv[2 + h, k : k + 1, :])
+            pair.append(ir * n + ii * (sgn * turned(n)))
+        added.append(pair)
+
+    rows = lax.broadcasted_iota(jnp.int32, (2 * LANES, 2 * LANES), 0)
+    cols = lax.broadcasted_iota(jnp.int32, (2 * LANES, 2 * LANES), 1)
+    target = jnp.where(rows < LANES, 2 * rows, 2 * (rows - LANES) + 1)
+    perm = jnp.where(cols == target, 1.0, 0.0).astype(jnp.bfloat16)
+    count = OWN_X * OWN_Y
+
+    def fine(x, y, value):
         col = x * OWN_Y + y
-        even = 0.5 * (value + up(value, first))
-        vv[col * 8 : col * 8 + 8, :LANES] = it2[col, 0] + even
-        vv[col * 8 : col * 8 + 8, LANES:] = it2[col, 1] + value
-
+        even = it2[col, 0] + 0.5 * (value + up(value, first))
+        odd = it2[col, 1] + value
+        if x in flags:
+            even = even + flags[x] * added[y][0]
+            odd = odd + flags[x] * added[y][1]
+        return even, odd
+
+    size = 2 * OWN_Y * 8
     for i in range(OWN_X // 2):
         for j in range(OWN_Y // 2):
             at = (i + 4) * NJ + j + 4
@@ -395,39 +468,29 @@
             mix = 0.5 * (left + here)
             below = cc[at - 1]
             mix_below = 0.5 * (cc[at - NJ - 1] + below)
-            put(2 * i + 1, 2 * j + 1, here)
-            put(2 * i, 2 * j + 1, mix)
-            put(2 * i + 1, 2 * j, 0.5 * (below + here))
-            put(2 * i, 2 * j, 0.5 * (mix_below + mix))
-
-    for k in range(OWN_Y):
-        at = pl.multiple_of((core * (OWN_X - 1) * OWN_Y + k) * 8, 8)
-        for h in range(2):
-            n = recv[CX * NJ + 4 * CX + 2 * k + h]
-            ir = spread(inv[h, k : k + 1, :])
-            ii = spread(inv[2 + h, k : k + 1, :])
-            where = (pl.ds(at, 8), slice(h * LANES, (h + 1) * LANES))
-            vv[where] = vv[where] + (ir * n + (ii * sgn) * turned(n))
-
-    rows = lax.broadcasted_iota(jnp.int32, (2 * LANES, 2 * LANES), 0)
-    cols = lax.broadcasted_iota(jnp.int32, (2 * LANES, 2 * LANES), 1)
-    target = jnp.where(rows < LANES, 2 * rows, 2 * (rows - LANES) + 1)
-    perm = jnp.where(cols == target, 1.0, 0.0).astype(jnp.bfloat16)
-    count = OWN_X * OWN_Y
-    for x in range(OWN_X):
-        value = vv[x * 64 : x * 64 + 64, :]
-        top = value.astype(jnp.bfloat16)
-        rest = value - top.astype(F32)
-        middle = rest.astype(jnp.bfloat16)
-        bottom = (rest - middle.astype(F32)).astype(jnp.bfloat16)
-        mixed = (
-            jnp.dot(bottom, perm, preferred_element_type=F32)
-            + jnp.dot(middle, perm, preferred_element_type=F32)
-        ) + jnp.dot(top, perm, preferred_element_type=F32)
-        for y in range(OWN_Y):
-            block = mixed[y * 8 : y * 8 + 8]
-            o0[pl.ds(x * OWN_Y + y, 8, stride=count), :] = block[:, :LANES]
-            o1[pl.ds(x * OWN_Y + y, 8, stride=count), :] = block[:, LANES:]
+            for x in range(2):
+                lower, upper = (
+                    (0.5 * (mix_below + mix), mix),
+                    (0.5 * (below + here), here),
+                )[x]
+                a = fine(2 * i + x, 2 * j, lower)
+                b = fine(2 * i + x, 2 * j + 1, upper)
+                for h in range(2):
+                    value = jnp.concatenate([a[h], b[h]], axis=0)
+                    top = value.astype(jnp.bfloat16)
+                    rest = (value - top.astype(F32)).astype(jnp.bfloat16)
+                    start = i * 2 * size + (x * OWN_Y + 2 * j) * 8
+                    half = slice(h * LANES, h * LANES + LANES)
+                    parts[start : start + 16, half] = top
+                    parts[start + size : start + size + 16, half] = rest
+        mixed = jnp.dot(
+            parts[i * 2 * size : (i + 1) * 2 * size, :], perm, preferred_element_type=F32
+        )
+        for n in range(2 * OWN_Y):
+            block = mixed[n * 8 : n * 8 + 8] + mixed[size + n * 8 : size + n * 8 + 8]
+            col = i * 2 * OWN_Y + n
+            o0[pl.ds(col, 8, stride=count), :] = block[:, :LANES]
+            o1[pl.ds(col, 8, stride=count), :] = block[:, LANES:]
     out[:, :LANES] = o0[...]
     out[:, LANES:] = o1[...]
 
@@ -452,14 +515,22 @@
     return [pltpu.with_memory_space_constraint(a, pltpu.VMEM) for a in arrays]
 
 
-def wave_call(ex, ey):
+def wave_call(real, imag, angles, picks, after):
+    small = pl.BlockSpec(memory_space=pltpu.HBM)
     return pl.pallas_call(
         wave_kernel,
-        out_shape=vmem(CELLS * 2, 8, LANES),
-        in_specs=[SPEC] * 2,
-        out_specs=SPEC,
-        compiler_params=limit(2),
-    )(*near_core(ex, ey))
+        out_shape=(vmem(CELLS * 2, 8, LANES), vmem(8, LANES)),
+        in_specs=[small] * 4 + [SPEC],
+        out_specs=(SPEC,) * 2,
+        scratch_shapes=[
+            pltpu.SMEM(a.shape, a.dtype) for a in (real, imag, angles, picks)
+        ]
+        + [pltpu.SemaphoreType.DMA((4,))],
+        compiler_params=limit(6),
+    )(
+        *(pltpu.with_memory_space_constraint(a, pltpu.HBM) for a in (real, imag, angles, picks)),
+        *near_core(after),
+    )
 
 
 def middle_call(sizes, labels, tab, wave):
@@ -507,8 +578,9 @@
         out_shape=jax.ShapeDtypeStruct((rows, 2 * LANES), F32),
         in_specs=[SPEC] * 5,
         out_specs=SPEC,
-        scratch_shapes=[vmem(points, 8, LANES)] * 6
-        + [vmem(rows, 2 * LANES)]
+        scratch_shapes=[vmem(points, 8, LANES), vmem(2, NI, 16, LANES)]
+        + [vmem(points, 8, LANES)] * 3
+        + [pltpu.VMEM((2 * rows, 2 * LANES), jnp.bfloat16)]
         + [vmem(rows, LANES)] * 2,
         compiler_params=limit(8),
     )(*near_core(*args))
@@ -527,21 +599,16 @@
     src_i = SOURCE_GAIN * ei
     ci_r, ci_i = complex_inverse(128.0 / 120.0 - med_r, -med_i)
     scale = 14.0 * DAMPING / 30.0
-    rows = jnp.stack(
-        [scale * inv_r, scale * inv_i, 1.2 * src_r, 1.2 * src_i,
-         DAMPING * ci_r, DAMPING * ci_i]
+    return (
+        scale * inv_r, scale * inv_i, 1.2 * src_r, 1.2 * src_i,
+        DAMPING * ci_r, DAMPING * ci_i,
     )
-    return jnp.pad(rows, ((0, 2), (0, LANES - MAT)))
-
-
-def local(labels, permittivity_real, permittivity_imag, angles, angle_pick):
+
+
+def body(labels, permittivity_real, permittivity_imag, angles, angle_pick):
     gx_n = lax.axis_size("gx")
     gy_n = lax.axis_size("gy")
-    gx = lax.axis_index("gx")
-    gy = lax.axis_index("gy")
-    core = gy % 2
-    x0 = OWN_X * gx - LOW * core
-    y0 = 2 * OWN_Y * (gy // 2) - LOW
+    core = lax.axis_index("gy") % 2
     is_low = core == 0
 
     def along_x(values, by):
@@ -566,6 +633,7 @@
         jnp.concatenate([labels, other], axis=1),
         jnp.concatenate([other, labels], axis=1),
     )
+    both = with_layout_constraint(both, Layout((0, 1, 2)))
     far = along_x(jnp.where(is_low, both[:4], both[2:]), 2)
     near = along_x(both, 1)
     region = jnp.where(
@@ -577,26 +645,9 @@
     low = along_y(region[2 * OWN_Y - LOW :], 2)
     high = along_y(region[: PY - LOW - 2 * OWN_Y], -2)
 
-    table = material_tables(permittivity_real, permittivity_imag)
-    pick = (angle_pick[:, None] == jnp.arange(NANG, dtype=jnp.int32)[None, :]).astype(F32)
-    incidence = jnp.sum(pick * angles[None, :], axis=1)
-    wavenumber = jnp.sqrt(WAVE_SQUARED)
-    pos_x = (x0 + jnp.arange(PX, dtype=jnp.int32)).astype(F32)
-    pos_y = (y0 + jnp.arange(PY, dtype=jnp.int32)).astype(F32)
-    phase_x = wavenumber * (jnp.cos(incidence)[None, :] * pos_x[:, None])
-    phase_y = wavenumber * (jnp.sin(incidence)[None, :] * pos_y[:, None])
-    phases = jnp.concatenate([phase_x, phase_y], axis=0)
-    cosine, sine = lax.optimization_barrier((jnp.cos(phases), jnp.sin(phases)))
-    cx, sx, cy, sny = cosine[:PX], sine[:PX], cosine[PX:], sine[PX:]
-    ex = jnp.stack(
-        [jnp.concatenate([cx, cx], axis=1), jnp.concatenate([sx, sx], axis=1)], axis=1
+    wave, table = wave_call(
+        permittivity_real, permittivity_imag, angles, angle_pick, both
     )
-    ey = jnp.stack(
-        [jnp.concatenate([cy, sny], axis=1), jnp.concatenate([-sny, cy], axis=1)], axis=1
-    )
-    ex = jnp.broadcast_to(ex[..., None], (PX, 2, 8, LANES))
-    ey = jnp.broadcast_to(ey[..., None], (PY, 2, 8, LANES))
-    wave = wave_call(ex, ey)
     sizes = (OWN_X * gx_n, OWN_Y * gy_n)
     shared = middle_call(sizes, region, table, wave)
     c1, ck, send, it2, inv = outer_call(sizes, low, high, table, wave, shared)
@@ -607,7 +658,7 @@
 
 def solution(mesh):
     return jax.shard_map(
-        local,
+        body,
         mesh=mesh,
         in_specs=(P("gx", "gy", None), P(), P(), P(), P()),
         out_specs=P(None, None, "gx", "gy", None),

time: 48.7 us -> 47.6 us (0.977)
  local copies, waits for them, and re-layouts: 1.38 us -> 0.09 us
  waiting for transfers between devices: 7.06 us -> 8.22 us
  other arithmetic: 2.07 us -> 1 us
  starting transfers between devices: 24 us -> 24.6 us
    ppermute x2, waiting for transfers between devices: 1.3 us -> 2.36 us  [core_swap(): return lax.ppermute(values, 'gy', [(j, j ^ 1) for j in range(gy_n)])]
    pallas_call x1, Pallas kernels: 0.6 us -> 1.59 us  [wave_call(): pl.pallas_call(wave_kernel, out_shape=(vmem(CELLS * 2, 8, LANES), vmem(8,...]
    select_n x2, other arithmetic: 0.03 us -> 0.91 us  [the longest x1 0.88 us: body(): jnp.where(is_low, jnp.concatenate([labels, other], axis=1), jnp.concatena...]
    reduce_sum x1 -> x0, other arithmetic: 0.87 us -> none  [local(): incidence = jnp.sum(pick * angles[None, :], axis=1)]
    ppermute x2, starting transfers between devices: 7.65 us -> 8.47 us  [core_swap(): return lax.ppermute(values, 'gy', [(j, j ^ 1) for j in range(gy_n)])]
    unnamed x1 -> x0, local copies, waits for them, and re-layouts: 0.82 us -> none
    another operation x6 -> x0, other arithmetic: 0.73 us -> none  [the longest x2 0.7 us: material_tables(): jnp.stack([scale * inv_r, scale * inv_i, 1.2 * src_r, 1.2 * src_i, DAMPIN...]
    pallas_call x1, Pallas kernels: 3.14 us -> 2.44 us  [cycle_call(): pl.pallas_call(cycle_kernel, out_shape=jax.ShapeDtypeStruct((rows, 2 * LA...]
  transfers between devices with their start and end apart: 6 -> 6, of which waited for: 2 -> 3; matrix products, arithmetic and copies ran while one was open for 5% -> 0% of each run, Pallas kernels for 10% -> 12%
where the time goes in v3:
time: 47.6 us; the launch traced here: 47.3 us
  starting transfers between devices  24.6 us (52%)
  Pallas kernels  13.3 us (28%)
  waiting for transfers between devices  8.22 us (17%)
  other arithmetic  1 us (2%)
    ppermute x2, starting transfers between devices, along_x(): return lax.ppermute(values, ('gx', 'gy'), pairs)  9.81 us
    ppermute x2, starting transfers between devices, core_swap(): return lax.ppermute(values, 'gy', [(j, j ^ 1) for j in range(gy_n)])  8.47 us
    ppermute x2, starting transfers between devices, along_y(): return lax.ppermute(values, 'gy', pairs)  6.34 us
    ppermute x2, waiting for transfers between devices, along_x(): return lax.ppermute(values, ('gx', 'gy'), pairs)  5.86 us
    pallas_call x1, Pallas kernels, outer_call(): pl.pallas_call(kernel, out_shape=SHARED + (vmem(CX, CY, 8, LANES), vmem(2...  5.31 us
    pallas_call x1, Pallas kernels, middle_call(): pl.pallas_call(kernel, out_shape=SHARED, in_specs=[SPEC] * 3, out_specs=(...  3.91 us
    pallas_call x1, Pallas kernels, cycle_call(): pl.pallas_call(cycle_kernel, out_shape=jax.ShapeDtypeStruct((rows, 2 * LA...  2.44 us
    ppermute x2, waiting for transfers between devices, core_swap(): return lax.ppermute(values, 'gy', [(j, j ^ 1) for j in range(gy_n)])  2.36 us
  transfers between devices with their start and end apart: 6, of which 3 were waited for; matrix products, arithmetic and copies ran while one was open for 0% of the time, Pallas kernels for 12%

profile of v3, /device:TPU:31, one launch (start us, length us, event | category | flops | bytes accessed | tf_op | source)
XLA Modules:
  0.0 47.3 jit_solution(14937537309242479754)
XLA Ops:
  0.0 2.6 %collective-permute-start = (s32[6,8,256]{2,1,0:T(8,128)}, s32[6,8,256]{2,1,0:T(8,128)S(1)}, u32[]{:S(2)}, u32[]{:S(2)}) collective-permute-start(s32[6,8,256]{2,1,0:T(8,128)} %param.5), channel_id=1, source_target_pairs={{0,1},{1,0},{2,3},{3,2},{4,5},{5,4},{6,7},{7,6},{8,9},{9,8},{10,11... | collective-permute-start | bytes 147464 | tf_op jit(solution)/shard_map/ppermute | solution.py:628
  2.6 1.1 %collective-permute-done = s32[6,8,256]{2,1,0:T(8,128)S(1)} collective-permute-done((s32[6,8,256]{2,1,0:T(8,128)}, s32[6,8,256]{2,1,0:T(8,128)S(1)}, u32[]{:S(2)}, u32[]{:S(2)}) %collective-permute-start) | collective-permute-done | bytes 49184 | tf_op jit(solution)/shard_map/ppermute | solution.py:628
  3.6 0.9 %add_select_fusion.1.after = s32[6,16,256]{2,1,0:T(8,128)S(1)} fusion(s32[6,8,256]{2,1,0:T(8,128)S(1)} %collective-permute-done, s32[6,8,256]{2,1,0:T(8,128)} %param.5, pred[]{:T(512)S(6)} %eq.5), kind=kLoop, calls=%fused_computation.2 | loop fusion | flops 73728 | bytes 196609 | tf_op jit(solution)/shard_map/jit(_where)/select_n | solution.py:631
  4.5 0.1 copy.21
  4.6 4.0 %collective-permute-start.1 = (s32[6,16,256]{2,0,1:T(8,128)S(1)}, s32[6,16,256]{2,0,1:T(8,128)S(1)}, u32[]{:S(2)}, u32[]{:S(2)}) collective-permute-start(s32[6,16,256]{2,0,1:T(8,128)S(1)} %copy.21), channel_id=1, source_target_pairs={{16,0},{32,16},{48,32},{64,48},{80,64},{96,80},{112,96},{128,112},... | collective-permute-start | bytes 294920 | tf_op jit(solution)/shard_map/ppermute | solution.py:621
  8.6 5.8 %collective-permute-start.2 = (s32[4,16,256]{2,0,1:T(4,128)S(1)}, s32[4,16,256]{2,0,1:T(4,128)S(1)}, u32[]{:S(2)}, u32[]{:S(2)}) collective-permute-start(s32[4,16,256]{2,0,1:T(4,128)S(1)} %slice_select_fusion), channel_id=1, source_target_pairs={{32,0},{48,16},{64,32},{80,48},{96,64},{112,80},{128,96},{144,112}... | collective-permute-start | bytes 196616 | tf_op jit(solution)/shard_map/ppermute | solution.py:621
  14.5 5.9 %collective-permute-done.2 = s32[4,16,256]{2,0,1:T(4,128)S(1)} collective-permute-done((s32[4,16,256]{2,0,1:T(4,128)S(1)}, s32[4,16,256]{2,0,1:T(4,128)S(1)}, u32[]{:S(2)}, u32[]{:S(2)}) %collective-permute-start.2) | collective-permute-done | bytes 65568 | tf_op jit(solution)/shard_map/ppermute | solution.py:621
  20.3 0.0 collective-permute-done.1
  20.3 0.1 fusion.refs_0_
  20.4 4.4 %collective-permute-start.3 = (s32[10,16,256]{2,1,0:T(8,128)S(1)}, s32[10,16,256]{2,1,0:T(8,128)S(1)}, u32[]{:S(2)}, u32[]{:S(2)}) collective-permute-start(s32[10,16,256]{2,1,0:T(8,128)S(1)} %slice.18), channel_id=1, source_target_pairs={{0,2},{1,3},{2,4},{3,5},{4,6},{5,7},{6,8},{7,9},{8,10},{9,11},{10,... | collective-permute-start | bytes 491528 | tf_op jit(solution)/shard_map/ppermute | solution.py:625
  24.9 1.9 %collective-permute-start.4 = (s32[9,16,256]{2,1,0:T(8,128)S(1)}, s32[9,16,256]{2,1,0:T(8,128)S(1)}, u32[]{:S(2)}, u32[]{:S(2)}) collective-permute-start(s32[9,16,256]{2,1,0:T(8,128)S(1)} %slice.19), channel_id=1, source_target_pairs={{2,0},{3,1},{4,2},{5,3},{6,4},{7,5},{8,6},{9,7},{10,8},{11,9},{12,... | collective-permute-start | bytes 442376 | tf_op jit(solution)/shard_map/ppermute | solution.py:625
  26.8 1.6 %shard_map.55 = (f32[1120,8,128]{2,1,0:T(8,128)S(1)}, f32[8,128]{1,0:T(8,128)S(1)}) custom-call(f32[8]{0:T(128)} %real_in.1, f32[8]{0:T(128)} %imag_in.1, f32[360]{0:T(512)} %angles_in.1, s32[4]{0:T(128)} %picks_in.1, s32[6,16,256]{2,1,0:T(8,128)S(1)} %add_select_fusion.1.after), custom_call_target="tpu_custom_call" | custom-call | tf_op jit(solution)/shard_map/pallas_call | solution.py:520
  28.4 3.9 %shard_map.56 = (f32[35,16,128]{2,1,0:T(8,128)S(1)}, f32[35,16,128]{2,1,0:T(8,128)S(1)}, f32[35,16,128]{2,1,0:T(8,128)S(1)}, f32[35,16,128]{2,1,0:T(8,128)S(1)},...) custom-call(s32[16,16,256]{2,1,0:T(8,128)S(1)} %fusion.refs_0_, ...), custom_call_target="tpu_custom_call" | custom-call | tf_op jit(solution)/shard_map/pallas_call | solution.py:540
  32.3 0.0 collective-permute-done.4.refs_1_
  32.3 0.0 collective-permute-done.3.refs_0_
  32.3 5.3 %shard_map.57 = (f32[35,16,128]{2,1,0:T(8,128)S(1)}, f32[35,16,128]{2,1,0:T(8,128)S(1)}, f32[35,16,128]{2,1,0:T(8,128)S(1)}, f32[35,16,128]{2,1,0:T(8,128)S(1)},...) custom-call(s32[10,16,256]{2,1,0:T(8,128)S(1)} %collective-permute-d, ...), custom_call_target="tpu_custom_call", output_to_operand_aliasing={{0}: (4, {}), {1}: (5, {}), {2}: (6, {}), {3}: (7, {}), {4}... | custom-call | tf_op jit(solution)/shard_map/pallas_call | solution.py:554
  37.7 5.9 %collective-permute-start.5 = (f32[91,8,128]{2,1,0:T(8,128)S(1)}, f32[91,8,128]{2,1,0:T(8,128)S(1)}, u32[]{:S(2)}, u32[]{:S(2)}) collective-permute-start(f32[91,8,128]{2,1,0:T(8,128)S(1)} %get-tuple-element.40), channel_id=1, source_target_pairs={{0,1},{1,0},{2,3},{3,2},{4,5},{5,4},{6,7},{7,6},{8,9},{9,8},{10,11... | collective-permute-start | bytes 1118216 | tf_op jit(solution)/shard_map/ppermute | solution.py:628
  43.6 1.3 %collective-permute-done.5.recv = f32[91,8,128]{2,1,0:T(8,128)S(1)} collective-permute-done((f32[91,8,128]{2,1,0:T(8,128)S(1)}, f32[91,8,128]{2,1,0:T(8,128)S(1)}, u32[]{:S(2)}, u32[]{:S(2)}) %collective-permute-start.5) | collective-permute-done | bytes 372768 | tf_op jit(solution)/shard_map/ppermute | solution.py:628
  44.9 2.4 %shard_map.58 = f32[384,256]{1,0:T(8,128)} custom-call(f32[5,15,8,128]{3,2,1,0:T(8,128)S(1)} %get-tuple-element.38.c1_own, f32[2,5,16,128]{3,2,1,0:T(8,128)S(1)} %get-tuple-element.39.ck_own, f32[91,8,128]{2,1,0:T(8,128)S(1)} %collective-permute-done.5.recv, f32[48,2,8,128]{3,2,1,0:T(8,128)S(1)} %get-tuple-element.41.it2, f32[4,8,128]{2,1,0:T(8,128)S(1)} %get-tuple-element.42.inv), custom_call_target="tpu_custom_call" | custom-call | tf_op jit(solution)/shard_map/pallas_call | solution.py:576
  (3 shorter events, 0.0 us)
Async XLA Ops:
  0.0 3.6 %collective-permute-start = (s32[6,8,256]{2,1,0:T(8,128)}, s32[6,8,256]{2,1,0:T(8,128)S(1)}, u32[]{:S(2)}, u32[]{:S(2)}) collective-permute-start(s32[6,8,256]{2,1,0:T(8,128)} %param.5), channel_id=1, source_target_pairs={{0,1},{1,0},{2,3},{3,2},{4,5},{5,4},{6,7},{7,6},{8,9},{9,8},{10,11... | collective-permute-start | bytes 147464 | tf_op jit(solution)/shard_map/ppermute | solution.py:628
  4.6 15.7 %collective-permute-start.1 = (s32[6,16,256]{2,0,1:T(8,128)S(1)}, s32[6,16,256]{2,0,1:T(8,128)S(1)}, u32[]{:S(2)}, u32[]{:S(2)}) collective-permute-start(s32[6,16,256]{2,0,1:T(8,128)S(1)} %copy.21), channel_id=1, source_target_pairs={{16,0},{32,16},{48,32},{64,48},{80,64},{96,80},{112,96},{128,112},... | collective-permute-start | bytes 294920 | tf_op jit(solution)/shard_map/ppermute | solution.py:621
  8.6 11.7 %collective-permute-start.2 = (s32[4,16,256]{2,0,1:T(4,128)S(1)}, s32[4,16,256]{2,0,1:T(4,128)S(1)}, u32[]{:S(2)}, u32[]{:S(2)}) collective-permute-start(s32[4,16,256]{2,0,1:T(4,128)S(1)} %slice_select_fusion), channel_id=1, source_target_pairs={{32,0},{48,16},{64,32},{80,48},{96,64},{112,80},{128,96},{144,112}... | collective-permute-start | bytes 196616 | tf_op jit(solution)/shard_map/ppermute | solution.py:621
  20.4 11.9 %collective-permute-start.3 = (s32[10,16,256]{2,1,0:T(8,128)S(1)}, s32[10,16,256]{2,1,0:T(8,128)S(1)}, u32[]{:S(2)}, u32[]{:S(2)}) collective-permute-start(s32[10,16,256]{2,1,0:T(8,128)S(1)} %slice.18), channel_id=1, source_target_pairs={{0,2},{1,3},{2,4},{3,5},{4,6},{5,7},{6,8},{7,9},{8,10},{9,11},{10,... | collective-permute-start | bytes 491528 | tf_op jit(solution)/shard_map/ppermute | solution.py:625
  24.9 7.4 %collective-permute-start.4 = (s32[9,16,256]{2,1,0:T(8,128)S(1)}, s32[9,16,256]{2,1,0:T(8,128)S(1)}, u32[]{:S(2)}, u32[]{:S(2)}) collective-permute-start(s32[9,16,256]{2,1,0:T(8,128)S(1)} %slice.19), channel_id=1, source_target_pairs={{2,0},{3,1},{4,2},{5,3},{6,4},{7,5},{8,6},{9,7},{10,8},{11,9},{12,... | collective-permute-start | bytes 442376 | tf_op jit(solution)/shard_map/ppermute | solution.py:625
  37.7 7.2 %collective-permute-start.5 = (f32[91,8,128]{2,1,0:T(8,128)S(1)}, f32[91,8,128]{2,1,0:T(8,128)S(1)}, u32[]{:S(2)}, u32[]{:S(2)}) collective-permute-start(f32[91,8,128]{2,1,0:T(8,128)S(1)} %get-tuple-element.40), channel_id=1, source_target_pairs={{0,1},{1,0},{2,3},{3,2},{4,5},{5,4},{6,7},{7,6},{8,9},{9,8},{10,11... | collective-permute-start | bytes 1118216 | tf_op jit(solution)/shard_map/ppermute | solution.py:628

commit v4 on v3

--- a/solution.py
+++ b/solution.py
@@ -64,6 +64,12 @@
     x0 = OWN_X * gx - LOW * core
     y0 = OWN_Y * (gy - core) - LOW
     return core, x0, y0
+
+
+def stay_kernel(labels, held, sem):
+    copy = pltpu.make_async_copy(labels, held, sem)
+    copy.start()
+    copy.wait()
 
 
 def splat(value):
@@ -307,16 +313,20 @@
     row_loop(LOW + 1, 2 * OWN_Y - 2, 7, region.second_stage)
 
 
-def outer_kernel(sizes, low, high, tab, wave, *refs):
+def low_kernel(sizes, labels, tab, wave, *refs):
+    region = Region(sizes, tab, wave, refs[12:24], refs[24:])
+    region.tables(labels, 0, LOW, LOW)
+    row_loop(0, LOW, 5, region.first_stage)
+    row_loop(1, LOW, 5, region.second_stage)
+
+
+def high_kernel(sizes, labels, tab, wave, *refs):
     region = Region(sizes, tab, wave, refs[12:24], refs[29:])
     c1_out, ck_out, send_out, it2_out, inv_out = refs[24:29]
     core, y0, ny = region.core, region.y0, region.ny
     it1 = region.it1
     top = LOW + 2 * OWN_Y
-    region.tables(low, 0, LOW, LOW)
-    row_loop(0, LOW, 5, region.first_stage)
-    row_loop(1, LOW, 5, region.second_stage)
-    region.tables(high, top, PY - top, PY - top)
+    region.tables(labels, top, PY - top, PY - top)
     row_loop(top, PY - top, 3, region.first_stage)
     row_loop(top - 1, PY - top, 3, region.second_stage)
 
@@ -515,6 +525,17 @@
     return [pltpu.with_memory_space_constraint(a, pltpu.VMEM) for a in arrays]
 
 
+def stay_call(labels):
+    return pl.pallas_call(
+        stay_kernel,
+        out_shape=pltpu.VMEM(labels.shape, labels.dtype),
+        in_specs=[pl.BlockSpec(memory_space=pltpu.HBM)],
+        out_specs=SPEC,
+        scratch_shapes=[pltpu.SemaphoreType.DMA(())],
+        compiler_params=limit(1),
+    )(pltpu.with_memory_space_constraint(labels, pltpu.HBM))
+
+
 def wave_call(real, imag, angles, picks, after):
     small = pl.BlockSpec(memory_space=pltpu.HBM)
     return pl.pallas_call(
@@ -547,9 +568,24 @@
     )(*near_core(labels, tab, wave))
 
 
-def outer_call(sizes, low, high, tab, wave, shared):
+def low_call(sizes, labels, tab, wave, shared):
     def kernel(*refs):
-        outer_kernel(sizes, *refs)
+        low_kernel(sizes, *refs)
+
+    return pl.pallas_call(
+        kernel,
+        out_shape=SHARED,
+        in_specs=[SPEC] * 15,
+        out_specs=(SPEC,) * 12,
+        input_output_aliases={3 + n: n for n in range(12)},
+        scratch_shapes=TABLES + [vmem(LOW * PX, 2 * LANES)],
+        compiler_params=limit(6),
+    )(*near_core(labels, tab, wave), *shared)
+
+
+def high_call(sizes, labels, tab, wave, shared):
+    def kernel(*refs):
+        high_kernel(sizes, *refs)
 
     results = pl.pallas_call(
         kernel,
@@ -561,12 +597,12 @@
             vmem(OWN_X * OWN_Y, 2, 8, LANES),
             vmem(4, 8, LANES),
         ),
-        in_specs=[SPEC] * 16,
+        in_specs=[SPEC] * 15,
         out_specs=(SPEC,) * 17,
-        input_output_aliases={4 + n: n for n in range(12)},
+        input_output_aliases={3 + n: n for n in range(12)},
         scratch_shapes=TABLES + [vmem(LOW * PX, 2 * LANES)],
         compiler_params=limit(6),
-    )(*near_core(low, high, tab, wave), *shared)
+    )(*near_core(labels, tab, wave), *shared)
     return results[12:]
 
 
@@ -628,6 +664,7 @@
         return lax.ppermute(values, "gy", [(j, j ^ 1) for j in range(gy_n)])
 
     other = core_swap(labels)
+    labels = stay_call(labels)
     both = jnp.where(
         is_low,
         jnp.concatenate([labels, other], axis=1),
@@ -636,6 +673,8 @@
     both = with_layout_constraint(both, Layout((0, 1, 2)))
     far = along_x(jnp.where(is_low, both[:4], both[2:]), 2)
     near = along_x(both, 1)
+    near = with_layout_constraint(near, Layout((0, 1, 2)))
+    far = with_layout_constraint(far, Layout((0, 1, 2)))
     region = jnp.where(
         is_low,
         jnp.concatenate([both, near, far], axis=0),
@@ -650,7 +689,8 @@
     )
     sizes = (OWN_X * gx_n, OWN_Y * gy_n)
     shared = middle_call(sizes, region, table, wave)
-    c1, ck, send, it2, inv = outer_call(sizes, low, high, table, wave, shared)
+    shared = low_call(sizes, low, table, wave, shared)
+    c1, ck, send, it2, inv = high_call(sizes, high, table, wave, shared)
     recv = core_swap(send)
     out = cycle_call(c1, ck, recv, it2, inv)
     return out.reshape(2, 4, OWN_X, OWN_Y, 2 * LANES)

time: 47.6 us -> 46.6 us (0.979)
  the two profiles are of different devices: /device:TPU:31 before, /device:TPU:38 now
where the time goes in v4:
time: 46.6 us; the launch traced here: 45.9 us
  starting transfers between devices  24.5 us (53%)
  Pallas kernels  14.1 us (30%)
  waiting for transfers between devices  6.77 us (15%)
    ppermute x2, starting transfers between devices, along_x(): return lax.ppermute(values, ('gx', 'gy'), pairs)  13.7 us
    ppermute x2, starting transfers between devices, along_y(): return lax.ppermute(values, 'gy', pairs)  7.05 us
    ppermute x2, waiting for transfers between devices, along_x(): return lax.ppermute(values, ('gx', 'gy'), pairs)  4.53 us
    pallas_call x1, Pallas kernels, middle_call(): pl.pallas_call(kernel, out_shape=SHARED, in_specs=[SPEC] * 3, out_specs=(...  3.95 us
    ppermute x2, starting transfers between devices, core_swap(): return lax.ppermute(values, 'gy', [(j, j ^ 1) for j in range(gy_n)])  3.83 us
    pallas_call x1, Pallas kernels, high_call(): pl.pallas_call(kernel, out_shape=SHARED + (vmem(CX, CY, 8, LANES), vmem(2...  3.27 us
    pallas_call x1, Pallas kernels, cycle_call(): pl.pallas_call(cycle_kernel, out_shape=jax.ShapeDtypeStruct((rows, 2 * LA...  2.44 us
    ppermute x2, waiting for transfers between devices, core_swap(): return lax.ppermute(values, 'gy', [(j, j ^ 1) for j in range(gy_n)])  2.23 us
  transfers between devices with their start and end apart: 6, of which 3 were waited for; matrix products, arithmetic and copies ran while one was open for 0% of the time, Pallas kernels for 18%

profile of v4, /device:TPU:38, one launch (start us, length us, event | category | flops | bytes accessed | tf_op | source)
XLA Modules:
  0.0 45.9 jit_solution(10511185385178664188)
XLA Ops:
  0.0 1.9 %collective-permute-start = (s32[6,8,256]{2,1,0:T(8,128)}, s32[6,8,256]{2,1,0:T(8,128)S(1)}, u32[]{:S(2)}, u32[]{:S(2)}) collective-permute-start(s32[6,8,256]{2,1,0:T(8,128)} %labels.1), channel_id=1, source_target_pairs={{0,1},{1,0},{2,3},{3,2},{4,5},{5,4},{6,7},{7,6},{8,9},{9,8},{10,11... | collective-permute-start | bytes 147464 | tf_op jit(solution)/shard_map/ppermute | solution.py:664
  1.9 0.8 %shard_map.55 = s32[6,8,256]{2,1,0:T(8,128)S(1)} custom-call(s32[6,8,256]{2,1,0:T(8,128)} %labels.1), custom_call_target="tpu_custom_call" | custom-call | tf_op jit(solution)/shard_map/pallas_call | solution.py:529
  2.8 0.6 %collective-permute-done = s32[6,8,256]{2,1,0:T(8,128)S(1)} collective-permute-done((s32[6,8,256]{2,1,0:T(8,128)}, s32[6,8,256]{2,1,0:T(8,128)S(1)}, u32[]{:S(2)}, u32[]{:S(2)}) %collective-permute-start) | collective-permute-done | bytes 49184 | tf_op jit(solution)/shard_map/ppermute | solution.py:664
  3.3 11.2 %collective-permute-start.1 = (s32[6,16,256]{2,1,0:T(8,128)S(1)}, s32[6,16,256]{2,1,0:T(8,128)S(1)}, u32[]{:S(2)}, u32[]{:S(2)}) collective-permute-start(s32[6,16,256]{2,1,0:T(8,128)S(1)} %add_select_fusion.1.after), channel_id=1, source_target_pairs={{16,0},{32,16},{48,32},{64,48},{80,64},{96,80},{112,96},{128,112},... | collective-permute-start | bytes 294920 | tf_op jit(solution)/shard_map/ppermute | solution.py:657
  14.6 2.5 %collective-permute-start.2 = (s32[4,16,256]{2,1,0:T(8,128)S(1)}, s32[4,16,256]{2,1,0:T(8,128)S(1)}, u32[]{:S(2)}, u32[]{:S(2)}) collective-permute-start(s32[4,16,256]{2,1,0:T(8,128)S(1)} %slice_select_fusion), channel_id=1, source_target_pairs={{32,0},{48,16},{64,32},{80,48},{96,64},{112,80},{128,96},{144,112}... | collective-permute-start | bytes 196616 | tf_op jit(solution)/shard_map/ppermute | solution.py:657
  17.0 0.1 copy.30
  17.1 4.5 %collective-permute-done.2 = s32[4,16,256]{2,1,0:T(8,128)S(1)} collective-permute-done((s32[4,16,256]{2,1,0:T(8,128)S(1)}, s32[4,16,256]{2,1,0:T(8,128)S(1)}, u32[]{:S(2)}, u32[]{:S(2)}) %collective-permute-start.2) | collective-permute-done | bytes 65568 | tf_op jit(solution)/shard_map/ppermute | solution.py:657
  21.7 0.0 collective-permute-done.1
  21.7 0.1 copy.31
  21.8 0.1 fusion.refs_0_
  21.9 2.6 %collective-permute-start.4 = (s32[10,16,256]{2,1,0:T(8,128)S(1)}, s32[10,16,256]{2,1,0:T(8,128)S(1)}, u32[]{:S(2)}, u32[]{:S(2)}) collective-permute-start(s32[10,16,256]{2,1,0:T(8,128)S(1)} %slice.19), channel_id=1, source_target_pairs={{0,2},{1,3},{2,4},{3,5},{4,6},{5,7},{6,8},{7,9},{8,10},{9,11},{10,... | collective-permute-start | bytes 491528 | tf_op jit(solution)/shard_map/ppermute | solution.py:661
  24.5 4.5 %collective-permute-start.3 = (s32[9,16,256]{2,1,0:T(8,128)S(1)}, s32[9,16,256]{2,1,0:T(8,128)S(1)}, u32[]{:S(2)}, u32[]{:S(2)}) collective-permute-start(s32[9,16,256]{2,1,0:T(8,128)S(1)} %slice.18), channel_id=1, source_target_pairs={{2,0},{3,1},{4,2},{5,3},{6,4},{7,5},{8,6},{9,7},{10,8},{11,9},{12,... | collective-permute-start | bytes 442376 | tf_op jit(solution)/shard_map/ppermute | solution.py:661
  29.0 1.6 %shard_map.56 = (f32[1120,8,128]{2,1,0:T(8,128)S(1)}, f32[8,128]{1,0:T(8,128)S(1)}) custom-call(f32[8]{0:T(128)} %real_in.1, f32[8]{0:T(128)} %imag_in.1, f32[360]{0:T(512)} %angles_in.1, s32[4]{0:T(128)} %picks_in.1, s32[6,16,256]{2,1,0:T(8,128)S(1)} %add_select_fusion.1.after), custom_call_target="tpu_custom_call" | custom-call | tf_op jit(solution)/shard_map/pallas_call | solution.py:541
  30.6 3.9 %shard_map.57 = (f32[35,16,128]{2,1,0:T(8,128)S(1)}, f32[35,16,128]{2,1,0:T(8,128)S(1)}, f32[35,16,128]{2,1,0:T(8,128)S(1)}, f32[35,16,128]{2,1,0:T(8,128)S(1)},...) custom-call(s32[16,16,256]{2,1,0:T(8,128)S(1)} %fusion.refs_0_, ...), custom_call_target="tpu_custom_call" | custom-call | tf_op jit(solution)/shard_map/pallas_call | solution.py:561
  34.5 0.0 collective-permute-done.4.refs_0_
  34.5 2.1 %shard_map.58 = (f32[35,16,128]{2,1,0:T(8,128)S(1)}, f32[35,16,128]{2,1,0:T(8,128)S(1)}, f32[35,16,128]{2,1,0:T(8,128)S(1)}, f32[35,16,128]{2,1,0:T(8,128)S(1)},...) custom-call(s32[10,16,256]{2,1,0:T(8,128)S(1)} %collective-permute-d, ...), custom_call_target="tpu_custom_call", output_to_operand_aliasing={{0}: (3, {}), {1}: (4, {}), {2}: (5, {}), {3}: (6, {}), {4}... | custom-call | tf_op jit(solution)/shard_map/pallas_call | solution.py:575
  36.6 0.0 collective-permute-done.3.refs_0_
  36.6 3.3 %shard_map.59 = (f32[35,16,128]{2,1,0:T(8,128)S(1)}, f32[35,16,128]{2,1,0:T(8,128)S(1)}, f32[35,16,128]{2,1,0:T(8,128)S(1)}, f32[35,16,128]{2,1,0:T(8,128)S(1)},...) custom-call(s32[9,16,256]{2,1,0:T(8,128)S(1)} %collective-permute-do, ...), custom_call_target="tpu_custom_call", output_to_operand_aliasing={{0}: (3, {}), {1}: (4, {}), {2}: (5, {}), {3}: (6, {}), {4}... | custom-call | tf_op jit(solution)/shard_map/pallas_call | solution.py:590
  39.9 1.9 %collective-permute-start.5 = (f32[91,8,128]{2,1,0:T(8,128)S(1)}, f32[91,8,128]{2,1,0:T(8,128)S(1)}, u32[]{:S(2)}, u32[]{:S(2)}) collective-permute-start(f32[91,8,128]{2,1,0:T(8,128)S(1)} %get-tuple-element.64), channel_id=1, source_target_pairs={{0,1},{1,0},{2,3},{3,2},{4,5},{5,4},{6,7},{7,6},{8,9},{9,8},{10,11... | collective-permute-start | bytes 1118216 | tf_op jit(solution)/shard_map/ppermute | solution.py:664
  41.8 1.7 %collective-permute-done.5.recv = f32[91,8,128]{2,1,0:T(8,128)S(1)} collective-permute-done((f32[91,8,128]{2,1,0:T(8,128)S(1)}, f32[91,8,128]{2,1,0:T(8,128)S(1)}, u32[]{:S(2)}, u32[]{:S(2)}) %collective-permute-start.5) | collective-permute-done | bytes 372768 | tf_op jit(solution)/shard_map/ppermute | solution.py:664
  43.5 2.4 %shard_map.60 = f32[384,256]{1,0:T(8,128)} custom-call(f32[5,15,8,128]{3,2,1,0:T(8,128)S(1)} %get-tuple-element.62.c1_own, f32[2,5,16,128]{3,2,1,0:T(8,128)S(1)} %get-tuple-element.63.ck_own, f32[91,8,128]{2,1,0:T(8,128)S(1)} %collective-permute-done.5.recv, f32[48,2,8,128]{3,2,1,0:T(8,128)S(1)} %get-tuple-element.65.it2, f32[4,8,128]{2,1,0:T(8,128)S(1)} %get-tuple-element.66.inv), custom_call_target="tpu_custom_call" | custom-call | tf_op jit(solution)/shard_map/pallas_call | solution.py:612
  (5 shorter events, 0.1 us)
Async XLA Ops:
  0.0 3.3 %collective-permute-start = (s32[6,8,256]{2,1,0:T(8,128)}, s32[6,8,256]{2,1,0:T(8,128)S(1)}, u32[]{:S(2)}, u32[]{:S(2)}) collective-permute-start(s32[6,8,256]{2,1,0:T(8,128)} %labels.1), channel_id=1, source_target_pairs={{0,1},{1,0},{2,3},{3,2},{4,5},{5,4},{6,7},{7,6},{8,9},{9,8},{10,11... | collective-permute-start | bytes 147464 | tf_op jit(solution)/shard_map/ppermute | solution.py:664
  3.3 18.3 %collective-permute-start.1 = (s32[6,16,256]{2,1,0:T(8,128)S(1)}, s32[6,16,256]{2,1,0:T(8,128)S(1)}, u32[]{:S(2)}, u32[]{:S(2)}) collective-permute-start(s32[6,16,256]{2,1,0:T(8,128)S(1)} %add_select_fusion.1.after), channel_id=1, source_target_pairs={{16,0},{32,16},{48,32},{64,48},{80,64},{96,80},{112,96},{128,112},... | collective-permute-start | bytes 294920 | tf_op jit(solution)/shard_map/ppermute | solution.py:657
  14.6 7.1 %collective-permute-start.2 = (s32[4,16,256]{2,1,0:T(8,128)S(1)}, s32[4,16,256]{2,1,0:T(8,128)S(1)}, u32[]{:S(2)}, u32[]{:S(2)}) collective-permute-start(s32[4,16,256]{2,1,0:T(8,128)S(1)} %slice_select_fusion), channel_id=1, source_target_pairs={{32,0},{48,16},{64,32},{80,48},{96,64},{112,80},{128,96},{144,112}... | collective-permute-start | bytes 196616 | tf_op jit(solution)/shard_map/ppermute | solution.py:657
  21.9 12.6 %collective-permute-start.4 = (s32[10,16,256]{2,1,0:T(8,128)S(1)}, s32[10,16,256]{2,1,0:T(8,128)S(1)}, u32[]{:S(2)}, u32[]{:S(2)}) collective-permute-start(s32[10,16,256]{2,1,0:T(8,128)S(1)} %slice.19), channel_id=1, source_target_pairs={{0,2},{1,3},{2,4},{3,5},{4,6},{5,7},{6,8},{7,9},{8,10},{9,11},{10,... | collective-permute-start | bytes 491528 | tf_op jit(solution)/shard_map/ppermute | solution.py:661
  24.5 12.1 %collective-permute-start.3 = (s32[9,16,256]{2,1,0:T(8,128)S(1)}, s32[9,16,256]{2,1,0:T(8,128)S(1)}, u32[]{:S(2)}, u32[]{:S(2)}) collective-permute-start(s32[9,16,256]{2,1,0:T(8,128)S(1)} %slice.18), channel_id=1, source_target_pairs={{2,0},{3,1},{4,2},{5,3},{6,4},{7,5},{8,6},{9,7},{10,8},{11,9},{12,... | collective-permute-start | bytes 442376 | tf_op jit(solution)/shard_map/ppermute | solution.py:661
  39.9 3.6 %collective-permute-start.5 = (f32[91,8,128]{2,1,0:T(8,128)S(1)}, f32[91,8,128]{2,1,0:T(8,128)S(1)}, u32[]{:S(2)}, u32[]{:S(2)}) collective-permute-start(f32[91,8,128]{2,1,0:T(8,128)S(1)} %get-tuple-element.64), channel_id=1, source_target_pairs={{0,1},{1,0},{2,3},{3,2},{4,5},{5,4},{6,7},{7,6},{8,9},{9,8},{10,11... | collective-permute-start | bytes 1118216 | tf_op jit(solution)/shard_map/ppermute | solution.py:664

commit v5 on v4

--- a/solution.py
+++ b/solution.py
@@ -321,8 +321,8 @@
 
 
 def high_kernel(sizes, labels, tab, wave, *refs):
-    region = Region(sizes, tab, wave, refs[12:24], refs[29:])
-    c1_out, ck_out, send_out, it2_out, inv_out = refs[24:29]
+    region = Region(sizes, tab, wave, refs[12:24], refs[27:])
+    c1_out, ck_out, send_out = refs[24:27]
     core, y0, ny = region.core, region.y0, region.ny
     it1 = region.it1
     top = LOW + 2 * OWN_Y
@@ -339,24 +339,7 @@
     for k in range(2):
         for i in range(CX):
             ck_out[k, i, 8:16, :] = jnp.zeros((8, LANES), F32)
-    row_loop(0, CY, 1, lambda j: region.third_stage(j, c1_out, ck_out))
-
-    xb = core * LOW
-    yb = LOW + core * OWN_Y
-    xe = core * (PX - 1)
-    tables = (region.ie_r, region.io_r, region.ie_i, region.io_i)
-
-    def own_stage(k):
-        y = yb + k
-        for xx in range(OWN_X):
-            x = xb + xx
-            at = (y * PX + x) * 2
-            for h in range(2):
-                it2_out[xx * OWN_Y + k, h] = 1.2 * it1[at + h] + region.update(y, x, h)
-        for n, ref in enumerate(tables):
-            inv_out[n, pl.ds(k, 1), :] = ref[y, pl.ds(xe, 1), :]
-
-    row_loop(0, OWN_Y, 2, own_stage)
+    row_loop(0, CY, 3, lambda j: region.third_stage(j, c1_out, ck_out))
 
     j0 = 4 - 4 * core
     for i in range(CX):
@@ -386,52 +369,90 @@
 SEND = CX * NJ + 4 * CX + 2 * OWN_Y
 
 
-def cycle_kernel(c1_own, ck_own, recv, it2, inv, out, c1, ck, cc, pp, qq, parts, o0, o1):
+class Own(Region):
+    def __init__(self, refs):
+        (self.ie_r, self.io_r, self.ie_i, self.io_i, self.it1, self.pp, self.qq) = refs
+        self.sgn = sign_rows()
+
+
+def coarse_sums(ref, pp, qq, i, sweep, first, last):
+    edges, faces, centres = {}, {}, {}
+    for j in range(sweep, NJ - sweep):
+        v = ref[i * NJ + j]
+        near = up(v, first) + down(v, last)
+        edges[j], faces[j] = edge_face(v, near)
+        centres[j] = near
+    for j in range(sweep + 1, NJ - sweep - 1):
+        pp[i * NJ + j] = centres[j] + (faces[j - 1] + faces[j + 1])
+        qq[i * NJ + j] = faces[j] + (edges[j - 1] + edges[j + 1])
+
+
+def own_kernel(*refs):
+    own = Own(refs[:7])
+    c1_own, ck_own, it2, inv, c1, ck, pp, qq = refs[7:]
+    core = where_am_i()[0]
+    lanes = lane_iota()
+    first = lanes == 0
+    last = lanes == LANES - 1
+
+    xb = core * LOW
+    yb = LOW + core * OWN_Y
+    xe = core * (PX - 1)
+    tables = (own.ie_r, own.io_r, own.ie_i, own.io_i)
+
+    def own_stage(k):
+        y = yb + k
+        for xx in range(OWN_X):
+            x = xb + xx
+            at = (y * PX + x) * 2
+            for h in range(2):
+                it2[xx * OWN_Y + k, h] = 1.2 * own.it1[at + h] + own.update(y, x, h)
+        for n, ref in enumerate(tables):
+            inv[n, pl.ds(k, 1), :] = ref[y, pl.ds(xe, 1), :]
+
+    own_i = CX - core * CX
+    for i in range(CX):
+        for j in range(NJ):
+            c1[(own_i + i) * NJ + j] = c1_own[i, 4 * core + j]
+        for k in range(2):
+            ck[k, own_i + i] = ck_own[k, i]
+    row_loop(
+        own_i, CX, 5, lambda i: coarse_sums(c1, pp, qq, i, 0, first, last)
+    )
+    row_loop(0, OWN_Y, 2, own_stage)
+
+
+def cycle_kernel(recv, it2, inv, *refs):
+    c1, ck, pp, qq, out, cc, parts, o0, o1 = refs[4:]
     core = where_am_i()[0]
     lanes = lane_iota()
     first = lanes == 0
     last = lanes == LANES - 1
     sgn = sign_rows()
     j0 = 4 * core
+    other_i = core * CX
 
     def spread(row):
         return jnp.broadcast_to(row, (8, LANES))
 
-    def assemble(which):
-        own_i, other_i = CX - which * CX, which * CX
-        for i in range(CX):
-            for j in range(NJ):
-                c1[(own_i + i) * NJ + j] = c1_own[i, 4 * which + j]
-                c1[(other_i + i) * NJ + j] = recv[i * NJ + j]
-            for k in range(2):
-                for h in range(2):
-                    tile = slice(8 * h, 8 * h + 8)
-                    ck[k, own_i + i, tile, :] = ck_own[k, i, tile, :]
-                    ck[k, other_i + i, tile, :] = recv[CX * NJ + (k * CX + i) * 2 + h]
-
-    @pl.when(core == 0)
-    def _():
-        assemble(0)
-
-    @pl.when(core == 1)
-    def _():
-        assemble(1)
+    for i in range(CX):
+        for j in range(NJ):
+            c1[(other_i + i) * NJ + j] = recv[i * NJ + j]
+        for k in range(2):
+            for h in range(2):
+                tile = slice(8 * h, 8 * h + 8)
+                ck[k, other_i + i, tile, :] = recv[CX * NJ + (k * CX + i) * 2 + h]
 
     for sweep, (sum_step, relax_step) in enumerate(((5, 4), (4, 3), (3, 4))):
         ref = c1 if sweep == 0 else cc
 
         def sums(i, ref=ref, sweep=sweep):
-            edges, faces, centres = {}, {}, {}
-            for j in range(sweep, NJ - sweep):
-                v = ref[i * NJ + j]
-                near = up(v, first) + down(v, last)
-                edges[j], faces[j] = edge_face(v, near)
-                centres[j] = near
-            for j in range(sweep + 1, NJ - sweep - 1):
-                pp[i * NJ + j] = centres[j] + (faces[j - 1] + faces[j + 1])
-                qq[i * NJ + j] = faces[j] + (edges[j - 1] + edges[j + 1])
-
-        row_loop(sweep, NI - 2 * sweep, sum_step, sums)
+            coarse_sums(ref, pp, qq, i, sweep, first, last)
+
+        if sweep:
+            row_loop(sweep, NI - 2 * sweep, sum_step, sums)
+        else:
+            row_loop(other_i, CX, sum_step, sums)
 
         def relax(i, ref=ref, sweep=sweep):
             for j in range(sweep + 1, NJ - sweep - 1):
@@ -594,32 +615,46 @@
             vmem(CX, CY, 8, LANES),
             vmem(2, CX, 16, LANES),
             vmem(SEND, 8, LANES),
-            vmem(OWN_X * OWN_Y, 2, 8, LANES),
-            vmem(4, 8, LANES),
         ),
         in_specs=[SPEC] * 15,
-        out_specs=(SPEC,) * 17,
+        out_specs=(SPEC,) * 15,
         input_output_aliases={3 + n: n for n in range(12)},
         scratch_shapes=TABLES + [vmem(LOW * PX, 2 * LANES)],
         compiler_params=limit(6),
     )(*near_core(labels, tab, wave), *shared)
-    return results[12:]
-
-
-def cycle_call(*args):
-    points = NI * NJ
+    return results[:12], results[12:]
+
+
+POINTS = NI * NJ
+HALF = (vmem(POINTS, 8, LANES), vmem(2, NI, 16, LANES)) + (vmem(POINTS, 8, LANES),) * 2
+
+
+def own_call(shared, c1, ck):
+    used = shared[:4] + shared[6:9]
+    results = pl.pallas_call(
+        own_kernel,
+        out_shape=(vmem(OWN_X * OWN_Y, 2, 8, LANES), vmem(4, 8, LANES)) + HALF,
+        in_specs=[SPEC] * 9,
+        out_specs=(SPEC,) * 6,
+        compiler_params=limit(6),
+    )(*used, c1, ck)
+    return results[:2], results[2:]
+
+
+def cycle_call(recv, block, half):
     rows = OWN_X * OWN_Y * 8
-    return pl.pallas_call(
+    results = pl.pallas_call(
         cycle_kernel,
-        out_shape=jax.ShapeDtypeStruct((rows, 2 * LANES), F32),
-        in_specs=[SPEC] * 5,
-        out_specs=SPEC,
-        scratch_shapes=[vmem(points, 8, LANES), vmem(2, NI, 16, LANES)]
-        + [vmem(points, 8, LANES)] * 3
+        out_shape=HALF + (jax.ShapeDtypeStruct((rows, 2 * LANES), F32),),
+        in_specs=[SPEC] * 7,
+        out_specs=(SPEC,) * 5,
+        input_output_aliases={3 + n: n for n in range(4)},
+        scratch_shapes=[vmem(POINTS, 8, LANES)]
         + [pltpu.VMEM((2 * rows, 2 * LANES), jnp.bfloat16)]
         + [vmem(rows, LANES)] * 2,
         compiler_params=limit(8),
-    )(*near_core(*args))
+    )(*near_core(recv), *block, *half)
+    return results[4]
 
 
 def complex_inverse(real, imag):
@@ -690,9 +725,10 @@
     sizes = (OWN_X * gx_n, OWN_Y * gy_n)
     shared = middle_call(sizes, region, table, wave)
     shared = low_call(sizes, low, table, wave, shared)
-    c1, ck, send, it2, inv = high_call(sizes, high, table, wave, shared)
+    shared, (c1, ck, send) = high_call(sizes, high, table, wave, shared)
     recv = core_swap(send)
-    out = cycle_call(c1, ck, recv, it2, inv)
+    block, half = own_call(shared, c1, ck)
+    out = cycle_call(recv, block, half)
     return out.reshape(2, 4, OWN_X, OWN_Y, 2 * LANES)
 
 

time: 46.6 us -> 46.1 us (0.989)
    pallas_call x1 -> x2, Pallas kernels: 2.44 us -> 2.56 us  [the longest x1 2.2 us: cycle_call(): pl.pallas_call(cycle_kernel, out_shape=HALF + (jax.ShapeDtypeStruct((rows...]
  transfers between devices with their start and end apart: 6 -> 6, of which waited for: 3 -> 3; matrix products, arithmetic and copies ran while one was open for 0% -> 0% of each run, Pallas kernels for 18% -> 19%
where the time goes in v5:
time: 46.1 us; the launch traced here: 45.5 us
  starting transfers between devices  24.5 us (53%)
  Pallas kernels  14 us (30%)
  waiting for transfers between devices  6.4 us (14%)
    ppermute x2, starting transfers between devices, along_x(): return lax.ppermute(values, ('gx', 'gy'), pairs)  13.7 us
    ppermute x2, starting transfers between devices, along_y(): return lax.ppermute(values, 'gy', pairs)  7.05 us
    ppermute x2, waiting for transfers between devices, along_x(): return lax.ppermute(values, ('gx', 'gy'), pairs)  4.53 us
    pallas_call x1, Pallas kernels, middle_call(): pl.pallas_call(kernel, out_shape=SHARED, in_specs=[SPEC] * 3, out_specs=(...  3.87 us
    ppermute x2, starting transfers between devices, core_swap(): return lax.ppermute(values, 'gy', [(j, j ^ 1) for j in range(gy_n)])  3.83 us
    pallas_call x1, Pallas kernels, high_call(): pl.pallas_call(kernel, out_shape=SHARED + (vmem(CX, CY, 8, LANES), vmem(2...  3.16 us
    pallas_call x1, Pallas kernels, cycle_call(): pl.pallas_call(cycle_kernel, out_shape=HALF + (jax.ShapeDtypeStruct((rows...  2.2 us
    pallas_call x1, Pallas kernels, low_call(): pl.pallas_call(kernel, out_shape=SHARED, in_specs=[SPEC] * 15, out_specs=...  2.04 us
  transfers between devices with their start and end apart: 6, of which 3 were waited for; matrix products, arithmetic and copies ran while one was open for 0% of the time, Pallas kernels for 19%

profile of v5, /device:TPU:38, one launch (start us, length us, event | category | flops | bytes accessed | tf_op | source)
XLA Modules:
  0.0 45.5 jit_solution(2264206765642733227)
XLA Ops:
  0.0 1.9 %collective-permute-start = (s32[6,8,256]{2,1,0:T(8,128)}, s32[6,8,256]{2,1,0:T(8,128)S(1)}, u32[]{:S(2)}, u32[]{:S(2)}) collective-permute-start(s32[6,8,256]{2,1,0:T(8,128)} %labels.1), channel_id=1, source_target_pairs={{0,1},{1,0},{2,3},{3,2},{4,5},{5,4},{6,7},{7,6},{8,9},{9,8},{10,11... | collective-permute-start | bytes 147464 | tf_op jit(solution)/shard_map/ppermute | solution.py:699
  1.9 0.8 %shard_map.55 = s32[6,8,256]{2,1,0:T(8,128)S(1)} custom-call(s32[6,8,256]{2,1,0:T(8,128)} %labels.1), custom_call_target="tpu_custom_call" | custom-call | tf_op jit(solution)/shard_map/pallas_call | solution.py:550
  2.8 0.6 %collective-permute-done = s32[6,8,256]{2,1,0:T(8,128)S(1)} collective-permute-done((s32[6,8,256]{2,1,0:T(8,128)}, s32[6,8,256]{2,1,0:T(8,128)S(1)}, u32[]{:S(2)}, u32[]{:S(2)}) %collective-permute-start) | collective-permute-done | bytes 49184 | tf_op jit(solution)/shard_map/ppermute | solution.py:699
  3.3 11.2 %collective-permute-start.1 = (s32[6,16,256]{2,1,0:T(8,128)S(1)}, s32[6,16,256]{2,1,0:T(8,128)S(1)}, u32[]{:S(2)}, u32[]{:S(2)}) collective-permute-start(s32[6,16,256]{2,1,0:T(8,128)S(1)} %add_select_fusion.1.after), channel_id=1, source_target_pairs={{16,0},{32,16},{48,32},{64,48},{80,64},{96,80},{112,96},{128,112},... | collective-permute-start | bytes 294920 | tf_op jit(solution)/shard_map/ppermute | solution.py:692
  14.6 2.5 %collective-permute-start.2 = (s32[4,16,256]{2,1,0:T(8,128)S(1)}, s32[4,16,256]{2,1,0:T(8,128)S(1)}, u32[]{:S(2)}, u32[]{:S(2)}) collective-permute-start(s32[4,16,256]{2,1,0:T(8,128)S(1)} %slice_select_fusion), channel_id=1, source_target_pairs={{32,0},{48,16},{64,32},{80,48},{96,64},{112,80},{128,96},{144,112}... | collective-permute-start | bytes 196616 | tf_op jit(solution)/shard_map/ppermute | solution.py:692
  17.0 0.1 copy.34
  17.1 4.5 %collective-permute-done.2 = s32[4,16,256]{2,1,0:T(8,128)S(1)} collective-permute-done((s32[4,16,256]{2,1,0:T(8,128)S(1)}, s32[4,16,256]{2,1,0:T(8,128)S(1)}, u32[]{:S(2)}, u32[]{:S(2)}) %collective-permute-start.2) | collective-permute-done | bytes 65568 | tf_op jit(solution)/shard_map/ppermute | solution.py:692
  21.7 0.0 collective-permute-done.1
  21.7 0.1 copy.35
  21.8 0.1 fusion.refs_0_
  21.9 2.6 %collective-permute-start.4 = (s32[10,16,256]{2,1,0:T(8,128)S(1)}, s32[10,16,256]{2,1,0:T(8,128)S(1)}, u32[]{:S(2)}, u32[]{:S(2)}) collective-permute-start(s32[10,16,256]{2,1,0:T(8,128)S(1)} %slice.19), channel_id=1, source_target_pairs={{0,2},{1,3},{2,4},{3,5},{4,6},{5,7},{6,8},{7,9},{8,10},{9,11},{10,... | collective-permute-start | bytes 491528 | tf_op jit(solution)/shard_map/ppermute | solution.py:696
  24.5 4.5 %collective-permute-start.3 = (s32[9,16,256]{2,1,0:T(8,128)S(1)}, s32[9,16,256]{2,1,0:T(8,128)S(1)}, u32[]{:S(2)}, u32[]{:S(2)}) collective-permute-start(s32[9,16,256]{2,1,0:T(8,128)S(1)} %slice.18), channel_id=1, source_target_pairs={{2,0},{3,1},{4,2},{5,3},{6,4},{7,5},{8,6},{9,7},{10,8},{11,9},{12,... | collective-permute-start | bytes 442376 | tf_op jit(solution)/shard_map/ppermute | solution.py:696
  29.0 1.6 %shard_map.56 = (f32[1120,8,128]{2,1,0:T(8,128)S(1)}, f32[8,128]{1,0:T(8,128)S(1)}) custom-call(f32[8]{0:T(128)} %real_in.1, f32[8]{0:T(128)} %imag_in.1, f32[360]{0:T(512)} %angles_in.1, s32[4]{0:T(128)} %picks_in.1, s32[6,16,256]{2,1,0:T(8,128)S(1)} %add_select_fusion.1.after), custom_call_target="tpu_custom_call" | custom-call | tf_op jit(solution)/shard_map/pallas_call | solution.py:562
  30.6 3.9 %shard_map.57 = (f32[35,16,128]{2,1,0:T(8,128)S(1)}, f32[35,16,128]{2,1,0:T(8,128)S(1)}, f32[35,16,128]{2,1,0:T(8,128)S(1)}, f32[35,16,128]{2,1,0:T(8,128)S(1)},...) custom-call(s32[16,16,256]{2,1,0:T(8,128)S(1)} %fusion.refs_0_, ...), custom_call_target="tpu_custom_call" | custom-call | tf_op jit(solution)/shard_map/pallas_call | solution.py:582
  34.5 0.0 collective-permute-done.4.refs_0_
  34.5 2.0 %shard_map.58 = (f32[35,16,128]{2,1,0:T(8,128)S(1)}, f32[35,16,128]{2,1,0:T(8,128)S(1)}, f32[35,16,128]{2,1,0:T(8,128)S(1)}, f32[35,16,128]{2,1,0:T(8,128)S(1)},...) custom-call(s32[10,16,256]{2,1,0:T(8,128)S(1)} %collective-permute-d, ...), custom_call_target="tpu_custom_call", output_to_operand_aliasing={{0}: (3, {}), {1}: (4, {}), {2}: (5, {}), {3}: (6, {}), {4}... | custom-call | tf_op jit(solution)/shard_map/pallas_call | solution.py:596
  36.5 0.0 collective-permute-done.3.refs_0_
  36.5 3.2 %shard_map.59 = (f32[35,16,128]{2,1,0:T(8,128)S(1)}, f32[35,16,128]{2,1,0:T(8,128)S(1)}, f32[35,16,128]{2,1,0:T(8,128)S(1)}, f32[35,16,128]{2,1,0:T(8,128)S(1)},...) custom-call(s32[9,16,256]{2,1,0:T(8,128)S(1)} %collective-permute-do, ...), custom_call_target="tpu_custom_call", output_to_operand_aliasing={{0}: (3, {}), {1}: (4, {}), {2}: (5, {}), {3}: (6, {}), {4}... | custom-call | tf_op jit(solution)/shard_map/pallas_call | solution.py:611
  39.7 1.9 %collective-permute-start.5 = (f32[91,8,128]{2,1,0:T(8,128)S(1)}, f32[91,8,128]{2,1,0:T(8,128)S(1)}, u32[]{:S(2)}, u32[]{:S(2)}) collective-permute-start(f32[91,8,128]{2,1,0:T(8,128)S(1)} %get-tuple-element.74), channel_id=1, source_target_pairs={{0,1},{1,0},{2,3},{3,2},{4,5},{5,4},{6,7},{7,6},{8,9},{9,8},{10,11... | collective-permute-start | bytes 1118216 | tf_op jit(solution)/shard_map/ppermute | solution.py:699
  41.6 0.4 shard_map.60
  42.0 1.3 %collective-permute-done.5.recv = f32[91,8,128]{2,1,0:T(8,128)S(1)} collective-permute-done((f32[91,8,128]{2,1,0:T(8,128)S(1)}, f32[91,8,128]{2,1,0:T(8,128)S(1)}, u32[]{:S(2)}, u32[]{:S(2)}) %collective-permute-start.5) | collective-permute-done | bytes 372768 | tf_op jit(solution)/shard_map/ppermute | solution.py:699
  43.3 2.2 %shard_map.61 = (f32[110,8,128]{2,1,0:T(8,128)S(1)}, f32[2,10,16,128]{3,2,1,0:T(8,128)S(1)}, f32[110,8,128]{2,1,0:T(8,128)S(1)}, f32[110,8,128]{2,1,0:T(8,128)S(1)}, f32[384,256]{1,0:T(8,128)}) custom-call(f32[91,8,128]{2,1,0:T(8,128)S(1)} %collective-permute-done.5.recv, ...), custom_call_target="tpu_custom_call", output_to_operand_aliasing={{0}: (3, {}), {1}: (4, {}), {2}: (5, {}), {3}: (6, {})} | custom-call | tf_op jit(solution)/shard_map/pallas_call | solution.py:646
  (5 shorter events, 0.1 us)
Async XLA Ops:
  0.0 3.3 %collective-permute-start = (s32[6,8,256]{2,1,0:T(8,128)}, s32[6,8,256]{2,1,0:T(8,128)S(1)}, u32[]{:S(2)}, u32[]{:S(2)}) collective-permute-start(s32[6,8,256]{2,1,0:T(8,128)} %labels.1), channel_id=1, source_target_pairs={{0,1},{1,0},{2,3},{3,2},{4,5},{5,4},{6,7},{7,6},{8,9},{9,8},{10,11... | collective-permute-start | bytes 147464 | tf_op jit(solution)/shard_map/ppermute | solution.py:699
  3.3 18.3 %collective-permute-start.1 = (s32[6,16,256]{2,1,0:T(8,128)S(1)}, s32[6,16,256]{2,1,0:T(8,128)S(1)}, u32[]{:S(2)}, u32[]{:S(2)}) collective-permute-start(s32[6,16,256]{2,1,0:T(8,128)S(1)} %add_select_fusion.1.after), channel_id=1, source_target_pairs={{16,0},{32,16},{48,32},{64,48},{80,64},{96,80},{112,96},{128,112},... | collective-permute-start | bytes 294920 | tf_op jit(solution)/shard_map/ppermute | solution.py:692
  14.6 7.1 %collective-permute-start.2 = (s32[4,16,256]{2,1,0:T(8,128)S(1)}, s32[4,16,256]{2,1,0:T(8,128)S(1)}, u32[]{:S(2)}, u32[]{:S(2)}) collective-permute-start(s32[4,16,256]{2,1,0:T(8,128)S(1)} %slice_select_fusion), channel_id=1, source_target_pairs={{32,0},{48,16},{64,32},{80,48},{96,64},{112,80},{128,96},{144,112}... | collective-permute-start | bytes 196616 | tf_op jit(solution)/shard_map/ppermute | solution.py:692
  21.9 12.6 %collective-permute-start.4 = (s32[10,16,256]{2,1,0:T(8,128)S(1)}, s32[10,16,256]{2,1,0:T(8,128)S(1)}, u32[]{:S(2)}, u32[]{:S(2)}) collective-permute-start(s32[10,16,256]{2,1,0:T(8,128)S(1)} %slice.19), channel_id=1, source_target_pairs={{0,2},{1,3},{2,4},{3,5},{4,6},{5,7},{6,8},{7,9},{8,10},{9,11},{10,... | collective-permute-start | bytes 491528 | tf_op jit(solution)/shard_map/ppermute | solution.py:696
  24.5 12.0 %collective-permute-start.3 = (s32[9,16,256]{2,1,0:T(8,128)S(1)}, s32[9,16,256]{2,1,0:T(8,128)S(1)}, u32[]{:S(2)}, u32[]{:S(2)}) collective-permute-start(s32[9,16,256]{2,1,0:T(8,128)S(1)} %slice.18), channel_id=1, source_target_pairs={{2,0},{3,1},{4,2},{5,3},{6,4},{7,5},{8,6},{9,7},{10,8},{11,9},{12,... | collective-permute-start | bytes 442376 | tf_op jit(solution)/shard_map/ppermute | solution.py:696
  39.7 3.6 %collective-permute-start.5 = (f32[91,8,128]{2,1,0:T(8,128)S(1)}, f32[91,8,128]{2,1,0:T(8,128)S(1)}, u32[]{:S(2)}, u32[]{:S(2)}) collective-permute-start(f32[91,8,128]{2,1,0:T(8,128)S(1)} %get-tuple-element.74), channel_id=1, source_target_pairs={{0,1},{1,0},{2,3},{3,2},{4,5},{5,4},{6,7},{7,6},{8,9},{9,8},{10,11... | collective-permute-start | bytes 1118216 | tf_op jit(solution)/shard_map/ppermute | solution.py:699

commit v6 on v5

--- a/solution.py
+++ b/solution.py
@@ -189,30 +189,28 @@
                     start = pl.multiple_of((n * step + k) * PX + 8 * h, 8)
                     part = self.apart[pl.ds(start, 8), :]
                     at = (y, pl.ds(8 * h, 8), slice(None))
-                    halves = []
-                    for odd, (inv_r, inv_i, g_r, g_i) in enumerate(
-                        (
-                            (self.ie_r, self.ie_i, self.ge_r, self.ge_i),
-                            (self.io_r, self.io_i, self.go_r, self.go_i),
-                        )
+                    label = part[:, :LANES].astype(jnp.int32)
+                    index = jnp.where(inside[h], label, OUTSIDE) + beyond
+                    even = [self.pick(n, index) for n in range(4)]
+                    label = part[:, LANES:].astype(jnp.int32)
+                    index = jnp.where(inside[h], label, OUTSIDE) + beyond
+                    chosen = 4 + 2 * ((first_row + k) % 2)
+                    odd = [self.pick(n, index) for n in range(chosen)]
+                    halves = (even, odd)
+                    for (ir, ii, sr, si), (inv_r, inv_i, g_r, g_i) in (
+                        (even, (self.ie_r, self.ie_i, self.ge_r, self.ge_i)),
+                        (odd[:4], (self.io_r, self.io_i, self.go_r, self.go_i)),
                     ):
-                        label = part[:, odd * LANES : (odd + 1) * LANES].astype(jnp.int32)
-                        index = jnp.where(inside[h], label, OUTSIDE) + beyond
-                        ir = self.pick(0, index)
-                        ii = self.pick(1, index)
-                        sr = self.pick(2, index)
-                        si = self.pick(3, index)
                         inv_r[at] = ir
                         inv_i[at] = ii
-                        g_r[at] = (25.0 / 14.0) * (ir * sr - ii * si)
-                        g_i[at] = (25.0 / 14.0) * (ir * si + ii * sr)
-                        halves.append((sr, si))
-                        if odd and (first_row + k) % 2 == 1:
-                            self.kr[at] = self.pick(4, index)
-                            self.ki[at] = self.pick(5, index)
+                        g_r[at] = (4.0 / 14.0) * (ir * sr - ii * si)
+                        g_i[at] = (4.0 / 14.0) * (ir * si + ii * sr)
+                    if chosen > 4:
+                        self.kr[at] = odd[4]
+                        self.ki[at] = odd[5]
                     for c, out in ((0, self.sa_r), (1, self.sa_i)):
-                        se = halves[0][c]
-                        out[at] = se + down(se, self.last) + 2.0 * halves[1][c]
+                        se = halves[0][2 + c]
+                        out[at] = (se + down(se, self.last) + 2.0 * halves[1][2 + c]) * (1.0 / 14.0)
             return carry
 
         lax.fori_loop(0, count // step, some, 0)
@@ -263,8 +261,8 @@
     def second_stage(self, y):
         for x in range(1, 14):
             at = (y * PX + x) * 2
-            we = 0.4 * self.it1[at] + self.update(y, x, 0)
-            wo = 0.4 * self.it1[at + 1] + self.update(y, x, 1)
+            we = self.it1[at] + self.update(y, x, 0)
+            wo = self.it1[at + 1] + self.update(y, x, 1)
             p = we + down(we, self.last)
             half = p + wo
             after = jnp.where(self.last, -wo, pltpu.roll(wo, LANES - 1, 1))
@@ -286,10 +284,10 @@
             u = ba + ab
             if 2 <= x <= 12:
                 at = base + x
-                gs[x] = (14.0 * u + 3.0 * bb) + (
+                gs[x] = (u + (3.0 / 14.0) * bb) + (
                     (self.sy[at] + self.sy[at + 2 * PX]) + 2.0 * self.sy[at + PX]
                 )
-            hs[x] = 14.0 * aa + (3.0 * u + bb)
+            hs[x] = aa + ((3.0 / 14.0) * u + (1.0 / 14.0) * bb)
         for i in range(CX):
             b = 2 + 2 * i
             mx = jnp.where(self.x0 + b + 2 == self.nx, 1.0, 2.0).astype(F32)
@@ -298,7 +296,7 @@
                 + 2.0 * (gs[b + 1] + (hs[b] + hs[b + 2]))
                 + (hs[b - 1] + hs[b + 3])
                 + mx * hs[b + 1]
-            ) * (1.0 / 1920.0)
+            ) * (14.0 / 1920.0)
             kr = row_of(self.kr, 3 + 2 * j, b + 1)
             ki = row_of(self.ki, 3 + 2 * j, b + 1)
             c1_out[i, j] = kr * raw + ki * (self.sgn * turned(raw))
@@ -339,7 +337,7 @@
     for k in range(2):
         for i in range(CX):
             ck_out[k, i, 8:16, :] = jnp.zeros((8, LANES), F32)
-    row_loop(0, CY, 3, lambda j: region.third_stage(j, c1_out, ck_out))
+    row_loop(0, CY, 1, lambda j: region.third_stage(j, c1_out, ck_out))
 
     j0 = 4 - 4 * core
     for i in range(CX):
@@ -406,7 +404,7 @@
             x = xb + xx
             at = (y * PX + x) * 2
             for h in range(2):
-                it2[xx * OWN_Y + k, h] = 1.2 * own.it1[at + h] + own.update(y, x, h)
+                it2[xx * OWN_Y + k, h] = 3.0 * own.it1[at + h] + own.update(y, x, h)
         for n, ref in enumerate(tables):
             inv[n, pl.ds(k, 1), :] = ref[y, pl.ds(xe, 1), :]
 
@@ -423,7 +421,7 @@
 
 
 def cycle_kernel(recv, it2, inv, *refs):
-    c1, ck, pp, qq, out, cc, parts, o0, o1 = refs[4:]
+    c1, ck, pp, qq, out, cc, parts, o0, o1, stage, sems = refs[4:]
     core = where_am_i()[0]
     lanes = lane_iota()
     first = lanes == 0
@@ -479,7 +477,6 @@
     cols = lax.broadcasted_iota(jnp.int32, (2 * LANES, 2 * LANES), 1)
     target = jnp.where(rows < LANES, 2 * rows, 2 * (rows - LANES) + 1)
     perm = jnp.where(cols == target, 1.0, 0.0).astype(jnp.bfloat16)
-    count = OWN_X * OWN_Y
 
     def fine(x, y, value):
         col = x * OWN_Y + y
@@ -491,6 +488,7 @@
         return even, odd
 
     size = 2 * OWN_Y * 8
+    copies = []
     for i in range(OWN_X // 2):
         for j in range(OWN_Y // 2):
             at = (i + 4) * NJ + j + 4
@@ -517,13 +515,23 @@
         mixed = jnp.dot(
             parts[i * 2 * size : (i + 1) * 2 * size, :], perm, preferred_element_type=F32
         )
-        for n in range(2 * OWN_Y):
+        rows_in = 2 * OWN_Y
+        for n in range(rows_in):
             block = mixed[n * 8 : n * 8 + 8] + mixed[size + n * 8 : size + n * 8 + 8]
-            col = i * 2 * OWN_Y + n
-            o0[pl.ds(col, 8, stride=count), :] = block[:, :LANES]
-            o1[pl.ds(col, 8, stride=count), :] = block[:, LANES:]
-    out[:, :LANES] = o0[...]
-    out[:, LANES:] = o1[...]
+            o0[pl.ds(i * size + n, 8, stride=rows_in), :] = block[:, :LANES]
+            o1[pl.ds(i * size + n, 8, stride=rows_in), :] = block[:, LANES:]
+        for f in range(8):
+            take = slice(i * size + f * rows_in, i * size + (f + 1) * rows_in)
+            stage[i, f, :, :LANES] = o0[take]
+            stage[i, f, :, LANES:] = o1[take]
+        copies.append(
+            pltpu.make_async_copy(
+                stage.at[i], out.at[:, pl.ds(i * rows_in, rows_in), :], sems.at[i]
+            )
+        )
+        copies[-1].start()
+    for copy in copies:
+        copy.wait()
 
 
 def vmem(*shape):
@@ -645,13 +653,15 @@
     rows = OWN_X * OWN_Y * 8
     results = pl.pallas_call(
         cycle_kernel,
-        out_shape=HALF + (jax.ShapeDtypeStruct((rows, 2 * LANES), F32),),
+        out_shape=HALF
+        + (jax.ShapeDtypeStruct((8, OWN_X * OWN_Y, 2 * LANES), F32),),
         in_specs=[SPEC] * 7,
-        out_specs=(SPEC,) * 5,
+        out_specs=(SPEC,) * 4 + (pl.BlockSpec(memory_space=pltpu.HBM),),
         input_output_aliases={3 + n: n for n in range(4)},
         scratch_shapes=[vmem(POINTS, 8, LANES)]
         + [pltpu.VMEM((2 * rows, 2 * LANES), jnp.bfloat16)]
-        + [vmem(rows, LANES)] * 2,
+        + [vmem(rows, LANES)] * 2
+        + [vmem(OWN_X // 2, 8, 2 * OWN_Y, 2 * LANES), pltpu.SemaphoreType.DMA((3,))],
         compiler_params=limit(8),
     )(*near_core(recv), *block, *half)
     return results[4]
@@ -669,7 +679,7 @@
     src_r = SOURCE_GAIN * (er - 1.0)
     src_i = SOURCE_GAIN * ei
     ci_r, ci_i = complex_inverse(128.0 / 120.0 - med_r, -med_i)
-    scale = 14.0 * DAMPING / 30.0
+    scale = 2.5 * 14.0 * DAMPING / 30.0
     return (
         scale * inv_r, scale * inv_i, 1.2 * src_r, 1.2 * src_i,
         DAMPING * ci_r, DAMPING * ci_i,

time: 46.1 us -> 46 us (level)
  no operation moved by 1% of the time
where the time goes in v6:
time: 46 us; the launch traced here: 45.4 us
  starting transfers between devices  24.5 us (53%)
  Pallas kernels  14 us (30%)
  waiting for transfers between devices  6.4 us (14%)
    ppermute x2, starting transfers between devices, along_x(): return lax.ppermute(values, ('gx', 'gy'), pairs)  13.7 us
    ppermute x2, starting transfers between devices, along_y(): return lax.ppermute(values, 'gy', pairs)  7.05 us
    ppermute x2, waiting for transfers between devices, along_x(): return lax.ppermute(values, ('gx', 'gy'), pairs)  4.53 us
    pallas_call x1, Pallas kernels, middle_call(): pl.pallas_call(kernel, out_shape=SHARED, in_specs=[SPEC] * 3, out_specs=(...  3.84 us
    ppermute x2, starting transfers between devices, core_swap(): return lax.ppermute(values, 'gy', [(j, j ^ 1) for j in range(gy_n)])  3.83 us
    pallas_call x1, Pallas kernels, high_call(): pl.pallas_call(kernel, out_shape=SHARED + (vmem(CX, CY, 8, LANES), vmem(2...  3.21 us
    pallas_call x1, Pallas kernels, cycle_call(): pl.pallas_call(cycle_kernel, out_shape=HALF + (jax.ShapeDtypeStruct((8, O...  2.14 us
    pallas_call x1, Pallas kernels, low_call(): pl.pallas_call(kernel, out_shape=SHARED, in_specs=[SPEC] * 15, out_specs=...  2.01 us
  transfers between devices with their start and end apart: 6, of which 3 were waited for; matrix products, arithmetic and copies ran while one was open for 0% of the time, Pallas kernels for 19%

profile of v6, /device:TPU:38, one launch (start us, length us, event | category | flops | bytes accessed | tf_op | source)
XLA Modules:
  0.0 45.4 jit_solution(12291171788254055366)
XLA Ops:
  0.0 1.9 %collective-permute-start = (s32[6,8,256]{2,1,0:T(8,128)}, s32[6,8,256]{2,1,0:T(8,128)S(1)}, u32[]{:S(2)}, u32[]{:S(2)}) collective-permute-start(s32[6,8,256]{2,1,0:T(8,128)} %labels.1), channel_id=1, source_target_pairs={{0,1},{1,0},{2,3},{3,2},{4,5},{5,4},{6,7},{7,6},{8,9},{9,8},{10,11... | collective-permute-start | bytes 147464 | tf_op jit(solution)/shard_map/ppermute | solution.py:709
  1.9 0.8 %shard_map.55 = s32[6,8,256]{2,1,0:T(8,128)S(1)} custom-call(s32[6,8,256]{2,1,0:T(8,128)} %labels.1), custom_call_target="tpu_custom_call" | custom-call | tf_op jit(solution)/shard_map/pallas_call | solution.py:558
  2.8 0.6 %collective-permute-done = s32[6,8,256]{2,1,0:T(8,128)S(1)} collective-permute-done((s32[6,8,256]{2,1,0:T(8,128)}, s32[6,8,256]{2,1,0:T(8,128)S(1)}, u32[]{:S(2)}, u32[]{:S(2)}) %collective-permute-start) | collective-permute-done | bytes 49184 | tf_op jit(solution)/shard_map/ppermute | solution.py:709
  3.3 11.2 %collective-permute-start.1 = (s32[6,16,256]{2,1,0:T(8,128)S(1)}, s32[6,16,256]{2,1,0:T(8,128)S(1)}, u32[]{:S(2)}, u32[]{:S(2)}) collective-permute-start(s32[6,16,256]{2,1,0:T(8,128)S(1)} %add_select_fusion.1.after), channel_id=1, source_target_pairs={{16,0},{32,16},{48,32},{64,48},{80,64},{96,80},{112,96},{128,112},... | collective-permute-start | bytes 294920 | tf_op jit(solution)/shard_map/ppermute | solution.py:702
  14.6 2.5 %collective-permute-start.2 = (s32[4,16,256]{2,1,0:T(8,128)S(1)}, s32[4,16,256]{2,1,0:T(8,128)S(1)}, u32[]{:S(2)}, u32[]{:S(2)}) collective-permute-start(s32[4,16,256]{2,1,0:T(8,128)S(1)} %slice_select_fusion), channel_id=1, source_target_pairs={{32,0},{48,16},{64,32},{80,48},{96,64},{112,80},{128,96},{144,112}... | collective-permute-start | bytes 196616 | tf_op jit(solution)/shard_map/ppermute | solution.py:702
  17.0 0.1 copy.34
  17.1 4.5 %collective-permute-done.2 = s32[4,16,256]{2,1,0:T(8,128)S(1)} collective-permute-done((s32[4,16,256]{2,1,0:T(8,128)S(1)}, s32[4,16,256]{2,1,0:T(8,128)S(1)}, u32[]{:S(2)}, u32[]{:S(2)}) %collective-permute-start.2) | collective-permute-done | bytes 65568 | tf_op jit(solution)/shard_map/ppermute | solution.py:702
  21.7 0.0 collective-permute-done.1
  21.7 0.1 copy.35
  21.8 0.1 fusion.refs_0_
  21.9 2.6 %collective-permute-start.4 = (s32[10,16,256]{2,1,0:T(8,128)S(1)}, s32[10,16,256]{2,1,0:T(8,128)S(1)}, u32[]{:S(2)}, u32[]{:S(2)}) collective-permute-start(s32[10,16,256]{2,1,0:T(8,128)S(1)} %slice.19), channel_id=1, source_target_pairs={{0,2},{1,3},{2,4},{3,5},{4,6},{5,7},{6,8},{7,9},{8,10},{9,11},{10,... | collective-permute-start | bytes 491528 | tf_op jit(solution)/shard_map/ppermute | solution.py:706
  24.5 4.5 %collective-permute-start.3 = (s32[9,16,256]{2,1,0:T(8,128)S(1)}, s32[9,16,256]{2,1,0:T(8,128)S(1)}, u32[]{:S(2)}, u32[]{:S(2)}) collective-permute-start(s32[9,16,256]{2,1,0:T(8,128)S(1)} %slice.18), channel_id=1, source_target_pairs={{2,0},{3,1},{4,2},{5,3},{6,4},{7,5},{8,6},{9,7},{10,8},{11,9},{12,... | collective-permute-start | bytes 442376 | tf_op jit(solution)/shard_map/ppermute | solution.py:706
  29.0 1.6 %shard_map.56 = (f32[1120,8,128]{2,1,0:T(8,128)S(1)}, f32[8,128]{1,0:T(8,128)S(1)}) custom-call(f32[8]{0:T(128)} %real_in.1, f32[8]{0:T(128)} %imag_in.1, f32[360]{0:T(512)} %angles_in.1, s32[4]{0:T(128)} %picks_in.1, s32[6,16,256]{2,1,0:T(8,128)S(1)} %add_select_fusion.1.after), custom_call_target="tpu_custom_call" | custom-call | tf_op jit(solution)/shard_map/pallas_call | solution.py:570
  30.6 3.8 %shard_map.57 = (f32[35,16,128]{2,1,0:T(8,128)S(1)}, f32[35,16,128]{2,1,0:T(8,128)S(1)}, f32[35,16,128]{2,1,0:T(8,128)S(1)}, f32[35,16,128]{2,1,0:T(8,128)S(1)},...) custom-call(s32[16,16,256]{2,1,0:T(8,128)S(1)} %fusion.refs_0_, ...), custom_call_target="tpu_custom_call" | custom-call | tf_op jit(solution)/shard_map/pallas_call | solution.py:590
  34.4 0.0 collective-permute-done.4.refs_0_
  34.4 2.0 %shard_map.58 = (f32[35,16,128]{2,1,0:T(8,128)S(1)}, f32[35,16,128]{2,1,0:T(8,128)S(1)}, f32[35,16,128]{2,1,0:T(8,128)S(1)}, f32[35,16,128]{2,1,0:T(8,128)S(1)},...) custom-call(s32[10,16,256]{2,1,0:T(8,128)S(1)} %collective-permute-d, ...), custom_call_target="tpu_custom_call", output_to_operand_aliasing={{0}: (3, {}), {1}: (4, {}), {2}: (5, {}), {3}: (6, {}), {4}... | custom-call | tf_op jit(solution)/shard_map/pallas_call | solution.py:604
  36.5 0.0 collective-permute-done.3.refs_0_
  36.5 3.2 %shard_map.59 = (f32[35,16,128]{2,1,0:T(8,128)S(1)}, f32[35,16,128]{2,1,0:T(8,128)S(1)}, f32[35,16,128]{2,1,0:T(8,128)S(1)}, f32[35,16,128]{2,1,0:T(8,128)S(1)},...) custom-call(s32[9,16,256]{2,1,0:T(8,128)S(1)} %collective-permute-do, ...), custom_call_target="tpu_custom_call", output_to_operand_aliasing={{0}: (3, {}), {1}: (4, {}), {2}: (5, {}), {3}: (6, {}), {4}... | custom-call | tf_op jit(solution)/shard_map/pallas_call | solution.py:619
  39.7 1.9 %collective-permute-start.5 = (f32[91,8,128]{2,1,0:T(8,128)S(1)}, f32[91,8,128]{2,1,0:T(8,128)S(1)}, u32[]{:S(2)}, u32[]{:S(2)}) collective-permute-start(f32[91,8,128]{2,1,0:T(8,128)S(1)} %get-tuple-element.74), channel_id=1, source_target_pairs={{0,1},{1,0},{2,3},{3,2},{4,5},{5,4},{6,7},{7,6},{8,9},{9,8},{10,11... | collective-permute-start | bytes 1118216 | tf_op jit(solution)/shard_map/ppermute | solution.py:709
  41.6 0.4 shard_map.60
  42.0 1.3 %collective-permute-done.5.recv = f32[91,8,128]{2,1,0:T(8,128)S(1)} collective-permute-done((f32[91,8,128]{2,1,0:T(8,128)S(1)}, f32[91,8,128]{2,1,0:T(8,128)S(1)}, u32[]{:S(2)}, u32[]{:S(2)}) %collective-permute-start.5) | collective-permute-done | bytes 372768 | tf_op jit(solution)/shard_map/ppermute | solution.py:709
  43.3 2.1 %shard_map.61 = (f32[110,8,128]{2,1,0:T(8,128)S(1)}, f32[2,10,16,128]{3,2,1,0:T(8,128)S(1)}, f32[110,8,128]{2,1,0:T(8,128)S(1)}, f32[110,8,128]{2,1,0:T(8,128)S(1)}, f32[8,48,256]{2,1,0:T(8,128)}) custom-call(f32[91,8,128]{2,1,0:T(8,128)S(1)} %collective-permute-done.5.recv, ...), custom_call_target="tpu_custom_call", output_to_operand_aliasing={{0}: (3, {}), {1}: (4, {}), {2}: (5, {}), {3}: (6, {})} | custom-call | tf_op jit(solution)/shard_map/pallas_call | solution.py:654
  (5 shorter events, 0.1 us)
Async XLA Ops:
  0.0 3.3 %collective-permute-start = (s32[6,8,256]{2,1,0:T(8,128)}, s32[6,8,256]{2,1,0:T(8,128)S(1)}, u32[]{:S(2)}, u32[]{:S(2)}) collective-permute-start(s32[6,8,256]{2,1,0:T(8,128)} %labels.1), channel_id=1, source_target_pairs={{0,1},{1,0},{2,3},{3,2},{4,5},{5,4},{6,7},{7,6},{8,9},{9,8},{10,11... | collective-permute-start | bytes 147464 | tf_op jit(solution)/shard_map/ppermute | solution.py:709
  3.3 18.3 %collective-permute-start.1 = (s32[6,16,256]{2,1,0:T(8,128)S(1)}, s32[6,16,256]{2,1,0:T(8,128)S(1)}, u32[]{:S(2)}, u32[]{:S(2)}) collective-permute-start(s32[6,16,256]{2,1,0:T(8,128)S(1)} %add_select_fusion.1.after), channel_id=1, source_target_pairs={{16,0},{32,16},{48,32},{64,48},{80,64},{96,80},{112,96},{128,112},... | collective-permute-start | bytes 294920 | tf_op jit(solution)/shard_map/ppermute | solution.py:702
  14.6 7.1 %collective-permute-start.2 = (s32[4,16,256]{2,1,0:T(8,128)S(1)}, s32[4,16,256]{2,1,0:T(8,128)S(1)}, u32[]{:S(2)}, u32[]{:S(2)}) collective-permute-start(s32[4,16,256]{2,1,0:T(8,128)S(1)} %slice_select_fusion), channel_id=1, source_target_pairs={{32,0},{48,16},{64,32},{80,48},{96,64},{112,80},{128,96},{144,112}... | collective-permute-start | bytes 196616 | tf_op jit(solution)/shard_map/ppermute | solution.py:702
  21.9 12.5 %collective-permute-start.4 = (s32[10,16,256]{2,1,0:T(8,128)S(1)}, s32[10,16,256]{2,1,0:T(8,128)S(1)}, u32[]{:S(2)}, u32[]{:S(2)}) collective-permute-start(s32[10,16,256]{2,1,0:T(8,128)S(1)} %slice.19), channel_id=1, source_target_pairs={{0,2},{1,3},{2,4},{3,5},{4,6},{5,7},{6,8},{7,9},{8,10},{9,11},{10,... | collective-permute-start | bytes 491528 | tf_op jit(solution)/shard_map/ppermute | solution.py:706
  24.5 12.0 %collective-permute-start.3 = (s32[9,16,256]{2,1,0:T(8,128)S(1)}, s32[9,16,256]{2,1,0:T(8,128)S(1)}, u32[]{:S(2)}, u32[]{:S(2)}) collective-permute-start(s32[9,16,256]{2,1,0:T(8,128)S(1)} %slice.18), channel_id=1, source_target_pairs={{2,0},{3,1},{4,2},{5,3},{6,4},{7,5},{8,6},{9,7},{10,8},{11,9},{12,... | collective-permute-start | bytes 442376 | tf_op jit(solution)/shard_map/ppermute | solution.py:706
  39.7 3.6 %collective-permute-start.5 = (f32[91,8,128]{2,1,0:T(8,128)S(1)}, f32[91,8,128]{2,1,0:T(8,128)S(1)}, u32[]{:S(2)}, u32[]{:S(2)}) collective-permute-start(f32[91,8,128]{2,1,0:T(8,128)S(1)} %get-tuple-element.74), channel_id=1, source_target_pairs={{0,1},{1,0},{2,3},{3,2},{4,5},{5,4},{6,7},{7,6},{8,9},{9,8},{10,11... | collective-permute-start | bytes 1118216 | tf_op jit(solution)/shard_map/ppermute | solution.py:709

commit v7 on v6

--- a/solution.py
+++ b/solution.py
@@ -55,6 +55,20 @@
     edge = (3.0 / 14.0) * (values + (1.0 / 3.0) * near)
     face = values + (3.0 / 14.0) * near
     return edge, face
+
+
+UPDATE_SCALE = 2.5 * 14.0 * DAMPING / 30.0
+
+
+def fine_diagonal(er, ei):
+    real = 128.0 / 30.0 - WAVE_SQUARED * (er + SHIFT_IMAG * ei)
+    imag = WAVE_SQUARED * (SHIFT_IMAG * er - ei)
+    return real, imag
+
+
+def scaled_inverse(real, imag, scale, keep):
+    ratio = jnp.where(keep, scale / (real * real + imag * imag), 0.0)
+    return real * ratio, -imag * ratio
 
 
 def where_am_i():
@@ -99,13 +113,13 @@
     lanes = lane_iota()
     rows = lax.broadcasted_iota(jnp.int32, (8, LANES), 0)
 
-    er = jnp.zeros((8, LANES), F32)
+    er = jnp.ones((8, LANES), F32)
     ei = jnp.zeros((8, LANES), F32)
     for m in range(MAT):
         er = jnp.where(lanes == m, splat(real[m]), er)
         ei = jnp.where(lanes == m, splat(imag[m]), ei)
-    for n, table in enumerate(material_tables(er, ei)):
-        tab[n : n + 1, :] = jnp.where(lanes < MAT, table, 0.0)[0:1]
+    tab[0:1, :] = er[0:1]
+    tab[1:2, :] = ei[0:1]
 
     incidence = jnp.zeros((8, LANES), F32)
     for c in range(4):
@@ -184,33 +198,39 @@
             for k in range(step):
                 y = first_row + n * step + k
                 y_in = jnp.logical_and(self.y0 + y >= 0, self.y0 + y < self.ny)
-                beyond = jnp.where(y_in, 0, OUTSIDE)
                 for h in range(2):
                     start = pl.multiple_of((n * step + k) * PX + 8 * h, 8)
                     part = self.apart[pl.ds(start, 8), :]
                     at = (y, pl.ds(8 * h, 8), slice(None))
-                    label = part[:, :LANES].astype(jnp.int32)
-                    index = jnp.where(inside[h], label, OUTSIDE) + beyond
-                    even = [self.pick(n, index) for n in range(4)]
-                    label = part[:, LANES:].astype(jnp.int32)
-                    index = jnp.where(inside[h], label, OUTSIDE) + beyond
-                    chosen = 4 + 2 * ((first_row + k) % 2)
-                    odd = [self.pick(n, index) for n in range(chosen)]
-                    halves = (even, odd)
-                    for (ir, ii, sr, si), (inv_r, inv_i, g_r, g_i) in (
-                        (even, (self.ie_r, self.ie_i, self.ge_r, self.ge_i)),
-                        (odd[:4], (self.io_r, self.io_i, self.go_r, self.go_i)),
+                    keep = jnp.logical_and(inside[h], y_in)
+                    sources = []
+                    for odd, (inv_r, inv_i, g_r, g_i) in enumerate(
+                        (
+                            (self.ie_r, self.ie_i, self.ge_r, self.ge_i),
+                            (self.io_r, self.io_i, self.go_r, self.go_i),
+                        )
                     ):
+                        label = part[:, odd * LANES : (odd + 1) * LANES].astype(jnp.int32)
+                        index = jnp.where(keep, label, OUTSIDE)
+                        er = self.pick(0, index)
+                        ei = self.pick(1, index)
+                        real, imag = fine_diagonal(er, ei)
+                        ir, ii = scaled_inverse(real, imag, UPDATE_SCALE, keep)
+                        sr, si = 1.2 * SOURCE_GAIN * (er - 1.0), 1.2 * SOURCE_GAIN * ei
                         inv_r[at] = ir
                         inv_i[at] = ii
                         g_r[at] = (4.0 / 14.0) * (ir * sr - ii * si)
                         g_i[at] = (4.0 / 14.0) * (ir * si + ii * sr)
-                    if chosen > 4:
-                        self.kr[at] = odd[4]
-                        self.ki[at] = odd[5]
+                        sources.append((sr, si))
+                        if odd and (first_row + k) % 2 == 1:
+                            kr, ki = scaled_inverse(
+                                real + (128.0 / 120.0 - 128.0 / 30.0), imag, DAMPING, keep
+                            )
+                            self.kr[at] = kr
+                            self.ki[at] = ki
                     for c, out in ((0, self.sa_r), (1, self.sa_i)):
-                        se = halves[0][2 + c]
-                        out[at] = (se + down(se, self.last) + 2.0 * halves[1][2 + c]) * (1.0 / 14.0)
+                        se = sources[0][c]
+                        out[at] = (se + down(se, self.last) + 2.0 * sources[1][c]) * (1.0 / 14.0)
             return carry
 
         lax.fori_loop(0, count // step, some, 0)
@@ -667,25 +687,6 @@
     return results[4]
 
 
-def complex_inverse(real, imag):
-    modulus = real * real + imag * imag
-    return real / modulus, -imag / modulus
-
-
-def material_tables(er, ei):
-    med_r = WAVE_SQUARED * (er + SHIFT_IMAG * ei)
-    med_i = WAVE_SQUARED * (ei - SHIFT_IMAG * er)
-    inv_r, inv_i = complex_inverse(128.0 / 30.0 - med_r, -med_i)
-    src_r = SOURCE_GAIN * (er - 1.0)
-    src_i = SOURCE_GAIN * ei
-    ci_r, ci_i = complex_inverse(128.0 / 120.0 - med_r, -med_i)
-    scale = 2.5 * 14.0 * DAMPING / 30.0
-    return (
-        scale * inv_r, scale * inv_i, 1.2 * src_r, 1.2 * src_i,
-        DAMPING * ci_r, DAMPING * ci_i,
-    )
-
-
 def body(labels, permittivity_real, permittivity_imag, angles, angle_pick):
     gx_n = lax.axis_size("gx")
     gy_n = lax.axis_size("gy")

time: 46 us -> 44.9 us (0.976)
  Pallas kernels: 14 us -> 12.9 us
    pallas_call x1, Pallas kernels: 3.84 us -> 2.94 us  [middle_call(): pl.pallas_call(kernel, out_shape=SHARED, in_specs=[SPEC] * 3, out_specs=(...]
  transfers between devices with their start and end apart: 6 -> 6, of which waited for: 3 -> 3; matrix products, arithmetic and copies ran while one was open for 0% -> 0% of each run, Pallas kernels for 19% -> 17%
where the time goes in v7:
time: 44.9 us; the launch traced here: 44.3 us
  starting transfers between devices  24.5 us (55%)
  Pallas kernels  12.9 us (29%)
  waiting for transfers between devices  6.4 us (14%)
    ppermute x2, starting transfers between devices, along_x(): return lax.ppermute(values, ('gx', 'gy'), pairs)  13.7 us
    ppermute x2, starting transfers between devices, along_y(): return lax.ppermute(values, 'gy', pairs)  7.05 us
    ppermute x2, waiting for transfers between devices, along_x(): return lax.ppermute(values, ('gx', 'gy'), pairs)  4.53 us
    ppermute x2, starting transfers between devices, core_swap(): return lax.ppermute(values, 'gy', [(j, j ^ 1) for j in range(gy_n)])  3.83 us
    pallas_call x1, Pallas kernels, high_call(): pl.pallas_call(kernel, out_shape=SHARED + (vmem(CX, CY, 8, LANES), vmem(2...  3.13 us
    pallas_call x1, Pallas kernels, middle_call(): pl.pallas_call(kernel, out_shape=SHARED, in_specs=[SPEC] * 3, out_specs=(...  2.94 us
    pallas_call x1, Pallas kernels, cycle_call(): pl.pallas_call(cycle_kernel, out_shape=HALF + (jax.ShapeDtypeStruct((8, O...  2.14 us
    pallas_call x1, Pallas kernels, low_call(): pl.pallas_call(kernel, out_shape=SHARED, in_specs=[SPEC] * 15, out_specs=...  1.9 us
  transfers between devices with their start and end apart: 6, of which 3 were waited for; matrix products, arithmetic and copies ran while one was open for 0% of the time, Pallas kernels for 17%

profile of v7, /device:TPU:38, one launch (start us, length us, event | category | flops | bytes accessed | tf_op | source)
XLA Modules:
  0.0 44.3 jit_solution(9745283341378743256)
XLA Ops:
  0.0 1.9 %collective-permute-start = (s32[6,8,256]{2,1,0:T(8,128)}, s32[6,8,256]{2,1,0:T(8,128)S(1)}, u32[]{:S(2)}, u32[]{:S(2)}) collective-permute-start(s32[6,8,256]{2,1,0:T(8,128)} %labels.1), channel_id=1, source_target_pairs={{0,1},{1,0},{2,3},{3,2},{4,5},{5,4},{6,7},{7,6},{8,9},{9,8},{10,11... | collective-permute-start | bytes 147464 | tf_op jit(solution)/shard_map/ppermute | solution.py:710
  1.9 0.8 %shard_map.55 = s32[6,8,256]{2,1,0:T(8,128)S(1)} custom-call(s32[6,8,256]{2,1,0:T(8,128)} %labels.1), custom_call_target="tpu_custom_call" | custom-call | tf_op jit(solution)/shard_map/pallas_call | solution.py:578
  2.8 0.6 %collective-permute-done = s32[6,8,256]{2,1,0:T(8,128)S(1)} collective-permute-done((s32[6,8,256]{2,1,0:T(8,128)}, s32[6,8,256]{2,1,0:T(8,128)S(1)}, u32[]{:S(2)}, u32[]{:S(2)}) %collective-permute-start) | collective-permute-done | bytes 49184 | tf_op jit(solution)/shard_map/ppermute | solution.py:710
  3.3 11.2 %collective-permute-start.1 = (s32[6,16,256]{2,1,0:T(8,128)S(1)}, s32[6,16,256]{2,1,0:T(8,128)S(1)}, u32[]{:S(2)}, u32[]{:S(2)}) collective-permute-start(s32[6,16,256]{2,1,0:T(8,128)S(1)} %add_select_fusion.1.after), channel_id=1, source_target_pairs={{16,0},{32,16},{48,32},{64,48},{80,64},{96,80},{112,96},{128,112},... | collective-permute-start | bytes 294920 | tf_op jit(solution)/shard_map/ppermute | solution.py:703
  14.6 2.5 %collective-permute-start.2 = (s32[4,16,256]{2,1,0:T(8,128)S(1)}, s32[4,16,256]{2,1,0:T(8,128)S(1)}, u32[]{:S(2)}, u32[]{:S(2)}) collective-permute-start(s32[4,16,256]{2,1,0:T(8,128)S(1)} %slice_select_fusion), channel_id=1, source_target_pairs={{32,0},{48,16},{64,32},{80,48},{96,64},{112,80},{128,96},{144,112}... | collective-permute-start | bytes 196616 | tf_op jit(solution)/shard_map/ppermute | solution.py:703
  17.0 0.1 copy.34
  17.1 4.5 %collective-permute-done.2 = s32[4,16,256]{2,1,0:T(8,128)S(1)} collective-permute-done((s32[4,16,256]{2,1,0:T(8,128)S(1)}, s32[4,16,256]{2,1,0:T(8,128)S(1)}, u32[]{:S(2)}, u32[]{:S(2)}) %collective-permute-start.2) | collective-permute-done | bytes 65568 | tf_op jit(solution)/shard_map/ppermute | solution.py:703
  21.7 0.0 collective-permute-done.1
  21.7 0.1 copy.35
  21.8 0.1 fusion.refs_0_
  21.9 2.6 %collective-permute-start.4 = (s32[10,16,256]{2,1,0:T(8,128)S(1)}, s32[10,16,256]{2,1,0:T(8,128)S(1)}, u32[]{:S(2)}, u32[]{:S(2)}) collective-permute-start(s32[10,16,256]{2,1,0:T(8,128)S(1)} %slice.19), channel_id=1, source_target_pairs={{0,2},{1,3},{2,4},{3,5},{4,6},{5,7},{6,8},{7,9},{8,10},{9,11},{10,... | collective-permute-start | bytes 491528 | tf_op jit(solution)/shard_map/ppermute | solution.py:707
  24.5 4.5 %collective-permute-start.3 = (s32[9,16,256]{2,1,0:T(8,128)S(1)}, s32[9,16,256]{2,1,0:T(8,128)S(1)}, u32[]{:S(2)}, u32[]{:S(2)}) collective-permute-start(s32[9,16,256]{2,1,0:T(8,128)S(1)} %slice.18), channel_id=1, source_target_pairs={{2,0},{3,1},{4,2},{5,3},{6,4},{7,5},{8,6},{9,7},{10,8},{11,9},{12,... | collective-permute-start | bytes 442376 | tf_op jit(solution)/shard_map/ppermute | solution.py:707
  29.0 1.6 %shard_map.56 = (f32[1120,8,128]{2,1,0:T(8,128)S(1)}, f32[8,128]{1,0:T(8,128)S(1)}) custom-call(f32[8]{0:T(128)} %real_in.1, f32[8]{0:T(128)} %imag_in.1, f32[360]{0:T(512)} %angles_in.1, s32[4]{0:T(128)} %picks_in.1, s32[6,16,256]{2,1,0:T(8,128)S(1)} %add_select_fusion.1.after), custom_call_target="tpu_custom_call" | custom-call | tf_op jit(solution)/shard_map/pallas_call | solution.py:590
  30.6 2.9 %shard_map.57 = (f32[35,16,128]{2,1,0:T(8,128)S(1)}, f32[35,16,128]{2,1,0:T(8,128)S(1)}, f32[35,16,128]{2,1,0:T(8,128)S(1)}, f32[35,16,128]{2,1,0:T(8,128)S(1)},...) custom-call(s32[16,16,256]{2,1,0:T(8,128)S(1)} %fusion.refs_0_, ...), custom_call_target="tpu_custom_call" | custom-call | tf_op jit(solution)/shard_map/pallas_call | solution.py:610
  33.5 0.0 collective-permute-done.4.refs_0_
  33.5 1.9 %shard_map.58 = (f32[35,16,128]{2,1,0:T(8,128)S(1)}, f32[35,16,128]{2,1,0:T(8,128)S(1)}, f32[35,16,128]{2,1,0:T(8,128)S(1)}, f32[35,16,128]{2,1,0:T(8,128)S(1)},...) custom-call(s32[10,16,256]{2,1,0:T(8,128)S(1)} %collective-permute-d, ...), custom_call_target="tpu_custom_call", output_to_operand_aliasing={{0}: (3, {}), {1}: (4, {}), {2}: (5, {}), {3}: (6, {}), {4}... | custom-call | tf_op jit(solution)/shard_map/pallas_call | solution.py:624
  35.4 0.0 collective-permute-done.3.refs_0_
  35.5 3.1 %shard_map.59 = (f32[35,16,128]{2,1,0:T(8,128)S(1)}, f32[35,16,128]{2,1,0:T(8,128)S(1)}, f32[35,16,128]{2,1,0:T(8,128)S(1)}, f32[35,16,128]{2,1,0:T(8,128)S(1)},...) custom-call(s32[9,16,256]{2,1,0:T(8,128)S(1)} %collective-permute-do, ...), custom_call_target="tpu_custom_call", output_to_operand_aliasing={{0}: (3, {}), {1}: (4, {}), {2}: (5, {}), {3}: (6, {}), {4}... | custom-call | tf_op jit(solution)/shard_map/pallas_call | solution.py:639
  38.6 1.9 %collective-permute-start.5 = (f32[91,8,128]{2,1,0:T(8,128)S(1)}, f32[91,8,128]{2,1,0:T(8,128)S(1)}, u32[]{:S(2)}, u32[]{:S(2)}) collective-permute-start(f32[91,8,128]{2,1,0:T(8,128)S(1)} %get-tuple-element.74), channel_id=1, source_target_pairs={{0,1},{1,0},{2,3},{3,2},{4,5},{5,4},{6,7},{7,6},{8,9},{9,8},{10,11... | collective-permute-start | bytes 1118216 | tf_op jit(solution)/shard_map/ppermute | solution.py:710
  40.5 0.4 shard_map.60
  40.9 1.3 %collective-permute-done.5.recv = f32[91,8,128]{2,1,0:T(8,128)S(1)} collective-permute-done((f32[91,8,128]{2,1,0:T(8,128)S(1)}, f32[91,8,128]{2,1,0:T(8,128)S(1)}, u32[]{:S(2)}, u32[]{:S(2)}) %collective-permute-start.5) | collective-permute-done | bytes 372768 | tf_op jit(solution)/shard_map/ppermute | solution.py:710
  42.2 2.1 %shard_map.61 = (f32[110,8,128]{2,1,0:T(8,128)S(1)}, f32[2,10,16,128]{3,2,1,0:T(8,128)S(1)}, f32[110,8,128]{2,1,0:T(8,128)S(1)}, f32[110,8,128]{2,1,0:T(8,128)S(1)}, f32[8,48,256]{2,1,0:T(8,128)}) custom-call(f32[91,8,128]{2,1,0:T(8,128)S(1)} %collective-permute-done.5.recv, ...), custom_call_target="tpu_custom_call", output_to_operand_aliasing={{0}: (3, {}), {1}: (4, {}), {2}: (5, {}), {3}: (6, {})} | custom-call | tf_op jit(solution)/shard_map/pallas_call | solution.py:674
  (5 shorter events, 0.1 us)
Async XLA Ops:
  0.0 3.3 %collective-permute-start = (s32[6,8,256]{2,1,0:T(8,128)}, s32[6,8,256]{2,1,0:T(8,128)S(1)}, u32[]{:S(2)}, u32[]{:S(2)}) collective-permute-start(s32[6,8,256]{2,1,0:T(8,128)} %labels.1), channel_id=1, source_target_pairs={{0,1},{1,0},{2,3},{3,2},{4,5},{5,4},{6,7},{7,6},{8,9},{9,8},{10,11... | collective-permute-start | bytes 147464 | tf_op jit(solution)/shard_map/ppermute | solution.py:710
  3.3 18.3 %collective-permute-start.1 = (s32[6,16,256]{2,1,0:T(8,128)S(1)}, s32[6,16,256]{2,1,0:T(8,128)S(1)}, u32[]{:S(2)}, u32[]{:S(2)}) collective-permute-start(s32[6,16,256]{2,1,0:T(8,128)S(1)} %add_select_fusion.1.after), channel_id=1, source_target_pairs={{16,0},{32,16},{48,32},{64,48},{80,64},{96,80},{112,96},{128,112},... | collective-permute-start | bytes 294920 | tf_op jit(solution)/shard_map/ppermute | solution.py:703
  14.6 7.1 %collective-permute-start.2 = (s32[4,16,256]{2,1,0:T(8,128)S(1)}, s32[4,16,256]{2,1,0:T(8,128)S(1)}, u32[]{:S(2)}, u32[]{:S(2)}) collective-permute-start(s32[4,16,256]{2,1,0:T(8,128)S(1)} %slice_select_fusion), channel_id=1, source_target_pairs={{32,0},{48,16},{64,32},{80,48},{96,64},{112,80},{128,96},{144,112}... | collective-permute-start | bytes 196616 | tf_op jit(solution)/shard_map/ppermute | solution.py:703
  21.9 11.6 %collective-permute-start.4 = (s32[10,16,256]{2,1,0:T(8,128)S(1)}, s32[10,16,256]{2,1,0:T(8,128)S(1)}, u32[]{:S(2)}, u32[]{:S(2)}) collective-permute-start(s32[10,16,256]{2,1,0:T(8,128)S(1)} %slice.19), channel_id=1, source_target_pairs={{0,2},{1,3},{2,4},{3,5},{4,6},{5,7},{6,8},{7,9},{8,10},{9,11},{10,... | collective-permute-start | bytes 491528 | tf_op jit(solution)/shard_map/ppermute | solution.py:707
  24.5 10.9 %collective-permute-start.3 = (s32[9,16,256]{2,1,0:T(8,128)S(1)}, s32[9,16,256]{2,1,0:T(8,128)S(1)}, u32[]{:S(2)}, u32[]{:S(2)}) collective-permute-start(s32[9,16,256]{2,1,0:T(8,128)S(1)} %slice.18), channel_id=1, source_target_pairs={{2,0},{3,1},{4,2},{5,3},{6,4},{7,5},{8,6},{9,7},{10,8},{11,9},{12,... | collective-permute-start | bytes 442376 | tf_op jit(solution)/shard_map/ppermute | solution.py:707
  38.6 3.6 %collective-permute-start.5 = (f32[91,8,128]{2,1,0:T(8,128)S(1)}, f32[91,8,128]{2,1,0:T(8,128)S(1)}, u32[]{:S(2)}, u32[]{:S(2)}) collective-permute-start(f32[91,8,128]{2,1,0:T(8,128)S(1)} %get-tuple-element.74), channel_id=1, source_target_pairs={{0,1},{1,0},{2,3},{3,2},{4,5},{5,4},{6,7},{7,6},{8,9},{9,8},{10,11... | collective-permute-start | bytes 1118216 | tf_op jit(solution)/shard_map/ppermute | solution.py:710

commit v8 on v7

--- a/solution.py
+++ b/solution.py
@@ -19,6 +19,7 @@
 PY = 35
 LOW = 10
 CX, CY = 5, 15
+EARLY = 10
 NI, NJ = 10, 11
 LANES = 128
 F32 = jnp.float32
@@ -332,15 +333,20 @@
 
 
 def low_kernel(sizes, labels, tab, wave, *refs):
-    region = Region(sizes, tab, wave, refs[12:24], refs[24:])
+    region = Region(sizes, tab, wave, refs[12:24], refs[26:])
+    c1_out, ck_out = refs[24:26]
     region.tables(labels, 0, LOW, LOW)
     row_loop(0, LOW, 5, region.first_stage)
     row_loop(1, LOW, 5, region.second_stage)
+    for k in range(2):
+        for i in range(CX):
+            ck_out[k, i, 8:16, :] = jnp.zeros((8, LANES), F32)
+    row_loop(0, EARLY, 1, lambda j: region.third_stage(j, c1_out, ck_out))
 
 
 def high_kernel(sizes, labels, tab, wave, *refs):
-    region = Region(sizes, tab, wave, refs[12:24], refs[27:])
-    c1_out, ck_out, send_out = refs[24:27]
+    region = Region(sizes, tab, wave, refs[14:26], refs[29:])
+    c1_out, ck_out, send_out = refs[26:29]
     core, y0, ny = region.core, region.y0, region.ny
     it1 = region.it1
     top = LOW + 2 * OWN_Y
@@ -354,10 +360,7 @@
             for ref in (region.va, region.vb):
                 ref[(top + 1) * PX + x] = -ref[(top - 1) * PX + x]
 
-    for k in range(2):
-        for i in range(CX):
-            ck_out[k, i, 8:16, :] = jnp.zeros((8, LANES), F32)
-    row_loop(0, CY, 1, lambda j: region.third_stage(j, c1_out, ck_out))
+    row_loop(EARLY, CY - EARLY, 1, lambda j: region.third_stage(j, c1_out, ck_out))
 
     j0 = 4 - 4 * core
     for i in range(CX):
@@ -563,6 +566,7 @@
 SHARED = (vmem(PY, PX, LANES),) * 6 + (vmem(CELLS * 2, 8, LANES),) * 3 + (
     vmem(CELLS, 8, LANES),
 ) * 3
+COARSE = (vmem(CX, CY, 8, LANES), vmem(2, CX, 16, LANES))
 TABLES = [vmem(PY, PX, LANES)] * 6
 
 
@@ -623,9 +627,9 @@
 
     return pl.pallas_call(
         kernel,
-        out_shape=SHARED,
+        out_shape=SHARED + COARSE,
         in_specs=[SPEC] * 15,
-        out_specs=(SPEC,) * 12,
+        out_specs=(SPEC,) * 14,
         input_output_aliases={3 + n: n for n in range(12)},
         scratch_shapes=TABLES + [vmem(LOW * PX, 2 * LANES)],
         compiler_params=limit(6),
@@ -638,15 +642,10 @@
 
     results = pl.pallas_call(
         kernel,
-        out_shape=SHARED
-        + (
-            vmem(CX, CY, 8, LANES),
-            vmem(2, CX, 16, LANES),
-            vmem(SEND, 8, LANES),
-        ),
-        in_specs=[SPEC] * 15,
+        out_shape=SHARED + COARSE + (vmem(SEND, 8, LANES),),
+        in_specs=[SPEC] * 17,
         out_specs=(SPEC,) * 15,
-        input_output_aliases={3 + n: n for n in range(12)},
+        input_output_aliases={3 + n: n for n in range(14)},
         scratch_shapes=TABLES + [vmem(LOW * PX, 2 * LANES)],
         compiler_params=limit(6),
     )(*near_core(labels, tab, wave), *shared)

time: 44.9 us -> 44.9 us (level)
  transfers between devices with their start and end apart: 6 -> 6, of which waited for: 3 -> 3; matrix products, arithmetic and copies ran while one was open for 0% -> 0% of each run, Pallas kernels for 17% -> 19%
where the time goes in v8:
time: 44.9 us; the launch traced here: 44.3 us
  starting transfers between devices  24.5 us (55%)
  Pallas kernels  12.9 us (29%)
  waiting for transfers between devices  6.4 us (14%)
    ppermute x2, starting transfers between devices, along_x(): return lax.ppermute(values, ('gx', 'gy'), pairs)  13.7 us
    ppermute x2, starting transfers between devices, along_y(): return lax.ppermute(values, 'gy', pairs)  7.05 us
    ppermute x2, waiting for transfers between devices, along_x(): return lax.ppermute(values, ('gx', 'gy'), pairs)  4.53 us
    ppermute x2, starting transfers between devices, core_swap(): return lax.ppermute(values, 'gy', [(j, j ^ 1) for j in range(gy_n)])  3.83 us
    pallas_call x1, Pallas kernels, middle_call(): pl.pallas_call(kernel, out_shape=SHARED, in_specs=[SPEC] * 3, out_specs=(...  2.94 us
    pallas_call x1, Pallas kernels, low_call(): pl.pallas_call(kernel, out_shape=SHARED + COARSE, in_specs=[SPEC] * 15, o...  2.67 us
    pallas_call x1, Pallas kernels, high_call(): pl.pallas_call(kernel, out_shape=SHARED + COARSE + (vmem(SEND, 8, LANES),...  2.36 us
    pallas_call x1, Pallas kernels, cycle_call(): pl.pallas_call(cycle_kernel, out_shape=HALF + (jax.ShapeDtypeStruct((8, O...  2.14 us
  transfers between devices with their start and end apart: 6, of which 3 were waited for; matrix products, arithmetic and copies ran while one was open for 0% of the time, Pallas kernels for 19%

profile of v8, /device:TPU:38, one launch (start us, length us, event | category | flops | bytes accessed | tf_op | source)
XLA Modules:
  0.0 44.3 jit_solution(7022921647418469187)
XLA Ops:
  0.0 1.9 %collective-permute-start = (s32[6,8,256]{2,1,0:T(8,128)}, s32[6,8,256]{2,1,0:T(8,128)S(1)}, u32[]{:S(2)}, u32[]{:S(2)}) collective-permute-start(s32[6,8,256]{2,1,0:T(8,128)} %labels.1), channel_id=1, source_target_pairs={{0,1},{1,0},{2,3},{3,2},{4,5},{5,4},{6,7},{7,6},{8,9},{9,8},{10,11... | collective-permute-start | bytes 147464 | tf_op jit(solution)/shard_map/ppermute | solution.py:709
  1.9 0.8 %shard_map.55 = s32[6,8,256]{2,1,0:T(8,128)S(1)} custom-call(s32[6,8,256]{2,1,0:T(8,128)} %labels.1), custom_call_target="tpu_custom_call" | custom-call | tf_op jit(solution)/shard_map/pallas_call | solution.py:582
  2.8 0.6 %collective-permute-done = s32[6,8,256]{2,1,0:T(8,128)S(1)} collective-permute-done((s32[6,8,256]{2,1,0:T(8,128)}, s32[6,8,256]{2,1,0:T(8,128)S(1)}, u32[]{:S(2)}, u32[]{:S(2)}) %collective-permute-start) | collective-permute-done | bytes 49184 | tf_op jit(solution)/shard_map/ppermute | solution.py:709
  3.3 11.2 %collective-permute-start.1 = (s32[6,16,256]{2,1,0:T(8,128)S(1)}, s32[6,16,256]{2,1,0:T(8,128)S(1)}, u32[]{:S(2)}, u32[]{:S(2)}) collective-permute-start(s32[6,16,256]{2,1,0:T(8,128)S(1)} %add_select_fusion.1.after), channel_id=1, source_target_pairs={{16,0},{32,16},{48,32},{64,48},{80,64},{96,80},{112,96},{128,112},... | collective-permute-start | bytes 294920 | tf_op jit(solution)/shard_map/ppermute | solution.py:702
  14.6 2.5 %collective-permute-start.2 = (s32[4,16,256]{2,1,0:T(8,128)S(1)}, s32[4,16,256]{2,1,0:T(8,128)S(1)}, u32[]{:S(2)}, u32[]{:S(2)}) collective-permute-start(s32[4,16,256]{2,1,0:T(8,128)S(1)} %slice_select_fusion), channel_id=1, source_target_pairs={{32,0},{48,16},{64,32},{80,48},{96,64},{112,80},{128,96},{144,112}... | collective-permute-start | bytes 196616 | tf_op jit(solution)/shard_map/ppermute | solution.py:702
  17.0 0.1 copy.36
  17.1 4.5 %collective-permute-done.2 = s32[4,16,256]{2,1,0:T(8,128)S(1)} collective-permute-done((s32[4,16,256]{2,1,0:T(8,128)S(1)}, s32[4,16,256]{2,1,0:T(8,128)S(1)}, u32[]{:S(2)}, u32[]{:S(2)}) %collective-permute-start.2) | collective-permute-done | bytes 65568 | tf_op jit(solution)/shard_map/ppermute | solution.py:702
  21.7 0.0 collective-permute-done.1
  21.7 0.1 copy.37
  21.8 0.1 fusion.refs_0_
  21.9 2.6 %collective-permute-start.4 = (s32[10,16,256]{2,1,0:T(8,128)S(1)}, s32[10,16,256]{2,1,0:T(8,128)S(1)}, u32[]{:S(2)}, u32[]{:S(2)}) collective-permute-start(s32[10,16,256]{2,1,0:T(8,128)S(1)} %slice.19), channel_id=1, source_target_pairs={{0,2},{1,3},{2,4},{3,5},{4,6},{5,7},{6,8},{7,9},{8,10},{9,11},{10,... | collective-permute-start | bytes 491528 | tf_op jit(solution)/shard_map/ppermute | solution.py:706
  24.5 4.5 %collective-permute-start.3 = (s32[9,16,256]{2,1,0:T(8,128)S(1)}, s32[9,16,256]{2,1,0:T(8,128)S(1)}, u32[]{:S(2)}, u32[]{:S(2)}) collective-permute-start(s32[9,16,256]{2,1,0:T(8,128)S(1)} %slice.18), channel_id=1, source_target_pairs={{2,0},{3,1},{4,2},{5,3},{6,4},{7,5},{8,6},{9,7},{10,8},{11,9},{12,... | collective-permute-start | bytes 442376 | tf_op jit(solution)/shard_map/ppermute | solution.py:706
  29.0 1.6 %shard_map.56 = (f32[1120,8,128]{2,1,0:T(8,128)S(1)}, f32[8,128]{1,0:T(8,128)S(1)}) custom-call(f32[8]{0:T(128)} %real_in.1, f32[8]{0:T(128)} %imag_in.1, f32[360]{0:T(512)} %angles_in.1, s32[4]{0:T(128)} %picks_in.1, s32[6,16,256]{2,1,0:T(8,128)S(1)} %add_select_fusion.1.after), custom_call_target="tpu_custom_call" | custom-call | tf_op jit(solution)/shard_map/pallas_call | solution.py:594
  30.6 2.9 %shard_map.57 = (f32[35,16,128]{2,1,0:T(8,128)S(1)}, f32[35,16,128]{2,1,0:T(8,128)S(1)}, f32[35,16,128]{2,1,0:T(8,128)S(1)}, f32[35,16,128]{2,1,0:T(8,128)S(1)},...) custom-call(s32[16,16,256]{2,1,0:T(8,128)S(1)} %fusion.refs_0_, ...), custom_call_target="tpu_custom_call" | custom-call | tf_op jit(solution)/shard_map/pallas_call | solution.py:614
  33.5 0.0 collective-permute-done.4.refs_0_
  33.5 2.7 %shard_map.58 = (f32[35,16,128]{2,1,0:T(8,128)S(1)}, f32[35,16,128]{2,1,0:T(8,128)S(1)}, f32[35,16,128]{2,1,0:T(8,128)S(1)}, f32[35,16,128]{2,1,0:T(8,128)S(1)},...) custom-call(s32[10,16,256]{2,1,0:T(8,128)S(1)} %collective-permute-d, ...), custom_call_target="tpu_custom_call", output_to_operand_aliasing={{0}: (3, {}), {1}: (4, {}), {2}: (5, {}), {3}: (6, {}), {4}... | custom-call | tf_op jit(solution)/shard_map/pallas_call | solution.py:628
  36.2 0.0 collective-permute-done.3.refs_0_
  36.2 2.4 %shard_map.59 = (f32[35,16,128]{2,1,0:T(8,128)S(1)}, f32[35,16,128]{2,1,0:T(8,128)S(1)}, f32[35,16,128]{2,1,0:T(8,128)S(1)}, f32[35,16,128]{2,1,0:T(8,128)S(1)},...) custom-call(s32[9,16,256]{2,1,0:T(8,128)S(1)} %collective-permute-do, ...), custom_call_target="tpu_custom_call", output_to_operand_aliasing={{0}: (3, {}), {1}: (4, {}), {2}: (5, {}), {3}: (6, {}), {4}... | custom-call | tf_op jit(solution)/shard_map/pallas_call | solution.py:643
  38.6 1.9 %collective-permute-start.5 = (f32[91,8,128]{2,1,0:T(8,128)S(1)}, f32[91,8,128]{2,1,0:T(8,128)S(1)}, u32[]{:S(2)}, u32[]{:S(2)}) collective-permute-start(f32[91,8,128]{2,1,0:T(8,128)S(1)} %get-tuple-element.78), channel_id=1, source_target_pairs={{0,1},{1,0},{2,3},{3,2},{4,5},{5,4},{6,7},{7,6},{8,9},{9,8},{10,11... | collective-permute-start | bytes 1118216 | tf_op jit(solution)/shard_map/ppermute | solution.py:709
  40.5 0.4 shard_map.60
  40.9 1.3 %collective-permute-done.5.recv = f32[91,8,128]{2,1,0:T(8,128)S(1)} collective-permute-done((f32[91,8,128]{2,1,0:T(8,128)S(1)}, f32[91,8,128]{2,1,0:T(8,128)S(1)}, u32[]{:S(2)}, u32[]{:S(2)}) %collective-permute-start.5) | collective-permute-done | bytes 372768 | tf_op jit(solution)/shard_map/ppermute | solution.py:709
  42.2 2.1 %shard_map.61 = (f32[110,8,128]{2,1,0:T(8,128)S(1)}, f32[2,10,16,128]{3,2,1,0:T(8,128)S(1)}, f32[110,8,128]{2,1,0:T(8,128)S(1)}, f32[110,8,128]{2,1,0:T(8,128)S(1)}, f32[8,48,256]{2,1,0:T(8,128)}) custom-call(f32[91,8,128]{2,1,0:T(8,128)S(1)} %collective-permute-done.5.recv, ...), custom_call_target="tpu_custom_call", output_to_operand_aliasing={{0}: (3, {}), {1}: (4, {}), {2}: (5, {}), {3}: (6, {})} | custom-call | tf_op jit(solution)/shard_map/pallas_call | solution.py:673
  (5 shorter events, 0.1 us)
Async XLA Ops:
  0.0 3.3 %collective-permute-start = (s32[6,8,256]{2,1,0:T(8,128)}, s32[6,8,256]{2,1,0:T(8,128)S(1)}, u32[]{:S(2)}, u32[]{:S(2)}) collective-permute-start(s32[6,8,256]{2,1,0:T(8,128)} %labels.1), channel_id=1, source_target_pairs={{0,1},{1,0},{2,3},{3,2},{4,5},{5,4},{6,7},{7,6},{8,9},{9,8},{10,11... | collective-permute-start | bytes 147464 | tf_op jit(solution)/shard_map/ppermute | solution.py:709
  3.3 18.3 %collective-permute-start.1 = (s32[6,16,256]{2,1,0:T(8,128)S(1)}, s32[6,16,256]{2,1,0:T(8,128)S(1)}, u32[]{:S(2)}, u32[]{:S(2)}) collective-permute-start(s32[6,16,256]{2,1,0:T(8,128)S(1)} %add_select_fusion.1.after), channel_id=1, source_target_pairs={{16,0},{32,16},{48,32},{64,48},{80,64},{96,80},{112,96},{128,112},... | collective-permute-start | bytes 294920 | tf_op jit(solution)/shard_map/ppermute | solution.py:702
  14.6 7.1 %collective-permute-start.2 = (s32[4,16,256]{2,1,0:T(8,128)S(1)}, s32[4,16,256]{2,1,0:T(8,128)S(1)}, u32[]{:S(2)}, u32[]{:S(2)}) collective-permute-start(s32[4,16,256]{2,1,0:T(8,128)S(1)} %slice_select_fusion), channel_id=1, source_target_pairs={{32,0},{48,16},{64,32},{80,48},{96,64},{112,80},{128,96},{144,112}... | collective-permute-start | bytes 196616 | tf_op jit(solution)/shard_map/ppermute | solution.py:702
  21.9 11.6 %collective-permute-start.4 = (s32[10,16,256]{2,1,0:T(8,128)S(1)}, s32[10,16,256]{2,1,0:T(8,128)S(1)}, u32[]{:S(2)}, u32[]{:S(2)}) collective-permute-start(s32[10,16,256]{2,1,0:T(8,128)S(1)} %slice.19), channel_id=1, source_target_pairs={{0,2},{1,3},{2,4},{3,5},{4,6},{5,7},{6,8},{7,9},{8,10},{9,11},{10,... | collective-permute-start | bytes 491528 | tf_op jit(solution)/shard_map/ppermute | solution.py:706
  24.5 11.7 %collective-permute-start.3 = (s32[9,16,256]{2,1,0:T(8,128)S(1)}, s32[9,16,256]{2,1,0:T(8,128)S(1)}, u32[]{:S(2)}, u32[]{:S(2)}) collective-permute-start(s32[9,16,256]{2,1,0:T(8,128)S(1)} %slice.18), channel_id=1, source_target_pairs={{2,0},{3,1},{4,2},{5,3},{6,4},{7,5},{8,6},{9,7},{10,8},{11,9},{12,... | collective-permute-start | bytes 442376 | tf_op jit(solution)/shard_map/ppermute | solution.py:706
  38.6 3.6 %collective-permute-start.5 = (f32[91,8,128]{2,1,0:T(8,128)S(1)}, f32[91,8,128]{2,1,0:T(8,128)S(1)}, u32[]{:S(2)}, u32[]{:S(2)}) collective-permute-start(f32[91,8,128]{2,1,0:T(8,128)S(1)} %get-tuple-element.78), channel_id=1, source_target_pairs={{0,1},{1,0},{2,3},{3,2},{4,5},{5,4},{6,7},{7,6},{8,9},{9,8},{10,11... | collective-permute-start | bytes 1118216 | tf_op jit(solution)/shard_map/ppermute | solution.py:709

commit v9 on v8

--- a/solution.py
+++ b/solution.py
@@ -694,11 +694,10 @@
 
     def along_x(values, by):
         pairs = []
-        for j in range(gy_n):
-            step = by if j % 2 == 0 else -by
-            for i in range(gx_n):
-                if 0 <= i + step < gx_n:
-                    pairs.append(((i + step) * gy_n + j, i * gy_n + j))
+        for j in range(0, gy_n, 2):
+            for i in range(gx_n - by):
+                here, there = i * gy_n + j, (i + by) * gy_n + j + 1
+                pairs += [(here, there), (there, here)]
         return lax.ppermute(values, ("gx", "gy"), pairs)
 
     def along_y(values, by):
@@ -716,7 +715,7 @@
         jnp.concatenate([other, labels], axis=1),
     )
     both = with_layout_constraint(both, Layout((0, 1, 2)))
-    far = along_x(jnp.where(is_low, both[:4], both[2:]), 2)
+    far = along_x(jnp.where(is_low, both[2:], both[:4]), 2)
     near = along_x(both, 1)
     near = with_layout_constraint(near, Layout((0, 1, 2)))
     far = with_layout_constraint(far, Layout((0, 1, 2)))

time: 44.9 us -> 45.9 us (1.022)
  starting transfers between devices: 24.5 us -> 27.5 us
  waiting for transfers between devices: 6.4 us -> 4.18 us
    ppermute x2, starting transfers between devices: 3.83 us -> 12.7 us  [core_swap(): return lax.ppermute(values, 'gy', [(j, j ^ 1) for j in range(gy_n)])]
    ppermute x2, starting transfers between devices: 13.7 us -> 7.77 us  [along_x(): return lax.ppermute(values, ('gx', 'gy'), pairs)]
    ppermute x2, waiting for transfers between devices: 4.53 us -> 2.68 us  [along_x(): return lax.ppermute(values, ('gx', 'gy'), pairs)]
where the time goes in v9:
time: 45.9 us; the launch traced here: 45 us
  starting transfers between devices  27.5 us (60%)
  Pallas kernels  12.9 us (28%)
  waiting for transfers between devices  4.18 us (9%)
    ppermute x2, starting transfers between devices, core_swap(): return lax.ppermute(values, 'gy', [(j, j ^ 1) for j in range(gy_n)])  12.7 us
    ppermute x2, starting transfers between devices, along_x(): return lax.ppermute(values, ('gx', 'gy'), pairs)  7.77 us
    ppermute x2, starting transfers between devices, along_y(): return lax.ppermute(values, 'gy', pairs)  7.05 us
    pallas_call x1, Pallas kernels, middle_call(): pl.pallas_call(kernel, out_shape=SHARED, in_specs=[SPEC] * 3, out_specs=(...  2.94 us
    ppermute x2, waiting for transfers between devices, along_x(): return lax.ppermute(values, ('gx', 'gy'), pairs)  2.68 us
    pallas_call x1, Pallas kernels, low_call(): pl.pallas_call(kernel, out_shape=SHARED + COARSE, in_specs=[SPEC] * 15, o...  2.67 us
    pallas_call x1, Pallas kernels, high_call(): pl.pallas_call(kernel, out_shape=SHARED + COARSE + (vmem(SEND, 8, LANES),...  2.36 us
    pallas_call x1, Pallas kernels, cycle_call(): pl.pallas_call(cycle_kernel, out_shape=HALF + (jax.ShapeDtypeStruct((8, O...  2.14 us
  transfers between devices with their start and end apart: 6, of which 3 were waited for; matrix products, arithmetic and copies ran while one was open for 0% of the time, Pallas kernels for 19%

profile of v9, /device:TPU:38, one launch (start us, length us, event | category | flops | bytes accessed | tf_op | source)
XLA Modules:
  0.0 45.0 jit_solution(8654789232429667008)
XLA Ops:
  0.0 1.9 %collective-permute-start = (s32[6,8,256]{2,1,0:T(8,128)}, s32[6,8,256]{2,1,0:T(8,128)S(1)}, u32[]{:S(2)}, u32[]{:S(2)}) collective-permute-start(s32[6,8,256]{2,1,0:T(8,128)} %labels.1), channel_id=1, source_target_pairs={{0,1},{1,0},{2,3},{3,2},{4,5},{5,4},{6,7},{7,6},{8,9},{9,8},{10,11... | collective-permute-start | bytes 147464 | tf_op jit(solution)/shard_map/ppermute | solution.py:708
  1.9 0.8 %shard_map.55 = s32[6,8,256]{2,1,0:T(8,128)S(1)} custom-call(s32[6,8,256]{2,1,0:T(8,128)} %labels.1), custom_call_target="tpu_custom_call" | custom-call | tf_op jit(solution)/shard_map/pallas_call | solution.py:582
  2.8 0.6 %collective-permute-done = s32[6,8,256]{2,1,0:T(8,128)S(1)} collective-permute-done((s32[6,8,256]{2,1,0:T(8,128)}, s32[6,8,256]{2,1,0:T(8,128)S(1)}, u32[]{:S(2)}, u32[]{:S(2)}) %collective-permute-start) | collective-permute-done | bytes 49184 | tf_op jit(solution)/shard_map/ppermute | solution.py:708
  3.3 4.0 %collective-permute-start.1 = (s32[6,16,256]{2,1,0:T(8,128)S(1)}, s32[6,16,256]{2,1,0:T(8,128)S(1)}, u32[]{:S(2)}, u32[]{:S(2)}) collective-permute-start(s32[6,16,256]{2,1,0:T(8,128)S(1)} %add_select_fusion.1.after), channel_id=1, source_target_pairs={{0,17},{17,0},{16,33},{33,16},{32,49},{49,32},{48,65},{65,48},{64,... | collective-permute-start | bytes 294920 | tf_op jit(solution)/shard_map/ppermute | solution.py:701
  7.4 3.7 %collective-permute-start.2 = (s32[4,16,256]{2,1,0:T(8,128)S(1)}, s32[4,16,256]{2,1,0:T(8,128)S(1)}, u32[]{:S(2)}, u32[]{:S(2)}) collective-permute-start(s32[4,16,256]{2,1,0:T(8,128)S(1)} %slice_select_fusion), channel_id=1, source_target_pairs={{0,33},{33,0},{16,49},{49,16},{32,65},{65,32},{48,81},{81,48},{64,... | collective-permute-start | bytes 196616 | tf_op jit(solution)/shard_map/ppermute | solution.py:701
  11.1 0.1 copy.36
  11.2 2.7 %collective-permute-done.2 = s32[4,16,256]{2,1,0:T(8,128)S(1)} collective-permute-done((s32[4,16,256]{2,1,0:T(8,128)S(1)}, s32[4,16,256]{2,1,0:T(8,128)S(1)}, u32[]{:S(2)}, u32[]{:S(2)}) %collective-permute-start.2) | collective-permute-done | bytes 65568 | tf_op jit(solution)/shard_map/ppermute | solution.py:701
  13.9 0.0 collective-permute-done.1
  13.9 0.1 copy.37
  14.0 0.1 fusion.refs_0_
  14.1 2.6 %collective-permute-start.4 = (s32[10,16,256]{2,1,0:T(8,128)S(1)}, s32[10,16,256]{2,1,0:T(8,128)S(1)}, u32[]{:S(2)}, u32[]{:S(2)}) collective-permute-start(s32[10,16,256]{2,1,0:T(8,128)S(1)} %slice.19), channel_id=1, source_target_pairs={{0,2},{1,3},{2,4},{3,5},{4,6},{5,7},{6,8},{7,9},{8,10},{9,11},{10,... | collective-permute-start | bytes 491528 | tf_op jit(solution)/shard_map/ppermute | solution.py:705
  16.8 4.5 %collective-permute-start.3 = (s32[9,16,256]{2,1,0:T(8,128)S(1)}, s32[9,16,256]{2,1,0:T(8,128)S(1)}, u32[]{:S(2)}, u32[]{:S(2)}) collective-permute-start(s32[9,16,256]{2,1,0:T(8,128)S(1)} %slice.18), channel_id=1, source_target_pairs={{2,0},{3,1},{4,2},{5,3},{6,4},{7,5},{8,6},{9,7},{10,8},{11,9},{12,... | collective-permute-start | bytes 442376 | tf_op jit(solution)/shard_map/ppermute | solution.py:705
  21.2 1.6 %shard_map.56 = (f32[1120,8,128]{2,1,0:T(8,128)S(1)}, f32[8,128]{1,0:T(8,128)S(1)}) custom-call(f32[8]{0:T(128)} %real_in.1, f32[8]{0:T(128)} %imag_in.1, f32[360]{0:T(512)} %angles_in.1, s32[4]{0:T(128)} %picks_in.1, s32[6,16,256]{2,1,0:T(8,128)S(1)} %add_select_fusion.1.after), custom_call_target="tpu_custom_call" | custom-call | tf_op jit(solution)/shard_map/pallas_call | solution.py:594
  22.8 2.9 %shard_map.57 = (f32[35,16,128]{2,1,0:T(8,128)S(1)}, f32[35,16,128]{2,1,0:T(8,128)S(1)}, f32[35,16,128]{2,1,0:T(8,128)S(1)}, f32[35,16,128]{2,1,0:T(8,128)S(1)},...) custom-call(s32[16,16,256]{2,1,0:T(8,128)S(1)} %fusion.refs_0_, ...), custom_call_target="tpu_custom_call" | custom-call | tf_op jit(solution)/shard_map/pallas_call | solution.py:614
  25.8 0.0 collective-permute-done.4.refs_0_
  25.8 2.7 %shard_map.58 = (f32[35,16,128]{2,1,0:T(8,128)S(1)}, f32[35,16,128]{2,1,0:T(8,128)S(1)}, f32[35,16,128]{2,1,0:T(8,128)S(1)}, f32[35,16,128]{2,1,0:T(8,128)S(1)},...) custom-call(s32[10,16,256]{2,1,0:T(8,128)S(1)} %collective-permute-d, ...), custom_call_target="tpu_custom_call", output_to_operand_aliasing={{0}: (3, {}), {1}: (4, {}), {2}: (5, {}), {3}: (6, {}), {4}... | custom-call | tf_op jit(solution)/shard_map/pallas_call | solution.py:628
  28.5 0.0 collective-permute-done.3.refs_0_
  28.5 2.4 %shard_map.59 = (f32[35,16,128]{2,1,0:T(8,128)S(1)}, f32[35,16,128]{2,1,0:T(8,128)S(1)}, f32[35,16,128]{2,1,0:T(8,128)S(1)}, f32[35,16,128]{2,1,0:T(8,128)S(1)},...) custom-call(s32[9,16,256]{2,1,0:T(8,128)S(1)} %collective-permute-do, ...), custom_call_target="tpu_custom_call", output_to_operand_aliasing={{0}: (3, {}), {1}: (4, {}), {2}: (5, {}), {3}: (6, {}), {4}... | custom-call | tf_op jit(solution)/shard_map/pallas_call | solution.py:643
  30.8 10.7 %collective-permute-start.5 = (f32[91,8,128]{2,1,0:T(8,128)S(1)}, f32[91,8,128]{2,1,0:T(8,128)S(1)}, u32[]{:S(2)}, u32[]{:S(2)}) collective-permute-start(f32[91,8,128]{2,1,0:T(8,128)S(1)} %get-tuple-element.78), channel_id=1, source_target_pairs={{0,1},{1,0},{2,3},{3,2},{4,5},{5,4},{6,7},{7,6},{8,9},{9,8},{10,11... | collective-permute-start | bytes 1118216 | tf_op jit(solution)/shard_map/ppermute | solution.py:708
  41.6 0.4 shard_map.60
  42.0 0.9 %collective-permute-done.5.recv = f32[91,8,128]{2,1,0:T(8,128)S(1)} collective-permute-done((f32[91,8,128]{2,1,0:T(8,128)S(1)}, f32[91,8,128]{2,1,0:T(8,128)S(1)}, u32[]{:S(2)}, u32[]{:S(2)}) %collective-permute-start.5) | collective-permute-done | bytes 372768 | tf_op jit(solution)/shard_map/ppermute | solution.py:708
  42.9 2.1 %shard_map.61 = (f32[110,8,128]{2,1,0:T(8,128)S(1)}, f32[2,10,16,128]{3,2,1,0:T(8,128)S(1)}, f32[110,8,128]{2,1,0:T(8,128)S(1)}, f32[110,8,128]{2,1,0:T(8,128)S(1)}, f32[8,48,256]{2,1,0:T(8,128)}) custom-call(f32[91,8,128]{2,1,0:T(8,128)S(1)} %collective-permute-done.5.recv, ...), custom_call_target="tpu_custom_call", output_to_operand_aliasing={{0}: (3, {}), {1}: (4, {}), {2}: (5, {}), {3}: (6, {})} | custom-call | tf_op jit(solution)/shard_map/pallas_call | solution.py:673
  (5 shorter events, 0.1 us)
Async XLA Ops:
  0.0 3.3 %collective-permute-start = (s32[6,8,256]{2,1,0:T(8,128)}, s32[6,8,256]{2,1,0:T(8,128)S(1)}, u32[]{:S(2)}, u32[]{:S(2)}) collective-permute-start(s32[6,8,256]{2,1,0:T(8,128)} %labels.1), channel_id=1, source_target_pairs={{0,1},{1,0},{2,3},{3,2},{4,5},{5,4},{6,7},{7,6},{8,9},{9,8},{10,11... | collective-permute-start | bytes 147464 | tf_op jit(solution)/shard_map/ppermute | solution.py:708
  3.3 10.6 %collective-permute-start.1 = (s32[6,16,256]{2,1,0:T(8,128)S(1)}, s32[6,16,256]{2,1,0:T(8,128)S(1)}, u32[]{:S(2)}, u32[]{:S(2)}) collective-permute-start(s32[6,16,256]{2,1,0:T(8,128)S(1)} %add_select_fusion.1.after), channel_id=1, source_target_pairs={{0,17},{17,0},{16,33},{33,16},{32,49},{49,32},{48,65},{65,48},{64,... | collective-permute-start | bytes 294920 | tf_op jit(solution)/shard_map/ppermute | solution.py:701
  7.4 6.5 %collective-permute-start.2 = (s32[4,16,256]{2,1,0:T(8,128)S(1)}, s32[4,16,256]{2,1,0:T(8,128)S(1)}, u32[]{:S(2)}, u32[]{:S(2)}) collective-permute-start(s32[4,16,256]{2,1,0:T(8,128)S(1)} %slice_select_fusion), channel_id=1, source_target_pairs={{0,33},{33,0},{16,49},{49,16},{32,65},{65,32},{48,81},{81,48},{64,... | collective-permute-start | bytes 196616 | tf_op jit(solution)/shard_map/ppermute | solution.py:701
  14.1 11.6 %collective-permute-start.4 = (s32[10,16,256]{2,1,0:T(8,128)S(1)}, s32[10,16,256]{2,1,0:T(8,128)S(1)}, u32[]{:S(2)}, u32[]{:S(2)}) collective-permute-start(s32[10,16,256]{2,1,0:T(8,128)S(1)} %slice.19), channel_id=1, source_target_pairs={{0,2},{1,3},{2,4},{3,5},{4,6},{5,7},{6,8},{7,9},{8,10},{9,11},{10,... | collective-permute-start | bytes 491528 | tf_op jit(solution)/shard_map/ppermute | solution.py:705
  16.8 11.7 %collective-permute-start.3 = (s32[9,16,256]{2,1,0:T(8,128)S(1)}, s32[9,16,256]{2,1,0:T(8,128)S(1)}, u32[]{:S(2)}, u32[]{:S(2)}) collective-permute-start(s32[9,16,256]{2,1,0:T(8,128)S(1)} %slice.18), channel_id=1, source_target_pairs={{2,0},{3,1},{4,2},{5,3},{6,4},{7,5},{8,6},{9,7},{10,8},{11,9},{12,... | collective-permute-start | bytes 442376 | tf_op jit(solution)/shard_map/ppermute | solution.py:705
  30.8 12.0 %collective-permute-start.5 = (f32[91,8,128]{2,1,0:T(8,128)S(1)}, f32[91,8,128]{2,1,0:T(8,128)S(1)}, u32[]{:S(2)}, u32[]{:S(2)}) collective-permute-start(f32[91,8,128]{2,1,0:T(8,128)S(1)} %get-tuple-element.78), channel_id=1, source_target_pairs={{0,1},{1,0},{2,3},{3,2},{4,5},{5,4},{6,7},{7,6},{8,9},{9,8},{10,11... | collective-permute-start | bytes 1118216 | tf_op jit(solution)/shard_map/ppermute | solution.py:708

commit v10 on v8

--- a/solution.py
+++ b/solution.py
@@ -72,11 +72,15 @@
     return real * ratio, -imag * ratio
 
 
+def side_of(core):
+    return 1 - core
+
+
 def where_am_i():
     gx = lax.axis_index("gx")
     gy = lax.axis_index("gy")
     core = lax.rem(gy, 2)
-    x0 = OWN_X * gx - LOW * core
+    x0 = OWN_X * gx - LOW * side_of(core)
     y0 = OWN_Y * (gy - core) - LOW
     return core, x0, y0
 
@@ -236,9 +240,10 @@
 
         lax.fori_loop(0, count // step, some, 0)
 
-    def first_stage(self, y):
+    def first_stage(self, y, full=True):
+        planes = PX if full else PX - 1
         edges, faces, centres = [[], []], [[], []], [[], []]
-        for x in range(PX):
+        for x in range(planes):
             at = (y * PX + x) * 2
             e = self.wave[at]
             e_t = self.wave[at + 1]
@@ -257,7 +262,7 @@
                 edges[h].append(edge)
                 faces[h].append(face)
                 centres[h].append(near)
-        for x in range(PX):
+        for x in range(PX) if full else range(1, 14):
             at = (y * PX + x) * 2
             for h in range(2):
                 p = centres[h][x]
@@ -336,7 +341,8 @@
     region = Region(sizes, tab, wave, refs[12:24], refs[26:])
     c1_out, ck_out = refs[24:26]
     region.tables(labels, 0, LOW, LOW)
-    row_loop(0, LOW, 5, region.first_stage)
+    row_loop(0, LOW - 1, 3, lambda y: region.first_stage(y, False))
+    region.first_stage(LOW - 1)
     row_loop(1, LOW, 5, region.second_stage)
     for k in range(2):
         for i in range(CX):
@@ -351,7 +357,8 @@
     it1 = region.it1
     top = LOW + 2 * OWN_Y
     region.tables(labels, top, PY - top, PY - top)
-    row_loop(top, PY - top, 3, region.first_stage)
+    region.first_stage(top)
+    row_loop(top + 1, PY - top - 1, 4, lambda y: region.first_stage(y, False))
     row_loop(top - 1, PY - top, 3, region.second_stage)
 
     @pl.when(y0 + top == ny)
@@ -369,7 +376,7 @@
         for k in range(2):
             send_out[CX * NJ + (k * CX + i) * 2] = ck_out[k, i, 0:8, :]
             send_out[CX * NJ + (k * CX + i) * 2 + 1] = ck_out[k, i, 8:16, :]
-    plane = 6 + 3 * core
+    plane = 6 + 3 * side_of(core)
     ys = LOW + OWN_Y - core * OWN_Y
     edges, faces = [], []
     for k in range(OWN_Y + 2):
@@ -416,9 +423,9 @@
     first = lanes == 0
     last = lanes == LANES - 1
 
-    xb = core * LOW
+    xb = side_of(core) * LOW
     yb = LOW + core * OWN_Y
-    xe = core * (PX - 1)
+    xe = side_of(core) * (PX - 1)
     tables = (own.ie_r, own.io_r, own.ie_i, own.io_i)
 
     def own_stage(k):
@@ -431,7 +438,7 @@
         for n, ref in enumerate(tables):
             inv[n, pl.ds(k, 1), :] = ref[y, pl.ds(xe, 1), :]
 
-    own_i = CX - core * CX
+    own_i = CX - side_of(core) * CX
     for i in range(CX):
         for j in range(NJ):
             c1[(own_i + i) * NJ + j] = c1_own[i, 4 * core + j]
@@ -451,7 +458,7 @@
     last = lanes == LANES - 1
     sgn = sign_rows()
     j0 = 4 * core
-    other_i = core * CX
+    other_i = side_of(core) * CX
 
     def spread(row):
         return jnp.broadcast_to(row, (8, LANES))
@@ -485,7 +492,7 @@
 
         row_loop(sweep + 1, NI - 2 * sweep - 2, relax_step, relax)
 
-    flags = {0: jnp.where(core == 0, 1.0, 0.0), OWN_X - 1: jnp.where(core == 1, 1.0, 0.0)}
+    flags = {0: jnp.where(core == 1, 1.0, 0.0), OWN_X - 1: jnp.where(core == 0, 1.0, 0.0)}
     added = []
     for k in range(OWN_Y):
         pair = []
@@ -695,7 +702,7 @@
     def along_x(values, by):
         pairs = []
         for j in range(gy_n):
-            step = by if j % 2 == 0 else -by
+            step = by if j % 2 == 1 else -by
             for i in range(gx_n):
                 if 0 <= i + step < gx_n:
                     pairs.append(((i + step) * gy_n + j, i * gy_n + j))
@@ -716,14 +723,14 @@
         jnp.concatenate([other, labels], axis=1),
     )
     both = with_layout_constraint(both, Layout((0, 1, 2)))
-    far = along_x(jnp.where(is_low, both[:4], both[2:]), 2)
+    far = along_x(jnp.where(is_low, both[2:], both[:4]), 2)
     near = along_x(both, 1)
     near = with_layout_constraint(near, Layout((0, 1, 2)))
     far = with_layout_constraint(far, Layout((0, 1, 2)))
     region = jnp.where(
         is_low,
+        jnp.concatenate([far, near, both], axis=0),
         jnp.concatenate([both, near, far], axis=0),
-        jnp.concatenate([far, near, both], axis=0),
     )
     region = jnp.transpose(region, (1, 0, 2))
     low = along_y(region[2 * OWN_Y - LOW :], 2)

time: 44.9 us -> 43.4 us (0.967)
  starting transfers between devices: 24.5 us -> 21.3 us
  waiting for transfers between devices: 6.4 us -> 8.22 us
    ppermute x2, starting transfers between devices: 13.7 us -> 10.4 us  [along_x(): return lax.ppermute(values, ('gx', 'gy'), pairs)]
    ppermute x2, waiting for transfers between devices: 4.53 us -> 6.38 us  [along_x(): return lax.ppermute(values, ('gx', 'gy'), pairs)]
  transfers between devices with their start and end apart: 6 -> 6, of which waited for: 3 -> 3; matrix products, arithmetic and copies ran while one was open for 0% -> 0% of each run, Pallas kernels for 19% -> 20%
where the time goes in v10:
time: 43.4 us; the launch traced here: 42.8 us
  starting transfers between devices  21.3 us (49%)
  Pallas kernels  12.8 us (29%)
  waiting for transfers between devices  8.22 us (19%)
    ppermute x2, starting transfers between devices, along_x(): return lax.ppermute(values, ('gx', 'gy'), pairs)  10.4 us
    ppermute x2, starting transfers between devices, along_y(): return lax.ppermute(values, 'gy', pairs)  7.05 us
    ppermute x2, waiting for transfers between devices, along_x(): return lax.ppermute(values, ('gx', 'gy'), pairs)  6.38 us
    ppermute x2, starting transfers between devices, core_swap(): return lax.ppermute(values, 'gy', [(j, j ^ 1) for j in range(gy_n)])  3.83 us
    pallas_call x1, Pallas kernels, middle_call(): pl.pallas_call(kernel, out_shape=SHARED, in_specs=[SPEC] * 3, out_specs=(...  2.94 us
    pallas_call x1, Pallas kernels, low_call(): pl.pallas_call(kernel, out_shape=SHARED + COARSE, in_specs=[SPEC] * 15, o...  2.72 us
    pallas_call x1, Pallas kernels, high_call(): pl.pallas_call(kernel, out_shape=SHARED + COARSE + (vmem(SEND, 8, LANES),...  2.26 us
    pallas_call x1, Pallas kernels, cycle_call(): pl.pallas_call(cycle_kernel, out_shape=HALF + (jax.ShapeDtypeStruct((8, O...  2.14 us
  transfers between devices with their start and end apart: 6, of which 3 were waited for; matrix products, arithmetic and copies ran while one was open for 0% of the time, Pallas kernels for 20%

profile of v10, /device:TPU:38, one launch (start us, length us, event | category | flops | bytes accessed | tf_op | source)
XLA Modules:
  0.0 42.8 jit_solution(9734945398324621780)
XLA Ops:
  0.0 1.9 %collective-permute-start = (s32[6,8,256]{2,1,0:T(8,128)}, s32[6,8,256]{2,1,0:T(8,128)S(1)}, u32[]{:S(2)}, u32[]{:S(2)}) collective-permute-start(s32[6,8,256]{2,1,0:T(8,128)} %labels.1), channel_id=1, source_target_pairs={{0,1},{1,0},{2,3},{3,2},{4,5},{5,4},{6,7},{7,6},{8,9},{9,8},{10,11... | collective-permute-start | bytes 147464 | tf_op jit(solution)/shard_map/ppermute | solution.py:716
  1.9 0.8 %shard_map.55 = s32[6,8,256]{2,1,0:T(8,128)S(1)} custom-call(s32[6,8,256]{2,1,0:T(8,128)} %labels.1), custom_call_target="tpu_custom_call" | custom-call | tf_op jit(solution)/shard_map/pallas_call | solution.py:589
  2.8 0.6 %collective-permute-done = s32[6,8,256]{2,1,0:T(8,128)S(1)} collective-permute-done((s32[6,8,256]{2,1,0:T(8,128)}, s32[6,8,256]{2,1,0:T(8,128)S(1)}, u32[]{:S(2)}, u32[]{:S(2)}) %collective-permute-start) | collective-permute-done | bytes 49184 | tf_op jit(solution)/shard_map/ppermute | solution.py:716
  3.3 4.3 %collective-permute-start.2 = (s32[6,16,256]{2,1,0:T(8,128)S(1)}, s32[6,16,256]{2,1,0:T(8,128)S(1)}, u32[]{:S(2)}, u32[]{:S(2)}) collective-permute-start(s32[6,16,256]{2,1,0:T(8,128)S(1)} %add_select_fusion.1.after), channel_id=1, source_target_pairs={{0,16},{16,32},{32,48},{48,64},{64,80},{80,96},{96,112},{112,128},... | collective-permute-start | bytes 294920 | tf_op jit(solution)/shard_map/ppermute | solution.py:709
  7.6 6.1 %collective-permute-start.1 = (s32[4,16,256]{2,1,0:T(8,128)S(1)}, s32[4,16,256]{2,1,0:T(8,128)S(1)}, u32[]{:S(2)}, u32[]{:S(2)}) collective-permute-start(s32[4,16,256]{2,1,0:T(8,128)S(1)} %slice_select_fusion), channel_id=1, source_target_pairs={{0,32},{16,48},{32,64},{48,80},{64,96},{80,112},{96,128},{112,144}... | collective-permute-start | bytes 196616 | tf_op jit(solution)/shard_map/ppermute | solution.py:709
  13.7 0.1 copy.38
  13.8 6.4 %collective-permute-done.1 = s32[4,16,256]{2,1,0:T(8,128)S(1)} collective-permute-done((s32[4,16,256]{2,1,0:T(8,128)S(1)}, s32[4,16,256]{2,1,0:T(8,128)S(1)}, u32[]{:S(2)}, u32[]{:S(2)}) %collective-permute-start.1) | collective-permute-done | bytes 65568 | tf_op jit(solution)/shard_map/ppermute | solution.py:709
  20.2 0.0 collective-permute-done.2
  20.2 0.1 copy.37
  20.3 0.1 fusion.refs_0_
  20.4 2.6 %collective-permute-start.4 = (s32[10,16,256]{2,1,0:T(8,128)S(1)}, s32[10,16,256]{2,1,0:T(8,128)S(1)}, u32[]{:S(2)}, u32[]{:S(2)}) collective-permute-start(s32[10,16,256]{2,1,0:T(8,128)S(1)} %slice.19), channel_id=1, source_target_pairs={{0,2},{1,3},{2,4},{3,5},{4,6},{5,7},{6,8},{7,9},{8,10},{9,11},{10,... | collective-permute-start | bytes 491528 | tf_op jit(solution)/shard_map/ppermute | solution.py:713
  23.1 4.5 %collective-permute-start.3 = (s32[9,16,256]{2,1,0:T(8,128)S(1)}, s32[9,16,256]{2,1,0:T(8,128)S(1)}, u32[]{:S(2)}, u32[]{:S(2)}) collective-permute-start(s32[9,16,256]{2,1,0:T(8,128)S(1)} %slice.18), channel_id=1, source_target_pairs={{2,0},{3,1},{4,2},{5,3},{6,4},{7,5},{8,6},{9,7},{10,8},{11,9},{12,... | collective-permute-start | bytes 442376 | tf_op jit(solution)/shard_map/ppermute | solution.py:713
  27.5 1.6 %shard_map.56 = (f32[1120,8,128]{2,1,0:T(8,128)S(1)}, f32[8,128]{1,0:T(8,128)S(1)}) custom-call(f32[8]{0:T(128)} %real_in.1, f32[8]{0:T(128)} %imag_in.1, f32[360]{0:T(512)} %angles_in.1, s32[4]{0:T(128)} %picks_in.1, s32[6,16,256]{2,1,0:T(8,128)S(1)} %add_select_fusion.1.after), custom_call_target="tpu_custom_call" | custom-call | tf_op jit(solution)/shard_map/pallas_call | solution.py:601
  29.1 2.9 %shard_map.57 = (f32[35,16,128]{2,1,0:T(8,128)S(1)}, f32[35,16,128]{2,1,0:T(8,128)S(1)}, f32[35,16,128]{2,1,0:T(8,128)S(1)}, f32[35,16,128]{2,1,0:T(8,128)S(1)},...) custom-call(s32[16,16,256]{2,1,0:T(8,128)S(1)} %fusion.refs_0_, ...), custom_call_target="tpu_custom_call" | custom-call | tf_op jit(solution)/shard_map/pallas_call | solution.py:621
  32.1 0.0 collective-permute-done.4.refs_0_
  32.1 2.7 %shard_map.58 = (f32[35,16,128]{2,1,0:T(8,128)S(1)}, f32[35,16,128]{2,1,0:T(8,128)S(1)}, f32[35,16,128]{2,1,0:T(8,128)S(1)}, f32[35,16,128]{2,1,0:T(8,128)S(1)},...) custom-call(s32[10,16,256]{2,1,0:T(8,128)S(1)} %collective-permute-d, ...), custom_call_target="tpu_custom_call", output_to_operand_aliasing={{0}: (3, {}), {1}: (4, {}), {2}: (5, {}), {3}: (6, {}), {4}... | custom-call | tf_op jit(solution)/shard_map/pallas_call | solution.py:635
  34.8 0.0 collective-permute-done.3.refs_0_
  34.8 2.3 %shard_map.59 = (f32[35,16,128]{2,1,0:T(8,128)S(1)}, f32[35,16,128]{2,1,0:T(8,128)S(1)}, f32[35,16,128]{2,1,0:T(8,128)S(1)}, f32[35,16,128]{2,1,0:T(8,128)S(1)},...) custom-call(s32[9,16,256]{2,1,0:T(8,128)S(1)} %collective-permute-do, ...), custom_call_target="tpu_custom_call", output_to_operand_aliasing={{0}: (3, {}), {1}: (4, {}), {2}: (5, {}), {3}: (6, {}), {4}... | custom-call | tf_op jit(solution)/shard_map/pallas_call | solution.py:650
  37.1 1.9 %collective-permute-start.5 = (f32[91,8,128]{2,1,0:T(8,128)S(1)}, f32[91,8,128]{2,1,0:T(8,128)S(1)}, u32[]{:S(2)}, u32[]{:S(2)}) collective-permute-start(f32[91,8,128]{2,1,0:T(8,128)S(1)} %get-tuple-element.78), channel_id=1, source_target_pairs={{0,1},{1,0},{2,3},{3,2},{4,5},{5,4},{6,7},{7,6},{8,9},{9,8},{10,11... | collective-permute-start | bytes 1118216 | tf_op jit(solution)/shard_map/ppermute | solution.py:716
  39.0 0.4 shard_map.60
  39.4 1.3 %collective-permute-done.5.recv = f32[91,8,128]{2,1,0:T(8,128)S(1)} collective-permute-done((f32[91,8,128]{2,1,0:T(8,128)S(1)}, f32[91,8,128]{2,1,0:T(8,128)S(1)}, u32[]{:S(2)}, u32[]{:S(2)}) %collective-permute-start.5) | collective-permute-done | bytes 372768 | tf_op jit(solution)/shard_map/ppermute | solution.py:716
  40.7 2.1 %shard_map.61 = (f32[110,8,128]{2,1,0:T(8,128)S(1)}, f32[2,10,16,128]{3,2,1,0:T(8,128)S(1)}, f32[110,8,128]{2,1,0:T(8,128)S(1)}, f32[110,8,128]{2,1,0:T(8,128)S(1)}, f32[8,48,256]{2,1,0:T(8,128)}) custom-call(f32[91,8,128]{2,1,0:T(8,128)S(1)} %collective-permute-done.5.recv, ...), custom_call_target="tpu_custom_call", output_to_operand_aliasing={{0}: (3, {}), {1}: (4, {}), {2}: (5, {}), {3}: (6, {})} | custom-call | tf_op jit(solution)/shard_map/pallas_call | solution.py:680
  (5 shorter events, 0.1 us)
Async XLA Ops:
  0.0 3.3 %collective-permute-start = (s32[6,8,256]{2,1,0:T(8,128)}, s32[6,8,256]{2,1,0:T(8,128)S(1)}, u32[]{:S(2)}, u32[]{:S(2)}) collective-permute-start(s32[6,8,256]{2,1,0:T(8,128)} %labels.1), channel_id=1, source_target_pairs={{0,1},{1,0},{2,3},{3,2},{4,5},{5,4},{6,7},{7,6},{8,9},{9,8},{10,11... | collective-permute-start | bytes 147464 | tf_op jit(solution)/shard_map/ppermute | solution.py:716
  3.3 16.9 %collective-permute-start.2 = (s32[6,16,256]{2,1,0:T(8,128)S(1)}, s32[6,16,256]{2,1,0:T(8,128)S(1)}, u32[]{:S(2)}, u32[]{:S(2)}) collective-permute-start(s32[6,16,256]{2,1,0:T(8,128)S(1)} %add_select_fusion.1.after), channel_id=1, source_target_pairs={{0,16},{16,32},{32,48},{48,64},{64,80},{80,96},{96,112},{112,128},... | collective-permute-start | bytes 294920 | tf_op jit(solution)/shard_map/ppermute | solution.py:709
  7.6 12.5 %collective-permute-start.1 = (s32[4,16,256]{2,1,0:T(8,128)S(1)}, s32[4,16,256]{2,1,0:T(8,128)S(1)}, u32[]{:S(2)}, u32[]{:S(2)}) collective-permute-start(s32[4,16,256]{2,1,0:T(8,128)S(1)} %slice_select_fusion), channel_id=1, source_target_pairs={{0,32},{16,48},{32,64},{48,80},{64,96},{80,112},{96,128},{112,144}... | collective-permute-start | bytes 196616 | tf_op jit(solution)/shard_map/ppermute | solution.py:709
  20.4 11.6 %collective-permute-start.4 = (s32[10,16,256]{2,1,0:T(8,128)S(1)}, s32[10,16,256]{2,1,0:T(8,128)S(1)}, u32[]{:S(2)}, u32[]{:S(2)}) collective-permute-start(s32[10,16,256]{2,1,0:T(8,128)S(1)} %slice.19), channel_id=1, source_target_pairs={{0,2},{1,3},{2,4},{3,5},{4,6},{5,7},{6,8},{7,9},{8,10},{9,11},{10,... | collective-permute-start | bytes 491528 | tf_op jit(solution)/shard_map/ppermute | solution.py:713
  23.1 11.8 %collective-permute-start.3 = (s32[9,16,256]{2,1,0:T(8,128)S(1)}, s32[9,16,256]{2,1,0:T(8,128)S(1)}, u32[]{:S(2)}, u32[]{:S(2)}) collective-permute-start(s32[9,16,256]{2,1,0:T(8,128)S(1)} %slice.18), channel_id=1, source_target_pairs={{2,0},{3,1},{4,2},{5,3},{6,4},{7,5},{8,6},{9,7},{10,8},{11,9},{12,... | collective-permute-start | bytes 442376 | tf_op jit(solution)/shard_map/ppermute | solution.py:713
  37.1 3.6 %collective-permute-start.5 = (f32[91,8,128]{2,1,0:T(8,128)S(1)}, f32[91,8,128]{2,1,0:T(8,128)S(1)}, u32[]{:S(2)}, u32[]{:S(2)}) collective-permute-start(f32[91,8,128]{2,1,0:T(8,128)S(1)} %get-tuple-element.78), channel_id=1, source_target_pairs={{0,1},{1,0},{2,3},{3,2},{4,5},{5,4},{6,7},{7,6},{8,9},{9,8},{10,11... | collective-permute-start | bytes 1118216 | tf_op jit(solution)/shard_map/ppermute | solution.py:716

commit v11 on v10

--- a/solution.py
+++ b/solution.py
@@ -338,8 +338,8 @@
 
 
 def low_kernel(sizes, labels, tab, wave, *refs):
-    region = Region(sizes, tab, wave, refs[12:24], refs[26:])
-    c1_out, ck_out = refs[24:26]
+    region = Region(sizes, tab, wave, refs[12:24], refs[27:])
+    c1_out, ck_out, send_out = refs[24:27]
     region.tables(labels, 0, LOW, LOW)
     row_loop(0, LOW - 1, 3, lambda y: region.first_stage(y, False))
     region.first_stage(LOW - 1)
@@ -348,11 +348,17 @@
         for i in range(CX):
             ck_out[k, i, 8:16, :] = jnp.zeros((8, LANES), F32)
     row_loop(0, EARLY, 1, lambda j: region.third_stage(j, c1_out, ck_out))
+    j0 = 4 - 4 * region.core
+    for i in range(CX):
+        for j in range(EARLY - 4):
+            send_out[i * NJ + j] = c1_out[i, j0 + j]
+        for k in range(2):
+            send_out[CX * NJ + (k * CX + i) * 2] = ck_out[k, i, 0:8, :]
 
 
 def high_kernel(sizes, labels, tab, wave, *refs):
-    region = Region(sizes, tab, wave, refs[14:26], refs[29:])
-    c1_out, ck_out, send_out = refs[26:29]
+    region = Region(sizes, tab, wave, refs[15:27], refs[30:])
+    c1_out, ck_out, send_out = refs[27:30]
     core, y0, ny = region.core, region.y0, region.ny
     it1 = region.it1
     top = LOW + 2 * OWN_Y
@@ -371,10 +377,9 @@
 
     j0 = 4 - 4 * core
     for i in range(CX):
-        for j in range(NJ):
+        for j in range(EARLY - 4, NJ):
             send_out[i * NJ + j] = c1_out[i, j0 + j]
         for k in range(2):
-            send_out[CX * NJ + (k * CX + i) * 2] = ck_out[k, i, 0:8, :]
             send_out[CX * NJ + (k * CX + i) * 2 + 1] = ck_out[k, i, 8:16, :]
     plane = 6 + 3 * side_of(core)
     ys = LOW + OWN_Y - core * OWN_Y
@@ -634,9 +639,9 @@
 
     return pl.pallas_call(
         kernel,
-        out_shape=SHARED + COARSE,
+        out_shape=SHARED + COARSE + (vmem(SEND, 8, LANES),),
         in_specs=[SPEC] * 15,
-        out_specs=(SPEC,) * 14,
+        out_specs=(SPEC,) * 15,
         input_output_aliases={3 + n: n for n in range(12)},
         scratch_shapes=TABLES + [vmem(LOW * PX, 2 * LANES)],
         compiler_params=limit(6),
@@ -650,9 +655,9 @@
     results = pl.pallas_call(
         kernel,
         out_shape=SHARED + COARSE + (vmem(SEND, 8, LANES),),
-        in_specs=[SPEC] * 17,
+        in_specs=[SPEC] * 18,
         out_specs=(SPEC,) * 15,
-        input_output_aliases={3 + n: n for n in range(14)},
+        input_output_aliases={3 + n: n for n in range(15)},
         scratch_shapes=TABLES + [vmem(LOW * PX, 2 * LANES)],
         compiler_params=limit(6),
     )(*near_core(labels, tab, wave), *shared)

time: 43.4 us -> 43.4 us (level)
  no operation moved by 1% of the time
where the time goes in v11:
time: 43.4 us; the launch traced here: 42.8 us
  starting transfers between devices  21.3 us (49%)
  Pallas kernels  12.9 us (30%)
  waiting for transfers between devices  8.22 us (19%)
    ppermute x2, starting transfers between devices, along_x(): return lax.ppermute(values, ('gx', 'gy'), pairs)  10.4 us
    ppermute x2, starting transfers between devices, along_y(): return lax.ppermute(values, 'gy', pairs)  7.05 us
    ppermute x2, waiting for transfers between devices, along_x(): return lax.ppermute(values, ('gx', 'gy'), pairs)  6.38 us
    ppermute x2, starting transfers between devices, core_swap(): return lax.ppermute(values, 'gy', [(j, j ^ 1) for j in range(gy_n)])  3.83 us
    pallas_call x1, Pallas kernels, middle_call(): pl.pallas_call(kernel, out_shape=SHARED, in_specs=[SPEC] * 3, out_specs=(...  2.94 us
    pallas_call x1, Pallas kernels, low_call(): pl.pallas_call(kernel, out_shape=SHARED + COARSE + (vmem(SEND, 8, LANES),...  2.73 us
    pallas_call x1, Pallas kernels, high_call(): pl.pallas_call(kernel, out_shape=SHARED + COARSE + (vmem(SEND, 8, LANES),...  2.26 us
    pallas_call x1, Pallas kernels, cycle_call(): pl.pallas_call(cycle_kernel, out_shape=HALF + (jax.ShapeDtypeStruct((8, O...  2.14 us
  transfers between devices with their start and end apart: 6, of which 3 were waited for; matrix products, arithmetic and copies ran while one was open for 0% of the time, Pallas kernels for 20%

profile of v11, /device:TPU:38, one launch (start us, length us, event | category | flops | bytes accessed | tf_op | source)
XLA Modules:
  0.0 42.8 jit_solution(1342806668461552127)
XLA Ops:
  0.0 1.9 %collective-permute-start = (s32[6,8,256]{2,1,0:T(8,128)}, s32[6,8,256]{2,1,0:T(8,128)S(1)}, u32[]{:S(2)}, u32[]{:S(2)}) collective-permute-start(s32[6,8,256]{2,1,0:T(8,128)} %labels.1), channel_id=1, source_target_pairs={{0,1},{1,0},{2,3},{3,2},{4,5},{5,4},{6,7},{7,6},{8,9},{9,8},{10,11... | collective-permute-start | bytes 147464 | tf_op jit(solution)/shard_map/ppermute | solution.py:721
  1.9 0.8 %shard_map.55 = s32[6,8,256]{2,1,0:T(8,128)S(1)} custom-call(s32[6,8,256]{2,1,0:T(8,128)} %labels.1), custom_call_target="tpu_custom_call" | custom-call | tf_op jit(solution)/shard_map/pallas_call | solution.py:594
  2.8 0.6 %collective-permute-done = s32[6,8,256]{2,1,0:T(8,128)S(1)} collective-permute-done((s32[6,8,256]{2,1,0:T(8,128)}, s32[6,8,256]{2,1,0:T(8,128)S(1)}, u32[]{:S(2)}, u32[]{:S(2)}) %collective-permute-start) | collective-permute-done | bytes 49184 | tf_op jit(solution)/shard_map/ppermute | solution.py:721
  3.3 4.3 %collective-permute-start.2 = (s32[6,16,256]{2,1,0:T(8,128)S(1)}, s32[6,16,256]{2,1,0:T(8,128)S(1)}, u32[]{:S(2)}, u32[]{:S(2)}) collective-permute-start(s32[6,16,256]{2,1,0:T(8,128)S(1)} %add_select_fusion.1.after), channel_id=1, source_target_pairs={{0,16},{16,32},{32,48},{48,64},{64,80},{80,96},{96,112},{112,128},... | collective-permute-start | bytes 294920 | tf_op jit(solution)/shard_map/ppermute | solution.py:714
  7.6 6.1 %collective-permute-start.1 = (s32[4,16,256]{2,1,0:T(8,128)S(1)}, s32[4,16,256]{2,1,0:T(8,128)S(1)}, u32[]{:S(2)}, u32[]{:S(2)}) collective-permute-start(s32[4,16,256]{2,1,0:T(8,128)S(1)} %slice_select_fusion), channel_id=1, source_target_pairs={{0,32},{16,48},{32,64},{48,80},{64,96},{80,112},{96,128},{112,144}... | collective-permute-start | bytes 196616 | tf_op jit(solution)/shard_map/ppermute | solution.py:714
  13.7 0.1 copy.39
  13.8 6.4 %collective-permute-done.1 = s32[4,16,256]{2,1,0:T(8,128)S(1)} collective-permute-done((s32[4,16,256]{2,1,0:T(8,128)S(1)}, s32[4,16,256]{2,1,0:T(8,128)S(1)}, u32[]{:S(2)}, u32[]{:S(2)}) %collective-permute-start.1) | collective-permute-done | bytes 65568 | tf_op jit(solution)/shard_map/ppermute | solution.py:714
  20.2 0.0 collective-permute-done.2
  20.2 0.1 copy.38
  20.3 0.1 fusion.refs_0_
  20.4 2.6 %collective-permute-start.4 = (s32[10,16,256]{2,1,0:T(8,128)S(1)}, s32[10,16,256]{2,1,0:T(8,128)S(1)}, u32[]{:S(2)}, u32[]{:S(2)}) collective-permute-start(s32[10,16,256]{2,1,0:T(8,128)S(1)} %slice.19), channel_id=1, source_target_pairs={{0,2},{1,3},{2,4},{3,5},{4,6},{5,7},{6,8},{7,9},{8,10},{9,11},{10,... | collective-permute-start | bytes 491528 | tf_op jit(solution)/shard_map/ppermute | solution.py:718
  23.1 4.5 %collective-permute-start.3 = (s32[9,16,256]{2,1,0:T(8,128)S(1)}, s32[9,16,256]{2,1,0:T(8,128)S(1)}, u32[]{:S(2)}, u32[]{:S(2)}) collective-permute-start(s32[9,16,256]{2,1,0:T(8,128)S(1)} %slice.18), channel_id=1, source_target_pairs={{2,0},{3,1},{4,2},{5,3},{6,4},{7,5},{8,6},{9,7},{10,8},{11,9},{12,... | collective-permute-start | bytes 442376 | tf_op jit(solution)/shard_map/ppermute | solution.py:718
  27.5 1.6 %shard_map.56 = (f32[1120,8,128]{2,1,0:T(8,128)S(1)}, f32[8,128]{1,0:T(8,128)S(1)}) custom-call(f32[8]{0:T(128)} %real_in.1, f32[8]{0:T(128)} %imag_in.1, f32[360]{0:T(512)} %angles_in.1, s32[4]{0:T(128)} %picks_in.1, s32[6,16,256]{2,1,0:T(8,128)S(1)} %add_select_fusion.1.after), custom_call_target="tpu_custom_call" | custom-call | tf_op jit(solution)/shard_map/pallas_call | solution.py:606
  29.1 2.9 %shard_map.57 = (f32[35,16,128]{2,1,0:T(8,128)S(1)}, f32[35,16,128]{2,1,0:T(8,128)S(1)}, f32[35,16,128]{2,1,0:T(8,128)S(1)}, f32[35,16,128]{2,1,0:T(8,128)S(1)},...) custom-call(s32[16,16,256]{2,1,0:T(8,128)S(1)} %fusion.refs_0_, ...), custom_call_target="tpu_custom_call" | custom-call | tf_op jit(solution)/shard_map/pallas_call | solution.py:626
  32.1 0.0 collective-permute-done.4.refs_0_
  32.1 2.7 %shard_map.58 = (f32[35,16,128]{2,1,0:T(8,128)S(1)}, f32[35,16,128]{2,1,0:T(8,128)S(1)}, f32[35,16,128]{2,1,0:T(8,128)S(1)}, f32[35,16,128]{2,1,0:T(8,128)S(1)},...) custom-call(s32[10,16,256]{2,1,0:T(8,128)S(1)} %collective-permute-d, ...), custom_call_target="tpu_custom_call", output_to_operand_aliasing={{0}: (3, {}), {1}: (4, {}), {2}: (5, {}), {3}: (6, {}), {4}... | custom-call | tf_op jit(solution)/shard_map/pallas_call | solution.py:640
  34.8 0.0 collective-permute-done.3.refs_0_
  34.8 2.3 %shard_map.59 = (f32[35,16,128]{2,1,0:T(8,128)S(1)}, f32[35,16,128]{2,1,0:T(8,128)S(1)}, f32[35,16,128]{2,1,0:T(8,128)S(1)}, f32[35,16,128]{2,1,0:T(8,128)S(1)},...) custom-call(s32[9,16,256]{2,1,0:T(8,128)S(1)} %collective-permute-do, ...), custom_call_target="tpu_custom_call", output_to_operand_aliasing={{0}: (3, {}), {1}: (4, {}), {2}: (5, {}), {3}: (6, {}), {4}... | custom-call | tf_op jit(solution)/shard_map/pallas_call | solution.py:655
  37.1 1.9 %collective-permute-start.5 = (f32[91,8,128]{2,1,0:T(8,128)S(1)}, f32[91,8,128]{2,1,0:T(8,128)S(1)}, u32[]{:S(2)}, u32[]{:S(2)}) collective-permute-start(f32[91,8,128]{2,1,0:T(8,128)S(1)} %get-tuple-element.80), channel_id=1, source_target_pairs={{0,1},{1,0},{2,3},{3,2},{4,5},{5,4},{6,7},{7,6},{8,9},{9,8},{10,11... | collective-permute-start | bytes 1118216 | tf_op jit(solution)/shard_map/ppermute | solution.py:721
  39.0 0.4 shard_map.60
  39.4 1.3 %collective-permute-done.5.recv = f32[91,8,128]{2,1,0:T(8,128)S(1)} collective-permute-done((f32[91,8,128]{2,1,0:T(8,128)S(1)}, f32[91,8,128]{2,1,0:T(8,128)S(1)}, u32[]{:S(2)}, u32[]{:S(2)}) %collective-permute-start.5) | collective-permute-done | bytes 372768 | tf_op jit(solution)/shard_map/ppermute | solution.py:721
  40.7 2.1 %shard_map.61 = (f32[110,8,128]{2,1,0:T(8,128)S(1)}, f32[2,10,16,128]{3,2,1,0:T(8,128)S(1)}, f32[110,8,128]{2,1,0:T(8,128)S(1)}, f32[110,8,128]{2,1,0:T(8,128)S(1)}, f32[8,48,256]{2,1,0:T(8,128)}) custom-call(f32[91,8,128]{2,1,0:T(8,128)S(1)} %collective-permute-done.5.recv, ...), custom_call_target="tpu_custom_call", output_to_operand_aliasing={{0}: (3, {}), {1}: (4, {}), {2}: (5, {}), {3}: (6, {})} | custom-call | tf_op jit(solution)/shard_map/pallas_call | solution.py:685
  (5 shorter events, 0.1 us)
Async XLA Ops:
  0.0 3.3 %collective-permute-start = (s32[6,8,256]{2,1,0:T(8,128)}, s32[6,8,256]{2,1,0:T(8,128)S(1)}, u32[]{:S(2)}, u32[]{:S(2)}) collective-permute-start(s32[6,8,256]{2,1,0:T(8,128)} %labels.1), channel_id=1, source_target_pairs={{0,1},{1,0},{2,3},{3,2},{4,5},{5,4},{6,7},{7,6},{8,9},{9,8},{10,11... | collective-permute-start | bytes 147464 | tf_op jit(solution)/shard_map/ppermute | solution.py:721
  3.3 16.9 %collective-permute-start.2 = (s32[6,16,256]{2,1,0:T(8,128)S(1)}, s32[6,16,256]{2,1,0:T(8,128)S(1)}, u32[]{:S(2)}, u32[]{:S(2)}) collective-permute-start(s32[6,16,256]{2,1,0:T(8,128)S(1)} %add_select_fusion.1.after), channel_id=1, source_target_pairs={{0,16},{16,32},{32,48},{48,64},{64,80},{80,96},{96,112},{112,128},... | collective-permute-start | bytes 294920 | tf_op jit(solution)/shard_map/ppermute | solution.py:714
  7.6 12.5 %collective-permute-start.1 = (s32[4,16,256]{2,1,0:T(8,128)S(1)}, s32[4,16,256]{2,1,0:T(8,128)S(1)}, u32[]{:S(2)}, u32[]{:S(2)}) collective-permute-start(s32[4,16,256]{2,1,0:T(8,128)S(1)} %slice_select_fusion), channel_id=1, source_target_pairs={{0,32},{16,48},{32,64},{48,80},{64,96},{80,112},{96,128},{112,144}... | collective-permute-start | bytes 196616 | tf_op jit(solution)/shard_map/ppermute | solution.py:714
  20.4 11.6 %collective-permute-start.4 = (s32[10,16,256]{2,1,0:T(8,128)S(1)}, s32[10,16,256]{2,1,0:T(8,128)S(1)}, u32[]{:S(2)}, u32[]{:S(2)}) collective-permute-start(s32[10,16,256]{2,1,0:T(8,128)S(1)} %slice.19), channel_id=1, source_target_pairs={{0,2},{1,3},{2,4},{3,5},{4,6},{5,7},{6,8},{7,9},{8,10},{9,11},{10,... | collective-permute-start | bytes 491528 | tf_op jit(solution)/shard_map/ppermute | solution.py:718
  23.1 11.8 %collective-permute-start.3 = (s32[9,16,256]{2,1,0:T(8,128)S(1)}, s32[9,16,256]{2,1,0:T(8,128)S(1)}, u32[]{:S(2)}, u32[]{:S(2)}) collective-permute-start(s32[9,16,256]{2,1,0:T(8,128)S(1)} %slice.18), channel_id=1, source_target_pairs={{2,0},{3,1},{4,2},{5,3},{6,4},{7,5},{8,6},{9,7},{10,8},{11,9},{12,... | collective-permute-start | bytes 442376 | tf_op jit(solution)/shard_map/ppermute | solution.py:718
  37.1 3.6 %collective-permute-start.5 = (f32[91,8,128]{2,1,0:T(8,128)S(1)}, f32[91,8,128]{2,1,0:T(8,128)S(1)}, u32[]{:S(2)}, u32[]{:S(2)}) collective-permute-start(f32[91,8,128]{2,1,0:T(8,128)S(1)} %get-tuple-element.80), channel_id=1, source_target_pairs={{0,1},{1,0},{2,3},{3,2},{4,5},{5,4},{6,7},{7,6},{8,9},{9,8},{10,11... | collective-permute-start | bytes 1118216 | tf_op jit(solution)/shard_map/ppermute | solution.py:721
